TPU v7x, 128 devices: a whole 4x4x4 slice. The times are simulated.
128 devices in a mesh: gx: 4 (over z), gy: 32 (over y, x, core).
Axes of the slice: x: 4, y: 4, z: 4, core: 2. Of those that a mesh axis runs over, the one named last changes fastest.
Arguments:
- velocity: float32 [3, 16, 1024, 1024], P(None, 'gx', 'gy'), may hold values from -6 to 6
- section: float32 [3, 16, 1024, 1024], P(None, 'gx', 'gy'), may hold values from -8 to 8
- diffusion: float32 [1024], replicated, may hold values from 1000 to 10000
- rhs_near: float32 [1024], P('gy'), may hold values from 0.6 to 1.2
- rhs_far: float32 [1024], P('gy'), may hold values from -0.2 to -0.05
- part_vel: float32 [3, 1048576], P(None, ('gx', 'gy')), may hold values from -6 to 6
- part_rate: float32 [1048576], P(('gx', 'gy')), may hold values from 0.5 to 5
- counts: int32 [128, 128], P(('gx', 'gy')), may hold values from 0 to 64, as said below
- cell_slot: int32 [128, 8192], P(('gx', 'gy')), may hold values from 0 to 131071
Outputs:
- velocity_new: float32 [3, 16, 1024, 1024], P(None, 'gx', 'gy')
- section_new: float32 [3, 16, 1024, 1024], P(None, 'gx', 'gy')
- part_new: float32 [3, 1048576], P(None, ('gx', 'gy'))
Inputs may be any that keep to these rules, and one draw needn't show every extreme that they name: counts[d, s] is the number of live slots, from the front, of the block that device s sends to device d; in every draw one receiving device gets 64 live slots from every sender.
All inputs are finite; a program needn't handle non-finite values.
Results may differ from a plain program's by a relative error of at most 0.0003.
The roundings to bfloat16 on the way count: a program that leaves them out, or rounds other values in their place, can miss the bound.
Values sent between devices are 32-bit elements; how exact they have to be, the bound alone decides.
No kernel may reach another device: no remote copies, remote signals or barrier semaphores. Data moves between devices by JAX's collectives and lax.ppermute only.
A program may use at most 128 MiB of HBM per device.

v0:
```python
import jax
import jax.numpy as jnp
from jax import lax
from jax.sharding import PartitionSpec as P

HIGH = lax.Precision.HIGHEST
TIME_STEP = 0.2
SECTION_KEEP = -5.0 / 9.0
SECTION_GAIN = 15.0 / 16.0
MAIN_WEIGHT = 2.5
NEAR_WEIGHT = -4.0 / 3.0
FAR_WEIGHT = 1.0 / 12.0


def extended(block, sides, width, periodic):
    for axis, dim in sides:
        count = lax.axis_size(axis)
        forward = [(i, i + 1) for i in range(count - 1)]
        if periodic:
            forward.append((count - 1, 0))
        backward = [(target, source) for source, target in forward]
        low = lax.ppermute(
            lax.slice_in_dim(block, block.shape[dim] - width, None, axis=dim), axis, forward
        )
        high = lax.ppermute(lax.slice_in_dim(block, 0, width, axis=dim), axis, backward)
        block = jnp.concatenate([low, block, high], axis=dim)
    return block


def carried_in(part, axis, combine, identity, reverse):
    count = lax.axis_size(axis)
    place = lax.axis_index(axis)
    ahead = count - 1 - place if reverse else place
    gathered = jax.tree.map(lambda a: lax.all_gather(a, axis), part)
    state = jax.tree.map(lambda a, e: jnp.zeros_like(a) + jnp.asarray(e, a.dtype), part, identity)

    def one(step, state):
        source = count - 1 - step if reverse else step
        return combine(
            state, jax.tree.map(lambda a: lax.dynamic_index_in_dim(a, source, 0, False), gathered)
        )

    return lax.fori_loop(0, ahead, one, state)


def invert_batch(matrix):
    extent = matrix.shape[-1]
    positions = jnp.arange(extent)
    identity_m = jnp.broadcast_to(jnp.eye(extent, dtype=jnp.float32), matrix.shape)

    def eliminate(row_index, state):
        working, result = state
        head_work = lax.dynamic_index_in_dim(working, row_index, working.ndim - 2, keepdims=False)
        pivot_value = lax.dynamic_index_in_dim(
            head_work, row_index, head_work.ndim - 1, keepdims=True
        )
        head_work = head_work / pivot_value
        head_result = (
            lax.dynamic_index_in_dim(result, row_index, result.ndim - 2, keepdims=False)
            / pivot_value
        )
        column = lax.dynamic_index_in_dim(working, row_index, working.ndim - 1, keepdims=False)
        is_head = positions == row_index
        column = jnp.where(is_head, 0.0, column)
        working = working - column[..., :, None] * head_work[..., None, :]
        result = result - column[..., :, None] * head_result[..., None, :]
        working = jnp.where(is_head[:, None], head_work[..., None, :], working)
        result = jnp.where(is_head[:, None], head_result[..., None, :], result)
        return (working, result)

    return lax.fori_loop(0, extent, eliminate, (matrix, identity_m))[1]


def slab_factors(diffusion, slabs, slab_rows):
    rate = diffusion.reshape(slabs, slab_rows)
    near = NEAR_WEIGHT * rate
    far = FAR_WEIGHT * rate
    offset = jnp.arange(slab_rows)[None, :] - jnp.arange(slab_rows)[:, None]

    def band_of(shift_by):
        return (offset == shift_by).astype(jnp.float32)[None]

    band = (
        band_of(0) * (1.0 + MAIN_WEIGHT * rate)[:, :, None]
        + (band_of(-1) + band_of(1)) * near[:, :, None]
        + (band_of(-2) + band_of(2)) * far[:, :, None]
    )
    inverse_band = invert_batch(band)
    not_first = (jnp.arange(slabs) > 0).astype(jnp.float32)
    not_last = (jnp.arange(slabs) < slabs - 1).astype(jnp.float32)
    couple_low = jnp.zeros((slabs, slab_rows, 2), jnp.float32)
    couple_low = (
        couple_low.at[:, 0, 0].set(far[:, 0]).at[:, 0, 1].set(near[:, 0]).at[:, 1, 1].set(far[:, 1])
    )
    couple_low = couple_low * not_first[:, None, None]
    couple_high = jnp.zeros((slabs, slab_rows, 2), jnp.float32)
    couple_high = couple_high.at[:, slab_rows - 2, 0].set(far[:, slab_rows - 2])
    couple_high = couple_high.at[:, slab_rows - 1, 0].set(near[:, slab_rows - 1])
    couple_high = couple_high.at[:, slab_rows - 1, 1].set(far[:, slab_rows - 1])
    couple_high = couple_high * not_last[:, None, None]
    lower_fix = jnp.einsum("sjk,skm->sjm", inverse_band, couple_low, precision=HIGH)
    upper_fix = jnp.einsum("sjk,skm->sjm", inverse_band, couple_high, precision=HIGH)
    tip_rows = [0, 1, slab_rows - 2, slab_rows - 1]
    lower_tip = jnp.stack([lower_fix[:, tip_row] for tip_row in tip_rows], axis=1)
    upper_tip = jnp.stack([upper_fix[:, tip_row] for tip_row in tip_rows], axis=1)
    zeros_half = jnp.zeros((slabs, 4, 2), jnp.float32)
    link_down = jnp.concatenate([zeros_half, lower_tip], axis=2)
    link_up = jnp.concatenate([upper_tip, zeros_half], axis=2)
    return (inverse_band, lower_fix, upper_fix, link_down, link_up)


def schur_factors(link_down, link_up):
    identity_four = jnp.eye(4, dtype=jnp.float32)

    def advance(carry, links):
        prev_inverse, prev_up = carry
        down_here, up_here = links
        mixer = -jnp.dot(down_here, prev_inverse, precision=HIGH)
        schur = identity_four + jnp.dot(mixer, prev_up, precision=HIGH)
        inverse_here = invert_batch(schur)
        return ((inverse_here, up_here), (mixer, inverse_here))

    start_state = (identity_four, jnp.zeros((4, 4), jnp.float32))
    final_state, stacked = lax.scan(advance, start_state, (link_down, link_up))
    mixers, inverses = stacked
    backs = -jnp.einsum("sab,sbc->sac", inverses, link_up, precision=HIGH)
    return (mixers, inverses, backs)


def apply_four(matrix, vectors):
    return jnp.einsum("ab,bcxz->acxz", matrix, vectors, precision=HIGH)


def compose(earlier, later):
    return (
        jnp.dot(later[0], earlier[0], precision=HIGH),
        apply_four(later[0], earlier[1]) + later[1],
    )


def pick(stacked, position):
    return lax.dynamic_index_in_dim(stacked, position, 0, keepdims=False)


def central(field, axis_id):
    return (
        8.0 * (jnp.roll(field, -1, axis_id) - jnp.roll(field, 1, axis_id))
        - (jnp.roll(field, -2, axis_id) - jnp.roll(field, 2, axis_id))
    ) / 12.0


def local(velocity, section, diffusion, rhs_near, rhs_far, part_vel, part_rate, counts, cell_slot):
    components, width_x, slab_rows, width_z = velocity.shape
    slabs = lax.axis_size("gy")
    slab_index = lax.axis_index("gy")
    devices_all = counts.shape[1]
    total_slots = part_vel.shape[1]
    slot_count = total_slots // devices_all
    planes = width_x * slab_rows
    moved_vel, moved_rate = (
        lax.all_to_all(part_vel, ("gx", "gy"), split_axis=1, concat_axis=1, tiled=True),
        lax.all_to_all(
            part_rate.reshape(1, total_slots), ("gx", "gy"), split_axis=1, concat_axis=1, tiled=True
        ),
    )
    live = jnp.arange(total_slots) % slot_count < jnp.repeat(
        counts[0], slot_count, total_repeat_length=total_slots
    )
    cell_ids = cell_slot[0]
    plane_ids = cell_ids // width_z
    span_ids = cell_ids % width_z
    span_table = (jnp.arange(width_z)[:, None] == span_ids[None, :]).astype(jnp.bfloat16)
    plane_table = jnp.arange(planes)[:, None] == plane_ids[None, :]
    velocity_bf = velocity.astype(jnp.bfloat16).reshape(components * planes, width_z)
    at_cells = jnp.einsum("hz,zp->hp", velocity_bf, span_table, preferred_element_type=jnp.float32)
    fluid_at = jnp.sum(
        at_cells.reshape(components, planes, total_slots) * plane_table.astype(jnp.float32)[None],
        axis=1,
    )
    relative = fluid_at - moved_vel
    part_new = jnp.where(live[None], moved_vel + TIME_STEP * moved_rate * relative, 0.0)
    push = jnp.where(live[None], -moved_rate * relative, 0.0).astype(jnp.bfloat16)
    spread = (push[:, None, :] * plane_table.astype(jnp.bfloat16)[None]).reshape(
        components * planes, total_slots
    )
    deposit = jnp.einsum("hp,zp->hz", spread, span_table, preferred_element_type=jnp.float32)
    deposit = deposit.reshape(components, width_x, slab_rows, width_z)
    axial_pad = extended(velocity, (("gx", 1),), 2, True)
    ddx = (
        8.0 * (axial_pad[:, 3 : width_x + 3] - axial_pad[:, 1 : width_x + 1])
        - (axial_pad[:, 4:] - axial_pad[:, :width_x])
    ) / 12.0
    ddz = central(velocity, 3)
    wall_pad = extended(velocity, (("gy", 2),), 2, False)
    ddy = rhs_near[None, None, :, None] * (
        wall_pad[:, :, 3 : slab_rows + 3] - wall_pad[:, :, 1 : slab_rows + 1]
    ) + rhs_far[None, None, :, None] * (wall_pad[:, :, 4:] - wall_pad[:, :, :slab_rows])
    rhs = -(velocity[0:1] * ddx + velocity[1:2] * ddy + velocity[2:3] * ddz) + deposit
    section_new = SECTION_KEEP * section + TIME_STEP * rhs
    source = SECTION_GAIN * section_new
    inverse_band, lower_fix, upper_fix, link_down, link_up = slab_factors(
        diffusion, slabs, slab_rows
    )
    partial_value = jnp.einsum(
        "jk,cxkz->cxjz", pick(inverse_band, slab_index), source, precision=HIGH
    )
    tips = jnp.stack(
        [
            partial_value[:, :, 0],
            partial_value[:, :, 1],
            partial_value[:, :, slab_rows - 2],
            partial_value[:, :, slab_rows - 1],
        ]
    )
    mixers, inverses, backs = schur_factors(link_down, link_up)
    identity_four = jnp.eye(4, dtype=jnp.float32)
    mixer_here = pick(mixers, slab_index)
    before = carried_in(
        (mixer_here, tips), "gy", compose, (identity_four, jnp.zeros_like(tips)), False
    )[1]
    reduced = tips + apply_four(mixer_here, before)
    settled = apply_four(pick(inverses, slab_index), reduced)
    back_here = pick(backs, slab_index)
    after = carried_in(
        (back_here, settled), "gy", compose, (identity_four, jnp.zeros_like(tips)), True
    )[1]
    own_tips = settled + apply_four(back_here, after)
    prev_index = jnp.maximum(slab_index - 1, 0)
    below = apply_four(
        pick(inverses, prev_index), before - apply_four(pick(link_up, prev_index), own_tips)
    )
    lower_vals = below[2:4]
    upper_vals = after[0:2]
    increment = (
        partial_value
        - jnp.einsum("jm,mcxz->cxjz", pick(lower_fix, slab_index), lower_vals, precision=HIGH)
        - jnp.einsum("jm,mcxz->cxjz", pick(upper_fix, slab_index), upper_vals, precision=HIGH)
    )
    velocity_new = velocity + increment
    return (velocity_new, section_new, part_new)


def solution(mesh):
    return jax.shard_map(
        local,
        mesh=mesh,
        in_specs=(
            P(None, "gx", "gy", None),
            P(None, "gx", "gy", None),
            P(),
            P("gy"),
            P("gy"),
            P(None, ("gx", "gy")),
            P(("gx", "gy")),
            P(("gx", "gy"), None),
            P(("gx", "gy"), None),
        ),
        out_specs=(P(None, "gx", "gy", None), P(None, "gx", "gy", None), P(None, ("gx", "gy"))),
        check_vma=False,
    )
```

profile of v0, /device:TPU:1, one launch (start us, length us, event | category | flops | bytes accessed | tf_op | source)
XLA Modules:
  0.0 717.0 jit_solution(17546694882314400195)
XLA Ops:
  13.3 10.5 %all-to-all-start = ((f32[1,128,64]{2,0,1:T(1,128)}), f32[1,128,64]{2,0,1:T(1,128)S(1)}, u32[]{:S(2)}, u32[]{:S(2)}) async-start(f32[1,128,64]{2,0,1:T(1,128)} %bitcast.17), calls=%async_computation | async-start | bytes 131072 | tf_op jit(solution)/shard_map/all_to_all | solution.py:162
  48.1 13.4 %while.99 = (s32[]{:T(128)}, f32[32,32,32]{0,2,1:T(8,128)S(1)}, f32[32,32,32]{0,2,1:T(8,128)S(1)}, s32[]{:T(128)}, s32[]{:T(128)}, /*index=5*/s32[]{:T(128)}) while((s32[]{:T(128)}, f32[32,32,32]{0,2,1:T(8,128)S(1)}, f32[32,32,32]{0,2,1:T(8,128)S(1)}, s32[]{:T(128)}, s32[]{:T(128)}, /*index=5*/s32[]{:T(128)}) %tuple.258), condition=%wide.region_2.3_spmd.clone, body=%wide.region_1.2_spmd.clone.sunk | while | flops 199715 | bytes 561733 | solution.py:71
  73.1 48.9 %gather_fusion = s32[8192]{0:T(1024)S(1)} fusion(s32[128]{0:T(128)S(1)} %bitcast.225, s32[8192]{0:T(1024)S(1)} %broadcast_clamp_fusion), kind=kCustom, calls=%fused_computation | custom fusion | bytes 98304 | tf_op jit(solution)/shard_map/jit(_take)/gather | solution.py:166
  127.2 8.4 %all-to-all-start.1 = ((f32[128,1,192]{2,1,0:T(1,128)}), f32[128,1,192]{2,1,0:T(1,128)S(1)}, u32[]{:S(2)}, u32[]{:S(2)}) async-start(f32[128,1,192]{2,1,0:T(1,128)} %reshape.597), calls=%async_computation.1 | async-start | bytes 262144 | tf_op jit(solution)/shard_map/all_to_all | solution.py:161
  137.4 8.2 %all-to-all-done.1 = f32[128,1,192]{2,1,0:T(1,128)S(1)} async-done(((f32[128,1,192]{2,1,0:T(1,128)}), f32[128,1,192]{2,1,0:T(1,128)S(1)}, u32[]{:S(2)}, u32[]{:S(2)}) %all-to-all-start.1) | async-done | bytes 98336 | tf_op jit(solution)/shard_map/all_to_all | solution.py:161
  151.2 10.5 %fusion.21 = f32[8192,384]{0,1:T(8,128)} fusion(bf16[384,1024]{1,0:T(8,128)(2,1)S(1)} %bitcast.230, s32[8192]{0:T(1024)S(1)} %bitcast.240), kind=kOutput, calls=%fused_computation.47 | convolution fusion | flops 6450839552 | bytes 13402112 | tf_op jit(solution)/shard_map/hz,zp->hp/dot_general | solution.py:175
  161.7 7.5 %multiply_reduce_fusion = f32[3,8192]{1,0:T(4,128)S(1)} fusion(f32[3,128,8192]{2,1,0:T(8,128)} %bitcast.226, f32[128,8192]{1,0:T(8,128)} %fusion.27), kind=kLoop, calls=%fused_computation.51 | loop fusion | flops 6266880 | bytes 16875520 | tf_op jit(solution)/shard_map/reduce_sum | solution.py:176
  173.8 16.5 %fusion.40 = f32[3,4,32,1024]{3,2,1,0:T(8,128)} fusion(f32[3,4,2,1024]{3,2,1,0:T(2,128)} %collective-permute-done.3, f32[3,4,32,1024]{3,2,1,0:T(8,128)S(1)} %copy-done.2, f32[3,4,34,1024]{3,2,1,0:T(8,128)} %constant_dynamic-update-slice_fusion.4, f32[3,6,32,1024]{3,2,1,0:T(8,128)} %get-tuple-element.824, ...), kind=kOutput, calls=%fused_computation.70 | convolution fusion | flops 6465388544 | bytes 24297728 | tf_op jit(solution)/shard_map/hp,zp->hz/dot_general | solution.py:186
  194.5 297.7 %while.101 = (s32[]{:T(128)}, f32[4,4]{0,1:T(4,128)S(1)}, f32[4,4]{1,0:T(4,128)S(1)}, f32[32,4,4]{2,1,0:T(4,128)}, f32[32,4,4]{2,1,0:T(4,128)}, /*index=5*/f32[3...) while((s32[]{:T(128)}, f32[4,4]{0,1:T(4,128)S(1)}, ...), condition=%wide.region_6.7_spmd.clone, body=%wide.region_3.6_spmd.clone.sunk | while | flops 1753 | bytes 10358 | solution.py:124
  196.2 6.3 while.102
  205.5 6.3 while.102
  214.8 6.3 while.102
  224.1 6.3 while.102
  233.3 6.3 while.102
  242.7 6.3 while.102
  251.9 6.3 while.102
  261.2 6.3 while.102
  270.5 6.3 while.102
  279.8 6.3 while.102
  289.0 6.3 while.102
  298.4 6.3 while.102
  316.9 6.3 while.102
  335.6 6.3 while.102
  354.2 6.3 while.102
  363.4 6.3 while.102
  372.8 6.3 while.102
  382.2 6.3 while.102
  391.4 6.3 while.102
  492.9 24.8 %all_gather.20 = f32[32,4,4]{2,1,0:T(4,128)} all-gather(f32[1,4,4]{2,1,0:T(4,128)S(1)} %constant_dynamic-slice_fusion.7), channel_id=1, replica_groups=mesh['gx'=4,'gy'=32] {'gy'}, dimensions={0}, use_global_device_ids=true | all-gather | bytes 2112 | tf_op jit(solution)/shard_map/all_gather | solution.py:34
  524.5 89.8 %all_gather.23 = f32[32,4,4]{2,1,0:T(4,128)} all-gather(f32[1,4,4]{2,1,0:T(4,128)S(1)} %dynamic-slice_negate_fusion), channel_id=1, replica_groups=mesh['gx'=4,'gy'=32] {'gy'}, dimensions={0}, use_global_device_ids=true | all-gather | bytes 2112 | tf_op jit(solution)/shard_map/all_gather | solution.py:34
  615.0 19.9 %all-gather.7.cloned.1.call-done = f32[128,3,4,1024]{3,2,1,0:T(4,128)} async-done(((f32[4,3,4,1024]{3,2,1,0:T(4,128)}), f32[128,3,4,1024]{3,2,1,0:T(4,128)}) %all-gather.7.cloned.1.call-update) | async-done | bytes 6291472 | tf_op jit(solution)/shard_map/all_gather | solution.py:34
  634.9 66.2 %while.98 = (s32[]{:T(128)}, f32[4,3,4,1024]{3,0,2,1:T(4,128)S(1)}, s32[]{:T(128)}, f32[32,4,4]{2,1,0:T(4,128)}, f32[32,4,3,4,1024]{4,3,2,1,0:T(4,128)}, /*index=5*/s32[]{:T(128)}, s32[]{:T(128)}, s32[]{:T(128)}, s32[]{:T(128)}) while((s32[]{:T(128)}, f32[4,3,4,1024]{3,0,2,1:T(4,128)S(1)}, s32[]{:T(128)}, f32[32,4,4]{2,1,0:T(4,128)}, ...), condition=%wide.region_10.11_spmd, body=%wide.region_9.10_spmd.sunk | while | flops 2408454 | bytes 1378451 | solution.py:43
  (1314 shorter events, 536.4 us)
Async XLA Ops:
  7.2 65.9 %copy-start = (s32[1,128]{1,0:T(1,128)S(1)}, s32[1,128]{1,0:T(1,128)}, u32[]{:S(2)}) copy-start(s32[1,128]{1,0:T(1,128)} %param.40) | copy-start | bytes 1540
  7.2 19.9 %copy-start.2 = (f32[3,4,32,1024]{3,2,1,0:T(8,128)S(1)}, f32[3,4,32,1024]{3,2,1,0:T(8,128)}, u32[]{:S(2)}) copy-start(f32[3,4,32,1024]{3,2,1,0:T(8,128)} %param.33) | copy-start | bytes 4718596
  7.2 5.4 copy-start.16
  10.1 137.3 %collective-permute-start.1 = (f32[3,2,32,1024]{3,2,1,0:T(8,128)}, f32[3,2,32,1024]{3,2,1,0:T(8,128)S(1)}, u32[]{:S(2)}, u32[]{:S(2)}) collective-permute-start(f32[3,2,32,1024]{3,2,1,0:T(8,128)} %get-tuple-element.835), channel_id=1, source_target_pairs={{0,32},{32,64},{64,96},{96,0},{1,33},{33,65},{65,97},{97,1},{2,34}... | collective-permute-start | bytes 2359304 | tf_op jit(solution)/shard_map/ppermute | solution.py:22
  13.3 113.9 %all-to-all-start = ((f32[1,128,64]{2,0,1:T(1,128)}), f32[1,128,64]{2,0,1:T(1,128)S(1)}, u32[]{:S(2)}, u32[]{:S(2)}) async-start(f32[1,128,64]{2,0,1:T(1,128)} %bitcast.17), calls=%async_computation | async-start | bytes 131072 | tf_op jit(solution)/shard_map/all_to_all | solution.py:162
  23.8 146.3 %collective-permute-start = (f32[3,2,32,1024]{3,2,1,0:T(8,128)}, f32[3,2,32,1024]{3,2,1,0:T(8,128)}, u32[]{:S(2)}, u32[]{:S(2)}) collective-permute-start(f32[3,2,32,1024]{3,2,1,0:T(8,128)} %get-tuple-element.834), channel_id=1, source_target_pairs={{32,0},{64,32},{96,64},{0,96},{33,1},{65,33},{97,65},{1,97},{34,2}... | collective-permute-start | bytes 2359304 | tf_op jit(solution)/shard_map/ppermute | solution.py:25
  27.9 144.4 %collective-permute-start.2 = (f32[3,4,2,1024]{3,2,1,0:T(2,128)}, f32[3,4,2,1024]{3,2,1,0:T(2,128)}, u32[]{:S(2)}, u32[]{:S(2)}) collective-permute-start(f32[3,4,2,1024]{3,2,1,0:T(2,128)} %get-tuple-element.836), channel_id=1, source_target_pairs={{1,0},{2,1},{3,2},{4,3},{5,4},{6,5},{7,6},{8,7},{9,8},{10,9},{11,1... | collective-permute-start | bytes 294920 | tf_op jit(solution)/shard_map/ppermute | solution.py:25
  30.4 143.4 %collective-permute-start.3 = (f32[3,4,2,1024]{3,2,1,0:T(2,128)}, f32[3,4,2,1024]{3,2,1,0:T(2,128)}, u32[]{:S(2)}, u32[]{:S(2)}) collective-permute-start(f32[3,4,2,1024]{3,2,1,0:T(2,128)} %get-tuple-element.837), channel_id=1, source_target_pairs={{0,1},{1,2},{2,3},{3,4},{4,5},{5,6},{6,7},{7,8},{8,9},{9,10},{10,1... | collective-permute-start | bytes 294920 | tf_op jit(solution)/shard_map/ppermute | solution.py:22
  36.9 2.2 copy-start.19
  36.9 4.5 copy-start.17
  42.2 2.4 copy-start.10
  62.0 60.0 %copy-start.3 = (f32[32,32,32]{2,1,0:T(8,128)}, f32[32,32,32]{2,1,0:T(8,128)S(1)}, u32[]{:S(2)}) copy-start(f32[32,32,32]{2,1,0:T(8,128)S(1)} %copy.110) | copy-start | bytes 393220
  67.9 0.6 copy-start.6
  72.4 0.6 copy-start.7
  73.1 48.9 %copy-start.14 = (f32[32,2,2]{1,2,0:T(2,128)}, f32[32,2,2]{1,2,0:T(2,128)S(1)}, u32[]{:S(2)}) copy-start(f32[32,2,2]{1,2,0:T(2,128)S(1)} %get-tuple-element.842) | copy-start | bytes 1540
  73.1 48.9 %copy-start.15 = (f32[32,2,2]{1,2,0:T(2,128)}, f32[32,2,2]{1,2,0:T(2,128)S(1)}, u32[]{:S(2)}) copy-start(f32[32,2,2]{1,2,0:T(2,128)S(1)} %get-tuple-element.843) | copy-start | bytes 1540
  122.9 2.3 copy-start.13
  127.2 18.4 %all-to-all-start.1 = ((f32[128,1,192]{2,1,0:T(1,128)}), f32[128,1,192]{2,1,0:T(1,128)S(1)}, u32[]{:S(2)}, u32[]{:S(2)}) async-start(f32[128,1,192]{2,1,0:T(1,128)} %reshape.597), calls=%async_computation.1 | async-start | bytes 262144 | tf_op jit(solution)/shard_map/all_to_all | solution.py:161
  135.6 382.1 %all-gather.5.cloned.1.call-start = ((), (), s32[]{:S(2)}) async-start(), calls=%async_computation.2 | async-start | bytes 6488064 | tf_op jit(solution)/shard_map/all_gather | solution.py:34
  148.3 2.8 copy-start.18
  161.7 7.5 %copy-start.11 = (f32[8192]{0:T(1024)S(1)}, f32[8192]{0:T(1024)}, u32[]{:S(2)}) copy-start(f32[8192]{0:T(1024)} %mul.387) | copy-start | bytes 98308
  161.7 7.5 %copy-start.12 = (f32[8192]{0:T(1024)S(1)}, f32[8192]{0:T(1024)}, u32[]{:S(2)}) copy-start(f32[8192]{0:T(1024)} %neg.26) | copy-start | bytes 98308
  169.3 4.6 copy-start.5
  169.3 4.5 copy-start.8
  169.3 4.5 copy-start.20
  170.1 3.8 copy-start.9
  170.1 3.8 copy-start.21
  194.5 440.4 %all-gather.7.cloned.1.call-start = ((), (), s32[]{:S(2)}) async-start(), calls=%async_computation.3 | async-start | bytes 6488064 | tf_op jit(solution)/shard_map/all_gather | solution.py:34
  521.7 0.7 copy-start.4
  706.4 3.8 copy-start.1
Sparse Core Ops, SparseCore 0:
  194.6 45.4 all-gather.4
  523.3 111.4 all-gather.6
where the time goes:
time: 723 us; the launch traced here: 717 us
  local copies, waits for them, and re-layouts  241 us (33%)
  other arithmetic  155 us (21%)
  matrix products  129 us (18%)
  blocking collectives  115 us (16%)
  starting transfers between devices  30.3 us (4%)
  waiting for transfers between devices  28.2 us (4%)
  between operations  14.6 us (2%)
    all_gather x2, blocking collectives, carried_in(): gathered = jax.tree.map(lambda a: lax.all_gather(a, axis), part)  115 us
    div x128, other arithmetic, eliminate(): head_work = head_work / pivot_value  108 us
    dynamic_slice x128, local copies, waits for them, and re-layouts, eliminate(): lax.dynamic_index_in_dim(head_work, row_index, head_work.ndim - 1, keepdi...  78.6 us
    gather x1, local copies, waits for them, and re-layouts, local(): jnp.repeat(counts[0], slot_count, total_repeat_length=total_slots)  48.9 us
    dot_general x32, matrix products, advance(): mixer = -jnp.dot(down_here, prev_inverse, precision=HIGH)  43.5 us
    dot_general x36, matrix products, apply_four(): return jnp.einsum('ab,bcxz->acxz', matrix, vectors, precision=HIGH)  42.2 us
    dynamic_slice x31, local copies, waits for them, and re-layouts, one(): lax.dynamic_index_in_dim(a, source, 0, False)  29.3 us
    dynamic_slice x64, local copies, waits for them, and re-layouts, schur_factors(): final_state, stacked = lax.scan(advance, start_state, (link_down, link_up))  24 us
  transfers between devices with their start and end apart: 8, of which 2 were waited for; matrix products, arithmetic and copies ran while one was open for 58% of the time, Pallas kernels for 0%

commit v1 on v0

v1 whole, which is shorter than its diff:
```python
import jax
import jax.numpy as jnp
from jax import lax
from jax.experimental import pallas as pl
from jax.experimental.pallas import tpu as pltpu
from jax.sharding import PartitionSpec as P

TIME_STEP = 0.2
SECTION_KEEP = -5.0 / 9.0
SECTION_GAIN = 15.0 / 16.0
MAIN = 2.5
NEAR = -4.0 / 3.0
FAR = 1.0 / 12.0
SLABS = 32
ROWS = 32
CX = 4
CZ = 1024
PLANES = CX * ROWS
SLOTS = 64
PEERS = 128
TOTAL = PEERS * SLOTS
CHUNK = 1024
HIGH = lax.Precision.HIGHEST
F32 = jnp.float32
BF16 = jnp.bfloat16


def params(mib=60):
    return pltpu.CompilerParams(vmem_limit_bytes=mib * 1024 * 1024)


VMEM = pl.BlockSpec(memory_space=pltpu.MemorySpace.VMEM)
SMEM = pl.BlockSpec(memory_space=pltpu.MemorySpace.SMEM)
ANY = pl.BlockSpec(memory_space=pl.ANY)


def shaped(*shape):
    return jax.ShapeDtypeStruct(shape, F32)


def mm(a, b):
    return tuple(
        tuple(a[i][0] * b[0][j] + a[i][1] * b[1][j] for j in range(2)) for i in range(2)
    )


def add(a, b, sign=1.0):
    return tuple(tuple(a[i][j] + sign * b[i][j] for j in range(2)) for i in range(2))


def neg(a):
    return tuple(tuple(-e for e in row) for row in a)


def each(a, fn):
    return tuple(tuple(fn(e) for e in row) for row in a)


def inverse_of_one_minus(a):
    p, q, r, s = 1.0 - a[0][0], -a[0][1], -a[1][0], 1.0 - a[1][1]
    scale = 1.0 / (p * s - q * r)
    return ((s * scale, -q * scale), (-r * scale, p * scale))


def factor_kernel(place_ref, rate_ref, scale_ref, tip_ref, fix_ref, solve_ref, green_ref, wide_ref, coef_ref):
    slab = place_ref[0]
    lane8 = lax.broadcasted_iota(jnp.int32, (8, 128), 1)
    sub8 = lax.broadcasted_iota(jnp.int32, (8, 128), 0)
    lane32 = lax.broadcasted_iota(jnp.int32, (ROWS, 128), 1)
    inv_rate = 1.0 / rate_ref[...]
    wide_ref[0:ROWS] = inv_rate + MAIN
    recip, low1, low2 = [], [], []
    zero = jnp.zeros((8, 128), F32)
    for k in range(ROWS):
        main = jnp.broadcast_to(wide_ref[k : k + 1, :], (8, 128))
        if k == 0:
            low1.append(zero)
            low2.append(zero)
            recip.append(1.0 / main)
            continue
        edge = NEAR - FAR * low1[k - 1]
        one = edge * recip[k - 1]
        two = FAR * recip[k - 2] if k > 1 else zero
        low1.append(one)
        low2.append(two)
        recip.append(1.0 / (main - edge * one - FAR * two))
    ends = (0, 1, ROWS - 2, ROWS - 1)
    half = []
    for k in range(ROWS):
        unit = (sub8 == ends.index(k)).astype(F32) if k in ends else zero
        value = unit
        if k > 0:
            value = value - low1[k] * half[k - 1]
        if k > 1:
            value = value - low2[k] * half[k - 2]
        half.append(value)
    full = [None] * ROWS
    for k in reversed(range(ROWS)):
        value = half[k] * recip[k]
        if k < ROWS - 1:
            value = value - low1[k + 1] * full[k + 1]
        if k < ROWS - 2:
            value = value - low2[k + 2] * full[k + 2]
        full[k] = value

    def entry(k, i):
        return jnp.broadcast_to(full[k][i : i + 1, :], (8, 128))

    not_first = ((lane8 > 0) & (lane8 < SLABS)).astype(F32)
    not_last = (lane8 < SLABS - 1).astype(F32)

    def lower(k):
        s0, s1 = entry(k, 0), entry(k, 1)
        return (FAR * s0 * not_first, (NEAR * s0 + FAR * s1) * not_first)

    def upper(k):
        s2, s3 = entry(k, 2), entry(k, 3)
        return ((FAR * s2 + NEAR * s3) * not_last, FAR * s3 * not_last)

    low_a = (lower(ends[0]), lower(ends[1]))
    low_c = (lower(ends[2]), lower(ends[3]))
    up_b = (upper(ends[0]), upper(ends[1]))
    up_e = (upper(ends[2]), upper(ends[3]))
    a, b, c, e = low_a, up_b, low_c, up_e
    for hop in (1, 2, 4, 8, 16):
        ax, bx, cx, ex = (each(m, lambda v: pltpu.roll(v, hop, 1)) for m in (a, b, c, e))
        w = inverse_of_one_minus(mm(a, ex))
        wa_c = mm(w, mm(a, cx))
        wb = mm(w, b)
        cy_ex = mm(c, ex)
        new_e = add(e, mm(cy_ex, wb))
        new_c = neg(add(mm(c, cx), mm(cy_ex, wa_c)))
        new_a = add(ax, mm(bx, wa_c))
        new_b = neg(mm(bx, wb))
        joined = lane8 >= hop

        def pick(new, old):
            return tuple(
                tuple(jnp.where(joined, new[i][j], old[i][j]) for j in range(2)) for i in range(2)
            )

        a, b, c, e = pick(new_a, a), pick(new_b, b), pick(new_c, c), pick(new_e, e)
    q = e
    q_prev = each(q, lambda v: jnp.where(lane8 > 0, pltpu.roll(v, 1, 1), 0.0))
    z = inverse_of_one_minus(mm(low_a, q_prev))
    gain = mm(mm(low_c, q_prev), z)
    carry = add(low_c, mm(gain, low_a))
    z_low = mm(z, low_a)
    z_up = mm(z, up_b)
    for group, mats in enumerate(((carry, gain), (z, z_low), (z_up, q))):
        block = jnp.zeros((8, 128), F32)
        for n, m in enumerate(mats):
            for i in range(2):
                for j in range(2):
                    block = jnp.where(sub8 == 4 * n + 2 * i + j, m[i][j], block)
        for s in range(SLABS):
            coef_ref[s, 8 * group : 8 * group + 8, :] = jnp.broadcast_to(block[:, s : s + 1], (8, 128))

    def coef(s, n):
        def one(i, j):
            at = 4 * n + 2 * i + j
            return jnp.broadcast_to(coef_ref[s, at : at + 1, :], (8, 128))

        return tuple(tuple(one(i, j) for j in range(2)) for i in range(2))

    def at_lane(n):
        return lane8 == n

    forward = []
    prev = None
    for s in range(SLABS):
        m, g = coef(s, 0), coef(s, 1)
        now = []
        for i in range(2):
            value = jnp.where(at_lane(4 * s), g[i][0], 0.0)
            value = jnp.where(at_lane(4 * s + 1), g[i][1], value)
            value = jnp.where(at_lane(4 * s + 2 + i), 1.0, value)
            if prev is not None:
                value = value - m[i][0] * prev[0] - m[i][1] * prev[1]
            now.append(value)
        forward.append(now)
        prev = now
    for row in (0, 1, 4 * SLABS - 2, 4 * SLABS - 1):
        green_ref[row : row + 1, :] = jnp.zeros((1, 128), F32)
    after = None
    for s in reversed(range(SLABS)):
        zc, zl, zu, qc = coef(s, 2), coef(s, 3), coef(s, 4), coef(s, 5)
        now = []
        for i in range(2):
            value = jnp.where(at_lane(4 * s), zc[i][0], 0.0)
            value = jnp.where(at_lane(4 * s + 1), zc[i][1], value)
            if s > 0:
                value = value - zl[i][0] * forward[s - 1][0] - zl[i][1] * forward[s - 1][1]
            if after is not None:
                value = value - zu[i][0] * after[0] - zu[i][1] * after[1]
            now.append(value)
        if s < SLABS - 1:
            for i in range(2):
                high = forward[s][i] - qc[i][0] * after[0] - qc[i][1] * after[1]
                green_ref[4 * (s + 1) + i : 4 * (s + 1) + i + 1, :] = high[0:1]
        if s > 0:
            for i in range(2):
                green_ref[4 * (s - 1) + 2 + i : 4 * (s - 1) + 3 + i, :] = now[i][0:1]
        after = now

    for k in range(ROWS):
        wide_ref[k : k + 1, :] = low1[k][0:1]
        wide_ref[ROWS + k : ROWS + k + 1, :] = low2[k][0:1]
        wide_ref[2 * ROWS + k : 2 * ROWS + k + 1, :] = recip[k][0:1]
    own = lane32 == slab

    def own_column(v):
        return jnp.broadcast_to(jnp.sum(jnp.where(own, v, 0.0), axis=1, keepdims=True), (ROWS, 128))

    for part in range(3):
        wide_ref[part * ROWS : (part + 1) * ROWS, :] = own_column(
            wide_ref[part * ROWS : (part + 1) * ROWS, :]
        )
    scale_ref[...] = SECTION_GAIN * own_column(inv_rate)

    def wide(part, k):
        return jnp.broadcast_to(wide_ref[part * ROWS + k : part * ROWS + k + 1, :], (8, 128))

    half = []
    for k in range(ROWS):
        value = (lane8 == k).astype(F32)
        if k > 0:
            value = value - wide(0, k) * half[k - 1]
        if k > 1:
            value = value - wide(1, k) * half[k - 2]
        half.append(value)
    full = [None] * ROWS
    for k in reversed(range(ROWS)):
        value = half[k] * wide(2, k)
        if k < ROWS - 1:
            value = value - wide(0, k + 1) * full[k + 1]
        if k < ROWS - 2:
            value = value - wide(1, k + 2) * full[k + 2]
        full[k] = value
        solve_ref[k : k + 1, :] = value[0:1]
    solve = solve_ref[...]
    cols = [jnp.broadcast_to(solve[:, n : n + 1], (ROWS, 128)) for n in ends]
    for n in range(4):
        tip_ref[n] = cols[n]
    has_low = jnp.where(slab > 0, 1.0, 0.0)
    has_high = jnp.where(slab < SLABS - 1, 1.0, 0.0)
    fix_ref[0] = FAR * cols[0] * has_low
    fix_ref[1] = (NEAR * cols[0] + FAR * cols[1]) * has_low
    fix_ref[2] = (FAR * cols[2] + NEAR * cols[3]) * has_high
    fix_ref[3] = FAR * cols[3] * has_high


def factors(place, rate):
    return pl.pallas_call(
        factor_kernel,
        out_shape=(
            shaped(ROWS, 128),
            shaped(4, ROWS, 128),
            shaped(4, ROWS, 128),
            shaped(ROWS, 128),
            shaped(128, 128),
        ),
        in_specs=[SMEM, VMEM],
        out_specs=(VMEM,) * 5,
        scratch_shapes=[pltpu.VMEM((3 * ROWS, 128), F32), pltpu.VMEM((SLABS, 24, 128), F32)],
        name="factors",
    )(place, rate)


def pack_kernel(vel_ref, rate_ref, out_ref):
    left = lax.broadcasted_iota(jnp.int32, (1, 128), 1) < SLOTS
    for r in range(PEERS // 2):
        part = [vel_ref[i : i + 1, 128 * r : 128 * r + 128] for i in range(3)]
        part.append(rate_ref[0:1, 128 * r : 128 * r + 128])
        for n in range(2):
            one, two = part[2 * n], part[2 * n + 1]
            out_ref[2 * r, n : n + 1, :] = jnp.where(left, one, pltpu.roll(two, SLOTS, 1))
            out_ref[2 * r + 1, n : n + 1, :] = jnp.where(left, pltpu.roll(one, SLOTS, 1), two)


def packed(part_vel, part_rate):
    return pl.pallas_call(
        pack_kernel,
        out_shape=shaped(PEERS, 2, 128),
        in_specs=[VMEM, VMEM],
        out_specs=VMEM,
        name="pack",
    )(part_vel, part_rate)


def halves(cells):
    plane = cells >> 10
    span = cells & (CZ - 1)
    return plane, span >> 7, span & 127


def span_table(high, low):
    width = high.shape[1]
    inner = lax.broadcasted_iota(jnp.int32, (128, width), 0) == low
    inner = inner.astype(F32).astype(BF16)
    rows = []
    for t in range(8):
        flag = (high == t).astype(F32).astype(BF16)
        rows.append(inner * flag)
    return jnp.concatenate(rows, axis=0)


def gather_kernel(vel_ref, cell_ref, out_ref, bf_ref):
    @pl.when(pl.program_id(0) == 0)
    def _():
        bf_ref[...] = vel_ref[...].astype(BF16)

    plane, high, low = halves(cell_ref[...])
    table = span_table(high, low)
    at = jnp.dot(bf_ref[...], table, preferred_element_type=F32)
    mask = lax.broadcasted_iota(jnp.int32, (PLANES, CHUNK), 0) == plane
    for n in range(3):
        out_ref[n : n + 1, :] = jnp.sum(
            jnp.where(mask, at[n * PLANES : (n + 1) * PLANES], 0.0), axis=0, keepdims=True
        )


def gathered(velocity, cells):
    return pl.pallas_call(
        gather_kernel,
        grid=(TOTAL // CHUNK,),
        out_shape=shaped(3, TOTAL),
        in_specs=[
            pl.BlockSpec((3 * PLANES, CZ), lambda i: (0, 0)),
            pl.BlockSpec((1, CHUNK), lambda i: (0, i)),
        ],
        out_specs=pl.BlockSpec((3, CHUNK), lambda i: (0, i)),
        scratch_shapes=[pltpu.VMEM((3 * PLANES, CZ), BF16)],
        compiler_params=params(),
        name="gather",
    )(velocity.reshape(3 * PLANES, CZ), cells)


def deposit_kernel(moved_ref, count_ref, cell_ref, fluid_ref, part_ref, sum_ref, got_ref):
    step = pl.program_id(0)
    senders = CHUNK // SLOTS
    left = lax.broadcasted_iota(jnp.int32, (1, 128), 1) < SLOTS
    lane = lax.broadcasted_iota(jnp.int32, (1, 128), 1)
    for r in range(senders // 2):
        for n in range(2):
            one = moved_ref[2 * r, n : n + 1, :]
            two = moved_ref[2 * r + 1, n : n + 1, :]
            got_ref[2 * n : 2 * n + 1, 128 * r : 128 * r + 128] = jnp.where(
                left, one, pltpu.roll(two, SLOTS, 1)
            )
            got_ref[2 * n + 1 : 2 * n + 2, 128 * r : 128 * r + 128] = jnp.where(
                left, pltpu.roll(one, SLOTS, 1), two
            )
        first = step * senders + 2 * r
        limit = jnp.where(left, count_ref[0, first], count_ref[0, first + 1])
        got_ref[4:5, 128 * r : 128 * r + 128] = ((lane & (SLOTS - 1)) < limit).astype(F32)
    live = got_ref[4:5, :] > 0.5
    rate = got_ref[3:4, :]
    plane, high, low = halves(cell_ref[...])
    table = span_table(high, low)
    mask = (lax.broadcasted_iota(jnp.int32, (PLANES, CHUNK), 0) == plane).astype(F32).astype(BF16)
    spread = []
    for n in range(3):
        old = got_ref[n : n + 1, :]
        relative = fluid_ref[n : n + 1, :] - old
        part_ref[n : n + 1, :] = jnp.where(live, old + TIME_STEP * rate * relative, 0.0)
        push = jnp.where(live, -rate * relative, 0.0).astype(BF16)
        spread.append(mask * push)
    spread = jnp.concatenate(spread, axis=0)
    new = lax.dot_general(
        spread, table, (((1,), (1,)), ((), ())), preferred_element_type=F32
    )

    @pl.when(step == 0)
    def _():
        sum_ref[...] = new

    @pl.when(step > 0)
    def _():
        sum_ref[...] += new


def deposited(moved, counts, cells, fluid):
    senders = CHUNK // SLOTS
    return pl.pallas_call(
        deposit_kernel,
        grid=(TOTAL // CHUNK,),
        out_shape=(shaped(3, TOTAL), shaped(3 * PLANES, CZ)),
        in_specs=[
            pl.BlockSpec((senders, 2, 128), lambda i: (i, 0, 0)),
            SMEM,
            pl.BlockSpec((1, CHUNK), lambda i: (0, i)),
            pl.BlockSpec((3, CHUNK), lambda i: (0, i)),
        ],
        out_specs=(
            pl.BlockSpec((3, CHUNK), lambda i: (0, i)),
            pl.BlockSpec((3 * PLANES, CZ), lambda i: (0, 0)),
        ),
        scratch_shapes=[pltpu.VMEM((8, CHUNK), F32)],
        compiler_params=params(),
        name="deposit",
    )(moved, counts, cells, fluid)


def column_of(row, length):
    wide = jnp.broadcast_to(row, (length, length))
    here = lax.broadcasted_iota(jnp.int32, (length, length), 0) == lax.broadcasted_iota(
        jnp.int32, (length, length), 1
    )
    return jnp.broadcast_to(
        jnp.sum(jnp.where(here, wide, 0.0), axis=1, keepdims=True), (length, 128)
    )


def rhs_kernel(
    vel_hbm, below_hbm, above_hbm, before_ref, behind_ref, section_ref, deposit_ref,
    near_ref, far_ref, scale_ref, tip_ref, out_ref, tips_ref, pad_ref, coef_ref, sems,
):
    copies = [
        pltpu.make_async_copy(vel_hbm, pad_ref.at[:, :, 8 : 8 + ROWS, :], sems.at[0]),
        pltpu.make_async_copy(below_hbm, pad_ref.at[:, :, 6:8, :], sems.at[1]),
        pltpu.make_async_copy(above_hbm, pad_ref.at[:, :, 8 + ROWS : 10 + ROWS, :], sems.at[2]),
    ]
    for copy in copies:
        copy.start()
    coef_ref[0] = column_of(near_ref[...], ROWS)
    coef_ref[1] = column_of(far_ref[...], ROWS)
    for copy in copies:
        copy.wait()

    def tiled(column):
        return jnp.concatenate([column] * 8, axis=1)

    def one(c, carry):
        for x in range(CX):
            def layer(i, rows):
                if i < 0:
                    return before_ref[c, 2 + i, rows, :]
                if i >= CX:
                    return behind_ref[c, i - CX, rows, :]
                return pad_ref[c, i, pl.ds(8 + rows.start, 8), :]

            tips = [[None] * 8 for _ in range(4)]
            for t in range(ROWS // 8):
                rows = pl.ds(8 * t, 8)
                here = layer(x, rows)
                ddx = (8.0 / 12.0) * (layer(x + 1, rows) - layer(x - 1, rows)) - (1.0 / 12.0) * (
                    layer(x + 2, rows) - layer(x - 2, rows)
                )
                rolled = {k: pltpu.roll(here, (-k) % CZ, 1) for k in (1, -1, 2, -2)}
                ddz = (8.0 / 12.0) * (rolled[1] - rolled[-1]) - (1.0 / 12.0) * (
                    rolled[2] - rolled[-2]
                )

                def shifted(k):
                    return pad_ref[c, x, 8 + 8 * t + k : 16 + 8 * t + k, :]

                near = tiled(coef_ref[0, 8 * t : 8 * t + 8, :])
                far = tiled(coef_ref[1, 8 * t : 8 * t + 8, :])
                ddy = near * (shifted(1) - shifted(-1)) + far * (shifted(2) - shifted(-2))
                top = pl.ds(8 + 8 * t, 8)
                moved = (
                    pad_ref[0, x, top, :] * ddx
                    + pad_ref[1, x, top, :] * ddy
                    + pad_ref[2, x, top, :] * ddz
                )
                rhs = deposit_ref[c, x, rows, :] - moved
                new = SECTION_KEEP * section_ref[c, x, rows, :] + TIME_STEP * rhs
                out_ref[c, x, rows, :] = new
                scaled = new * tiled(scale_ref[8 * t : 8 * t + 8, :])
                for r in range(4):
                    weighted = scaled * tiled(tip_ref[r, 8 * t : 8 * t + 8, :])
                    tips[r] = weighted if t == 0 else tips[r] + weighted
            for r in range(4):
                tips_ref[c, x, r : r + 1, :] = jnp.sum(tips[r], axis=0, keepdims=True)
        return carry

    lax.fori_loop(0, 3, one, 0)


def right_side(velocity, below, above, before, behind, section, deposit, near, far, scale, tip):
    return pl.pallas_call(
        rhs_kernel,
        out_shape=(shaped(3, CX, ROWS, CZ), shaped(3, CX, 4, CZ)),
        in_specs=[ANY, ANY, ANY] + [VMEM] * 8,
        out_specs=(VMEM, VMEM),
        scratch_shapes=[
            pltpu.VMEM((3, CX, ROWS + 16, CZ), F32),
            pltpu.VMEM((2, ROWS, 128), F32),
            pltpu.SemaphoreType.DMA((3,)),
        ],
        compiler_params=params(),
        name="right_side",
    )(velocity, below, above, before, behind, section, deposit, near, far, scale, tip)


WIDTH = 3 * CX * CZ // SLABS


def spread_kernel(tips_ref, out_ref):
    for n in range(3 * CX * CZ // 128):
        plane, t = divmod(n, CZ // 128)
        m, k = divmod(n, WIDTH // 128)
        out_ref[m, :, 128 * k : 128 * k + 128] = tips_ref[
            plane // CX, plane % CX, :, 128 * t : 128 * t + 128
        ]


def spread_tips(tips):
    return pl.pallas_call(
        spread_kernel,
        out_shape=shaped(SLABS, 4, WIDTH),
        in_specs=[VMEM],
        out_specs=VMEM,
        name="spread_tips",
    )(tips)


def solve_kernel(tips_ref, green_ref, out_ref, all_ref):
    for s in range(SLABS):
        all_ref[4 * s : 4 * s + 4, :] = tips_ref[s]
    found = jnp.dot(green_ref[...], all_ref[...], precision=HIGH, preferred_element_type=F32)
    for s in range(SLABS):
        out_ref[s] = found[4 * s : 4 * s + 4, :]


def solved(tips, green):
    return pl.pallas_call(
        solve_kernel,
        out_shape=shaped(SLABS, 4, WIDTH),
        in_specs=[VMEM, VMEM],
        out_specs=VMEM,
        scratch_shapes=[pltpu.VMEM((4 * SLABS, WIDTH), F32)],
        name="solve",
    )(tips, green)


def local_kernel(section_ref, scale_ref, solve_ref, out_ref):
    whole = solve_ref[:, 0:ROWS]
    head = whole.astype(BF16)
    rest = (whole - head.astype(F32)).astype(BF16)
    left = jnp.concatenate([head, rest, head], axis=1)
    scale = jnp.concatenate([scale_ref[...]] * 8, axis=1)

    def one(c, carry):
        for x in range(CX):
            value = section_ref[c, x] * scale
            high = value.astype(BF16)
            low = (value - high.astype(F32)).astype(BF16)
            right = jnp.concatenate([high, high, low], axis=0)
            out_ref[c, x] = jnp.dot(left, right, preferred_element_type=F32)
        return carry

    lax.fori_loop(0, 3, one, 0)


def local_solve(section_new, scale, solve):
    return pl.pallas_call(
        local_kernel,
        out_shape=shaped(3, CX, ROWS, CZ),
        in_specs=[VMEM] * 3,
        out_specs=VMEM,
        compiler_params=params(),
        name="local_solve",
    )(section_new, scale, solve)


def final_kernel(vel_ref, partial_ref, edge_ref, fix_ref, out_ref):
    for plane in range(3 * CX):
        c, x = divmod(plane, CX)
        for t in range(CZ // 128):
            m, k = divmod(plane * (CZ // 128) + t, WIDTH // 128)
            lanes = slice(128 * t, 128 * t + 128)
            edge = edge_ref[m, :, 128 * k : 128 * k + 128]
            value = vel_ref[c, x, :, lanes] + partial_ref[c, x, :, lanes]
            for r in range(4):
                value = value - fix_ref[r] * edge[r : r + 1, :]
            out_ref[c, x, :, lanes] = value


def finished(velocity, partial, edges, fix):
    return pl.pallas_call(
        final_kernel,
        out_shape=shaped(3, CX, ROWS, CZ),
        in_specs=[VMEM] * 4,
        out_specs=VMEM,
        compiler_params=params(),
        name="finish",
    )(velocity, partial, edges, fix)


def local(velocity, section, diffusion, rhs_near, rhs_far, part_vel, part_rate, counts, cell_slot):
    n_gx, n_gy = lax.axis_size("gx"), lax.axis_size("gy")
    up_x = [(i, (i + 1) % n_gx) for i in range(n_gx)]
    down_x = [(t, s) for s, t in up_x]
    up_y = [(i, i + 1) for i in range(n_gy - 1)]
    down_y = [(t, s) for s, t in up_y]
    before = lax.ppermute(velocity[:, CX - 2 :], "gx", up_x)
    behind = lax.ppermute(velocity[:, :2], "gx", down_x)
    moved = lax.all_to_all(
        packed(part_vel, part_rate.reshape(1, TOTAL)),
        ("gx", "gy"), split_axis=0, concat_axis=0, tiled=True,
    )
    below = lax.ppermute(velocity[:, :, ROWS - 2 :], "gy", up_y)
    above = lax.ppermute(velocity[:, :, :2], "gy", down_y)
    place = lax.axis_index("gy").astype(jnp.int32).reshape(1)
    rate = jnp.pad(
        diffusion.reshape(SLABS, ROWS).T, ((0, 0), (0, 128 - SLABS)), constant_values=1000.0
    )
    scale, tip, fix, solve, green = factors(place, rate)
    fluid = gathered(velocity, cell_slot)
    part_new, deposit = deposited(moved, counts, cell_slot, fluid)
    section_new, tips = right_side(
        velocity, below, above, before, behind, section, deposit.reshape(3, CX, ROWS, CZ),
        rhs_near.reshape(1, ROWS), rhs_far.reshape(1, ROWS), scale, tip,
    )
    all_tips = lax.all_to_all(spread_tips(tips), "gy", split_axis=0, concat_axis=0, tiled=True)
    partial = local_solve(section_new, scale, solve)
    edges = lax.all_to_all(solved(all_tips, green), "gy", split_axis=0, concat_axis=0, tiled=True)
    velocity_new = finished(velocity, partial, edges, fix)
    return (velocity_new, section_new, part_new)


def solution(mesh):
    return jax.shard_map(
        local,
        mesh=mesh,
        in_specs=(
            P(None, "gx", "gy", None),
            P(None, "gx", "gy", None),
            P(),
            P("gy"),
            P("gy"),
            P(None, ("gx", "gy")),
            P(("gx", "gy")),
            P(("gx", "gy"), None),
            P(("gx", "gy"), None),
        ),
        out_specs=(P(None, "gx", "gy", None), P(None, "gx", "gy", None), P(None, ("gx", "gy"))),
        check_vma=False,
    )
```

time: 723 us -> 99.5 us (0.14)
  local copies, waits for them, and re-layouts: 241 us -> 5.91 us
  other arithmetic: 155 us -> 0 us
  matrix products: 129 us -> 0 us
  blocking collectives: 115 us -> 17.3 us
  Pallas kernels: 0 us -> 45.8 us
  waiting for transfers between devices: 28.2 us -> 4.86 us
  between operations: 14.6 us -> 0.75 us
    dynamic_slice x224 -> x0, local copies, waits for them, and re-layouts: 133 us -> none  [the longest x128 78.6 us: eliminate(): lax.dynamic_index_in_dim(head_work, row_index, head_work.ndim - 1, keepdi...]
    dot_general x108 -> x0, matrix products: 129 us -> none  [the longest x32 43.5 us: advance(): mixer = -jnp.dot(down_here, prev_inverse, precision=HIGH)]
    all_gather x2 -> x0, blocking collectives: 115 us -> none  [carried_in(): gathered = jax.tree.map(lambda a: lax.all_gather(a, axis), part)]
    div x128 -> x0, other arithmetic: 108 us -> none  [eliminate(): head_work = head_work / pivot_value]
    gather x1 -> x0, local copies, waits for them, and re-layouts: 48.9 us -> none  [local(): jnp.repeat(counts[0], slot_count, total_repeat_length=total_slots)]
    pallas_call x0 -> x9, Pallas kernels: none -> 45.8 us  [the longest x1 11.9 us: deposited(): pl.pallas_call(deposit_kernel, grid=(TOTAL // CHUNK,), out_shape=(shaped(...]
    select_n x196 -> x0, other arithmetic: 22.9 us -> none  [the longest x160 18 us: eliminate(): result = jnp.where(is_head[:, None], head_result[..., None, :], result)]
    all_gather x2 -> x0, waiting for transfers between devices: 19.9 us -> none  [carried_in(): gathered = jax.tree.map(lambda a: lax.all_gather(a, axis), part)]
  transfers between devices with their start and end apart: 8 -> 6, of which waited for: 2 -> 1; matrix products, arithmetic and copies ran while one was open for 58% -> 2% of each run, Pallas kernels for 0% -> 31%
where the time goes in v1:
time: 99.5 us; the launch traced here: 98.8 us
  Pallas kernels  45.8 us (46%)
  starting transfers between devices  24.2 us (24%)
  blocking collectives  17.3 us (17%)
  local copies, waits for them, and re-layouts  5.91 us (6%)
  waiting for transfers between devices  4.86 us (5%)
    all_to_all x1, blocking collectives, local(): lax.all_to_all(spread_tips(tips), 'gy', split_axis=0, concat_axis=0, tile...  17.3 us
    pallas_call x1, Pallas kernels, deposited(): pl.pallas_call(deposit_kernel, grid=(TOTAL // CHUNK,), out_shape=(shaped(...  11.9 us
    pallas_call x1, Pallas kernels, gathered(): pl.pallas_call(gather_kernel, grid=(TOTAL // CHUNK,), out_shape=shaped(3,...  10.6 us
    all_to_all x1, starting transfers between devices, local(): lax.all_to_all(packed(part_vel, part_rate.reshape(1, TOTAL)), ('gx', 'gy'...  10.1 us
    pallas_call x1, Pallas kernels, right_side(): pl.pallas_call(rhs_kernel, out_shape=(shaped(3, CX, ROWS, CZ), shaped(3,...  8.18 us
    all_to_all x1, waiting for transfers between devices, local(): lax.all_to_all(solved(all_tips, green), 'gy', split_axis=0, concat_axis=0...  4.84 us
    ppermute x1, starting transfers between devices, local(): behind = lax.ppermute(velocity[:, :2], 'gx', down_x)  4.66 us
    all_to_all x1, starting transfers between devices, local(): lax.all_to_all(solved(all_tips, green), 'gy', split_axis=0, concat_axis=0...  3.8 us
  transfers between devices with their start and end apart: 6, of which 1 were waited for; matrix products, arithmetic and copies ran while one was open for 2% of the time, Pallas kernels for 31%

profile of v1, /device:TPU:1, one launch (start us, length us, event | category | flops | bytes accessed | tf_op | source)
XLA Modules:
  0.0 98.8 jit_solution(9370313246588028106)
XLA Ops:
  0.6 1.5 %fusion = (f32[3,2,32,1024]{3,2,1,0:T(8,128)S(1)}, f32[3,2,32,1024]{3,2,1,0:T(8,128)S(1)}) fusion(f32[3,4,32,1024]{3,2,1,0:T(8,128)} %vel_ref.3), kind=kLoop, calls=%fused_computation | loop fusion | bytes 3145728 | tf_op jit(solution)/shard_map/slice | solution.py:599
  2.1 4.7 %collective-permute-start.3 = (f32[3,2,32,1024]{3,2,1,0:T(8,128)S(1)}, f32[3,2,32,1024]{3,2,1,0:T(8,128)S(1)}, u32[]{:S(2)}, u32[]{:S(2)}) collective-permute-start(f32[3,2,32,1024]{3,2,1,0:T(8,128)S(1)} %get-tuple-element.21), channel_id=1, source_target_pairs={{32,0},{64,32},{96,64},{0,96},{33,1},{65,33},{97,65},{1,97},{34,2}... | collective-permute-start | bytes 2359304 | tf_op jit(solution)/shard_map/ppermute | solution.py:599
  6.8 0.0 collective-permute-start.2
  6.8 1.9 %pack.1 = f32[128,2,128]{2,1,0:T(2,128)} custom-call(f32[3,8192]{1,0:T(4,128)} %vel_ref.2, f32[1,8192]{1,0:T(1,128)} %bitcast.10), custom_call_target="tpu_custom_call" | custom-call | tf_op jit(solution)/shard_map/pack/pallas_call | solution.py:282
  8.7 10.1 %all-to-all-start = ((f32[128,2,128]{2,1,0:T(2,128)}), f32[128,2,128]{2,1,0:T(2,128)S(1)}, u32[]{:S(2)}, u32[]{:S(2)}) async-start(f32[128,2,128]{2,1,0:T(2,128)} %pack.1), calls=%async_computation | async-start | bytes 262144 | tf_op jit(solution)/shard_map/all_to_all | solution.py:600
  18.8 1.2 %fusion.1 = (f32[3,4,2,1024]{3,2,1,0:T(2,128)S(1)}, f32[3,4,2,1024]{3,2,1,0:T(2,128)S(1)}) fusion(f32[3,4,32,1024]{3,2,1,0:T(8,128)} %vel_ref.3), kind=kLoop, calls=%fused_computation.1 | loop fusion | bytes 393216 | tf_op jit(solution)/shard_map/slice | solution.py:605
  20.0 3.0 %collective-permute-start.1 = (f32[3,4,2,1024]{3,2,1,0:T(2,128)S(1)}, f32[3,4,2,1024]{3,2,1,0:T(2,128)}, u32[]{:S(2)}, u32[]{:S(2)}) collective-permute-start(f32[3,4,2,1024]{3,2,1,0:T(2,128)S(1)} %get-tuple-element.23), channel_id=1, source_target_pairs={{1,0},{2,1},{3,2},{4,3},{5,4},{6,5},{7,6},{8,7},{9,8},{10,9},{11,1... | collective-permute-start | bytes 294920 | tf_op jit(solution)/shard_map/ppermute | solution.py:605
  23.0 2.6 %collective-permute-start = (f32[3,4,2,1024]{3,2,1,0:T(2,128)S(1)}, f32[3,4,2,1024]{3,2,1,0:T(2,128)}, u32[]{:S(2)}, u32[]{:S(2)}) collective-permute-start(f32[3,4,2,1024]{3,2,1,0:T(2,128)S(1)} %get-tuple-element.24), channel_id=1, source_target_pairs={{0,1},{1,2},{2,3},{3,4},{4,5},{5,6},{6,7},{7,8},{8,9},{9,10},{10,1... | collective-permute-start | bytes 294920 | tf_op jit(solution)/shard_map/ppermute | solution.py:604
  25.6 0.1 reshape.33
  25.7 0.1 copy.12
  25.8 0.6 pad.4.rate_ref
  26.4 10.6 %gather.1.fluid_ref = f32[3,8192]{1,0:T(4,128)} custom-call(f32[384,1024]{1,0:T(8,128)} %bitcast.7, s32[1,8192]{1,0:T(1,128)} %cell_ref.3), custom_call_target="tpu_custom_call" | custom-call | tf_op jit(solution)/shard_map/gather/pallas_call | solution.py:324
  36.9 2.8 %factors.1 = (f32[32,128]{1,0:T(8,128)}, f32[4,32,128]{2,1,0:T(8,128)}, f32[4,32,128]{2,1,0:T(8,128)}, f32[32,128]{1,0:T(8,128)}, f32[128,128]{1,0:T(8,128)}) custom-call(s32[1]{0:T(128)} %bitcast.5.place_ref, f32[32,128]{1,0:T(8,128)} %pad.4.rate_ref), custom_call_target="tpu_custom_call" | custom-call | tf_op jit(solution)/shard_map/factors/pallas_call | solution.py:254
  39.7 0.0 all-to-all-done.moved_ref
  39.7 0.7 copy-done.3
  40.4 11.9 %deposit.1 = (f32[3,8192]{1,0:T(4,128)}, f32[384,1024]{1,0:T(8,128)}) custom-call(f32[128,2,128]{2,1,0:T(2,128)} %copy-done.3, s32[1,128]{1,0:T(1,128)} %count_ref.1, s32[1,8192]{1,0:T(1,128)} %cell_ref.3, f32[3,8192]{1,0:T(4,128)} %gather.1.fluid_ref), custom_call_target="tpu_custom_call" | custom-call | tf_op jit(solution)/shard_map/deposit/pallas_call | solution.py:385
  52.3 0.0 collective-permute-done.1.above_hbm
  52.3 0.0 collective-permute-done.below_hbm
  52.3 0.0 collective-permute-done.3.behind_ref
  52.3 0.0 copy-start.1
  52.3 0.0 collective-permute-done.2.before_ref
  52.3 0.9 copy-done.1
  53.2 0.2 copy-done.2
  53.5 8.2 %right_side.1 = (f32[3,4,32,1024]{3,2,1,0:T(8,128)}, f32[3,4,4,1024]{3,2,1,0:T(4,128)}) custom-call(f32[3,4,32,1024]{3,2,1,0:T(8,128)} %vel_ref.3, f32[3,4,2,1024]{3,2,1,0:T(2,128)} %collective-permute-done.below_hbm, f32[3,4,2,1024]{3,2,1,0:T(2,128)} %collective-permute-done.1.above_hbm, f32[3,2,32,1024]{3,2,1,0:T(8,128)} %copy-done.2, ...), custom_call_target="tpu_custom_call" | custom-call | tf_op jit(solution)/shard_map/right_side/pallas_call | solution.py:482
  61.7 1.6 %spread_tips.1 = f32[32,4,384]{2,1,0:T(4,128)} custom-call(f32[3,4,4,1024]{3,2,1,0:T(4,128)} %get-tuple-element.17.tips_ref), custom_call_target="tpu_custom_call" | custom-call | tf_op jit(solution)/shard_map/spread_tips/pallas_call | solution.py:510
  63.3 17.3 %all_to_all.15.tips_ref = f32[32,4,384]{2,1,0:T(4,128)} all-to-all(f32[32,4,384]{2,1,0:T(4,128)} %spread_tips.1), channel_id=1, replica_groups=mesh['gx'=4,'gy'=32] {'gy'}, dimensions={0} | all-to-all | bytes 393216 | tf_op jit(solution)/shard_map/all_to_all | solution.py:617
  80.6 2.0 %solve.1 = f32[32,4,384]{2,1,0:T(4,128)} custom-call(f32[32,4,384]{2,1,0:T(4,128)} %all_to_all.15.tips_ref, f32[128,128]{1,0:T(8,128)} %get-tuple-element.18.green_ref), custom_call_target="tpu_custom_call" | custom-call | tf_op jit(solution)/shard_map/solve/pallas_call | solution.py:528
  82.6 3.8 %all-to-all-start.2 = ((f32[32,4,384]{2,1,0:T(4,128)}), f32[32,4,384]{2,1,0:T(4,128)S(1)}, u32[]{:S(2)}, u32[]{:S(2)}) async-start(f32[32,4,384]{2,1,0:T(4,128)} %solve.1), calls=%async_computation.2 | async-start | bytes 393216 | tf_op jit(solution)/shard_map/all_to_all | solution.py:619
  86.4 3.4 %local_solve.1.partial_ref = f32[3,4,32,1024]{3,2,1,0:T(8,128)} custom-call(f32[3,4,32,1024]{3,2,1,0:T(8,128)} %get-tuple-element.10.section_ref, f32[32,128]{1,0:T(8,128)} %get-tuple-element.13.scale_ref, f32[32,128]{1,0:T(8,128)} %get-tuple-element.16.solve_ref), custom_call_target="tpu_custom_call" | custom-call | tf_op jit(solution)/shard_map/local_solve/pallas_call | solution.py:558
  89.8 4.8 %all-to-all-done.2.edge_ref = f32[32,4,384]{2,1,0:T(4,128)S(1)} async-done(((f32[32,4,384]{2,1,0:T(4,128)}), f32[32,4,384]{2,1,0:T(4,128)S(1)}, u32[]{:S(2)}, u32[]{:S(2)}) %all-to-all-start.2) | async-done | bytes 196640 | tf_op jit(solution)/shard_map/all_to_all | solution.py:619
  94.7 0.7 copy-done
  95.3 3.5 %finish.1 = f32[3,4,32,1024]{3,2,1,0:T(8,128)} custom-call(f32[3,4,32,1024]{3,2,1,0:T(8,128)} %vel_ref.3, f32[3,4,32,1024]{3,2,1,0:T(8,128)} %local_solve.1.partial_ref, f32[32,4,384]{2,1,0:T(4,128)} %copy-done, f32[4,32,128]{2,1,0:T(8,128)} %get-tuple-element.19.fix_ref), custom_call_target="tpu_custom_call" | custom-call | tf_op jit(solution)/shard_map/finish/pallas_call | solution.py:582
  (5 shorter events, 0.0 us)
Async XLA Ops:
  0.6 25.0 %copy-start.4 = (f32[1024]{0:T(1024)S(1)}, f32[1024]{0:T(1024)}, u32[]{:S(2)}) copy-start(f32[1024]{0:T(1024)} %param.11) | copy-start | bytes 12292
  2.1 50.2 %collective-permute-start.3 = (f32[3,2,32,1024]{3,2,1,0:T(8,128)S(1)}, f32[3,2,32,1024]{3,2,1,0:T(8,128)S(1)}, u32[]{:S(2)}, u32[]{:S(2)}) collective-permute-start(f32[3,2,32,1024]{3,2,1,0:T(8,128)S(1)} %get-tuple-element.21), channel_id=1, source_target_pairs={{32,0},{64,32},{96,64},{0,96},{33,1},{65,33},{97,65},{1,97},{34,2}... | collective-permute-start | bytes 2359304 | tf_op jit(solution)/shard_map/ppermute | solution.py:599
  6.8 45.6 %collective-permute-start.2 = (f32[3,2,32,1024]{3,2,1,0:T(8,128)S(1)}, f32[3,2,32,1024]{3,2,1,0:T(8,128)S(1)}, u32[]{:S(2)}, u32[]{:S(2)}) collective-permute-start(f32[3,2,32,1024]{3,2,1,0:T(8,128)S(1)} %get-tuple-element.22), channel_id=1, source_target_pairs={{0,32},{32,64},{64,96},{96,0},{1,33},{33,65},{65,97},{97,1},{2,34}... | collective-permute-start | bytes 2359304 | tf_op jit(solution)/shard_map/ppermute | solution.py:598
  8.7 31.0 %all-to-all-start = ((f32[128,2,128]{2,1,0:T(2,128)}), f32[128,2,128]{2,1,0:T(2,128)S(1)}, u32[]{:S(2)}, u32[]{:S(2)}) async-start(f32[128,2,128]{2,1,0:T(2,128)} %pack.1), calls=%async_computation | async-start | bytes 262144 | tf_op jit(solution)/shard_map/all_to_all | solution.py:600
  20.0 32.3 %collective-permute-start.1 = (f32[3,4,2,1024]{3,2,1,0:T(2,128)S(1)}, f32[3,4,2,1024]{3,2,1,0:T(2,128)}, u32[]{:S(2)}, u32[]{:S(2)}) collective-permute-start(f32[3,4,2,1024]{3,2,1,0:T(2,128)S(1)} %get-tuple-element.23), channel_id=1, source_target_pairs={{1,0},{2,1},{3,2},{4,3},{5,4},{6,5},{7,6},{8,7},{9,8},{10,9},{11,1... | collective-permute-start | bytes 294920 | tf_op jit(solution)/shard_map/ppermute | solution.py:605
  23.0 29.3 %collective-permute-start = (f32[3,4,2,1024]{3,2,1,0:T(2,128)S(1)}, f32[3,4,2,1024]{3,2,1,0:T(2,128)}, u32[]{:S(2)}, u32[]{:S(2)}) collective-permute-start(f32[3,4,2,1024]{3,2,1,0:T(2,128)S(1)} %get-tuple-element.24), channel_id=1, source_target_pairs={{0,1},{1,2},{2,3},{3,4},{4,5},{5,6},{6,7},{7,8},{8,9},{9,10},{10,1... | collective-permute-start | bytes 294920 | tf_op jit(solution)/shard_map/ppermute | solution.py:604
  39.7 0.7 copy-start.3
  52.3 0.9 copy-start.1
  52.3 1.1 %copy-start.2 = (f32[3,2,32,1024]{3,2,1,0:T(8,128)}, f32[3,2,32,1024]{3,2,1,0:T(8,128)S(1)}, u32[]{:S(2)}) copy-start(f32[3,2,32,1024]{3,2,1,0:T(8,128)S(1)} %collective-permute-done.2.before_ref) | copy-start | bytes 2359300
  82.6 12.1 %all-to-all-start.2 = ((f32[32,4,384]{2,1,0:T(4,128)}), f32[32,4,384]{2,1,0:T(4,128)S(1)}, u32[]{:S(2)}, u32[]{:S(2)}) async-start(f32[32,4,384]{2,1,0:T(4,128)} %solve.1), calls=%async_computation.2 | async-start | bytes 393216 | tf_op jit(solution)/shard_map/all_to_all | solution.py:619
  94.7 0.7 copy-start

commit v2 on v1

v2 whole, which is shorter than its diff:
```python
import jax
import jax.numpy as jnp
from jax import lax
from jax.experimental import pallas as pl
from jax.experimental.pallas import tpu as pltpu
from jax.sharding import PartitionSpec as P

TIME_STEP = 0.2
SECTION_KEEP = -5.0 / 9.0
SECTION_GAIN = 15.0 / 16.0
MAIN = 2.5
NEAR = -4.0 / 3.0
FAR = 1.0 / 12.0
SLABS = 32
ROWS = 32
CX = 4
CZ = 1024
PLANES = CX * ROWS
SLOTS = 64
PEERS = 128
TOTAL = PEERS * SLOTS
CHUNK = 2048
HIGH = lax.Precision.HIGHEST
F32 = jnp.float32
BF16 = jnp.bfloat16


def params(mib=60):
    return pltpu.CompilerParams(vmem_limit_bytes=mib * 1024 * 1024)


VMEM = pl.BlockSpec(memory_space=pltpu.MemorySpace.VMEM)
SMEM = pl.BlockSpec(memory_space=pltpu.MemorySpace.SMEM)
ANY = pl.BlockSpec(memory_space=pl.ANY)


def shaped(*shape):
    return jax.ShapeDtypeStruct(shape, F32)


def mm(a, b):
    return tuple(
        tuple(a[i][0] * b[0][j] + a[i][1] * b[1][j] for j in range(2)) for i in range(2)
    )


def add(a, b, sign=1.0):
    return tuple(tuple(a[i][j] + sign * b[i][j] for j in range(2)) for i in range(2))


def neg(a):
    return tuple(tuple(-e for e in row) for row in a)


def each(a, fn):
    return tuple(tuple(fn(e) for e in row) for row in a)


def inverse_of_one_minus(a):
    p, q, r, s = 1.0 - a[0][0], -a[0][1], -a[1][0], 1.0 - a[1][1]
    scale = 1.0 / (p * s - q * r)
    return ((s * scale, -q * scale), (-r * scale, p * scale))


def ldl(main_of, zero):
    recip, low1, low2 = [], [], []
    for k in range(ROWS):
        main = main_of(k)
        if k == 0:
            low1.append(zero)
            low2.append(zero)
            recip.append(1.0 / main)
            continue
        edge = NEAR - FAR * low1[k - 1]
        one = edge * recip[k - 1]
        two = FAR * recip[k - 2] if k > 1 else zero
        low1.append(one)
        low2.append(two)
        recip.append(1.0 / (main - edge * one - FAR * two))
    return recip, low1, low2


def substitute(rows, recip, low1, low2):
    half = []
    for k in range(ROWS):
        value = rows[k]
        if k > 0:
            value = value - low1[k] * half[k - 1]
        if k > 1:
            value = value - low2[k] * half[k - 2]
        half.append(value)
    full = [None] * ROWS
    for k in reversed(range(ROWS)):
        value = half[k] * recip[k]
        if k < ROWS - 1:
            value = value - low1[k + 1] * full[k + 1]
        if k < ROWS - 2:
            value = value - low2[k + 2] * full[k + 2]
        full[k] = value
    return full


ENDS = (0, 1, ROWS - 2, ROWS - 1)


def own_kernel(place_ref, rate_ref, scale_ref, tip_ref, fix_ref, solve_ref, wide_ref):
    slab = place_ref[0]
    lane8 = lax.broadcasted_iota(jnp.int32, (8, 128), 1)
    row = rate_ref[pl.ds(slab // 4, 1), :]
    row = pltpu.roll(jnp.broadcast_to(row, (8, 128)), 128 - ROWS * (slab % 4), 1)
    inv_rate = 1.0 / column_of(row[0:1, 0:ROWS], ROWS)
    scale_ref[...] = SECTION_GAIN * inv_rate
    wide_ref[...] = inv_rate + MAIN
    recip, low1, low2 = ldl(
        lambda k: jnp.broadcast_to(wide_ref[k : k + 1, :], (8, 128)), jnp.zeros((8, 128), F32)
    )
    full = substitute([(lane8 == k).astype(F32) for k in range(ROWS)], recip, low1, low2)
    for k in range(ROWS):
        solve_ref[k : k + 1, :] = full[k][0:1]
    solve = solve_ref[...]
    cols = [jnp.broadcast_to(solve[:, n : n + 1], (ROWS, 128)) for n in ENDS]
    for n in range(4):
        tip_ref[n] = cols[n]
    has_low = jnp.where(slab > 0, 1.0, 0.0)
    has_high = jnp.where(slab < SLABS - 1, 1.0, 0.0)
    fix_ref[0] = FAR * cols[0] * has_low
    fix_ref[1] = (NEAR * cols[0] + FAR * cols[1]) * has_low
    fix_ref[2] = (FAR * cols[2] + NEAR * cols[3]) * has_high
    fix_ref[3] = FAR * cols[3] * has_high


def own_factors(place, rate):
    return pl.pallas_call(
        own_kernel,
        out_shape=(
            shaped(ROWS, 128),
            shaped(4, ROWS, 128),
            shaped(4, ROWS, 128),
            shaped(ROWS, 128),
        ),
        in_specs=[SMEM, VMEM],
        out_specs=(VMEM,) * 4,
        scratch_shapes=[pltpu.VMEM((ROWS, 128), F32)],
        name="own_factors",
    )(place, rate)


def green_kernel(rate_ref, green_ref, wide_ref, coef_ref):
    lane8 = lax.broadcasted_iota(jnp.int32, (8, 128), 1)
    sub8 = lax.broadcasted_iota(jnp.int32, (8, 128), 0)
    wide_ref[...] = 1.0 / rate_ref[...] + MAIN
    zero = jnp.zeros((8, 128), F32)
    recip, low1, low2 = ldl(lambda k: jnp.broadcast_to(wide_ref[k : k + 1, :], (8, 128)), zero)
    units = [(sub8 == ENDS.index(k)).astype(F32) if k in ENDS else zero for k in range(ROWS)]
    full = substitute(units, recip, low1, low2)

    def entry(k, i):
        return jnp.broadcast_to(full[k][i : i + 1, :], (8, 128))

    not_first = ((lane8 > 0) & (lane8 < SLABS)).astype(F32)
    not_last = (lane8 < SLABS - 1).astype(F32)

    def lower(k):
        s0, s1 = entry(k, 0), entry(k, 1)
        return (FAR * s0 * not_first, (NEAR * s0 + FAR * s1) * not_first)

    def upper(k):
        s2, s3 = entry(k, 2), entry(k, 3)
        return ((FAR * s2 + NEAR * s3) * not_last, FAR * s3 * not_last)

    low_a = (lower(ENDS[0]), lower(ENDS[1]))
    low_c = (lower(ENDS[2]), lower(ENDS[3]))
    up_b = (upper(ENDS[0]), upper(ENDS[1]))
    up_e = (upper(ENDS[2]), upper(ENDS[3]))
    a, b, c, e = low_a, up_b, low_c, up_e
    for hop in (1, 2, 4, 8, 16):
        ax, bx, cx, ex = (each(m, lambda v: pltpu.roll(v, hop, 1)) for m in (a, b, c, e))
        w = inverse_of_one_minus(mm(a, ex))
        wa_c = mm(w, mm(a, cx))
        wb = mm(w, b)
        cy_ex = mm(c, ex)
        new_e = add(e, mm(cy_ex, wb))
        new_c = neg(add(mm(c, cx), mm(cy_ex, wa_c)))
        new_a = add(ax, mm(bx, wa_c))
        new_b = neg(mm(bx, wb))
        joined = lane8 >= hop

        def pick(new, old):
            return tuple(
                tuple(jnp.where(joined, new[i][j], old[i][j]) for j in range(2)) for i in range(2)
            )

        a, b, c, e = pick(new_a, a), pick(new_b, b), pick(new_c, c), pick(new_e, e)
    q = e
    q_prev = each(q, lambda v: jnp.where(lane8 > 0, pltpu.roll(v, 1, 1), 0.0))
    z = inverse_of_one_minus(mm(low_a, q_prev))
    gain = mm(mm(low_c, q_prev), z)
    carry = add(low_c, mm(gain, low_a))
    z_low = mm(z, low_a)
    z_up = mm(z, up_b)
    for group, mats in enumerate(((carry, gain), (z, z_low), (z_up, q))):
        block = jnp.zeros((8, 128), F32)
        for n, m in enumerate(mats):
            for i in range(2):
                for j in range(2):
                    block = jnp.where(sub8 == 4 * n + 2 * i + j, m[i][j], block)
        for s in range(SLABS):
            coef_ref[s, 8 * group : 8 * group + 8, :] = jnp.broadcast_to(block[:, s : s + 1], (8, 128))

    def coef(s, n):
        def one(i, j):
            at = 4 * n + 2 * i + j
            return jnp.broadcast_to(coef_ref[s, at : at + 1, :], (8, 128))

        return tuple(tuple(one(i, j) for j in range(2)) for i in range(2))

    def at_lane(n):
        return lane8 == n

    forward = []
    prev = None
    for s in range(SLABS):
        m, g = coef(s, 0), coef(s, 1)
        now = []
        for i in range(2):
            value = jnp.where(at_lane(4 * s), g[i][0], 0.0)
            value = jnp.where(at_lane(4 * s + 1), g[i][1], value)
            value = jnp.where(at_lane(4 * s + 2 + i), 1.0, value)
            if prev is not None:
                value = value - m[i][0] * prev[0] - m[i][1] * prev[1]
            now.append(value)
        forward.append(now)
        prev = now
    for row in (0, 1, 4 * SLABS - 2, 4 * SLABS - 1):
        green_ref[row : row + 1, :] = jnp.zeros((1, 128), F32)
    after = None
    for s in reversed(range(SLABS)):
        zc, zl, zu, qc = coef(s, 2), coef(s, 3), coef(s, 4), coef(s, 5)
        now = []
        for i in range(2):
            value = jnp.where(at_lane(4 * s), zc[i][0], 0.0)
            value = jnp.where(at_lane(4 * s + 1), zc[i][1], value)
            if s > 0:
                value = value - zl[i][0] * forward[s - 1][0] - zl[i][1] * forward[s - 1][1]
            if after is not None:
                value = value - zu[i][0] * after[0] - zu[i][1] * after[1]
            now.append(value)
        if s < SLABS - 1:
            for i in range(2):
                high = forward[s][i] - qc[i][0] * after[0] - qc[i][1] * after[1]
                green_ref[4 * (s + 1) + i : 4 * (s + 1) + i + 1, :] = high[0:1]
        if s > 0:
            for i in range(2):
                green_ref[4 * (s - 1) + 2 + i : 4 * (s - 1) + 3 + i, :] = now[i][0:1]
        after = now


def green_operator(rate):
    return pl.pallas_call(
        green_kernel,
        out_shape=shaped(128, 128),
        in_specs=[VMEM],
        out_specs=VMEM,
        scratch_shapes=[pltpu.VMEM((ROWS, 128), F32), pltpu.VMEM((SLABS, 24, 128), F32)],
        name="green_operator",
    )(rate)


def pack_kernel(vel_ref, rate_ref, out_ref):
    left = lax.broadcasted_iota(jnp.int32, (1, 128), 1) < SLOTS
    for r in range(PEERS // 2):
        part = [vel_ref[i : i + 1, 128 * r : 128 * r + 128] for i in range(3)]
        part.append(rate_ref[0:1, 128 * r : 128 * r + 128])
        for n in range(2):
            one, two = part[2 * n], part[2 * n + 1]
            out_ref[2 * r, n : n + 1, :] = jnp.where(left, one, pltpu.roll(two, SLOTS, 1))
            out_ref[2 * r + 1, n : n + 1, :] = jnp.where(left, pltpu.roll(one, SLOTS, 1), two)


def packed(part_vel, part_rate):
    return pl.pallas_call(
        pack_kernel,
        out_shape=shaped(PEERS, 2, 128),
        in_specs=[VMEM, VMEM],
        out_specs=VMEM,
        name="pack",
    )(part_vel, part_rate)


def halves(cells):
    plane = cells >> 10
    span = cells & (CZ - 1)
    return plane, span >> 7, span & 127


def span_table(high, low):
    width = high.shape[1]
    inner = lax.broadcasted_iota(jnp.int32, (128, width), 0) == low
    inner = inner.astype(F32).astype(BF16)
    rows = []
    for t in range(8):
        flag = (high == t).astype(F32).astype(BF16)
        rows.append(inner * flag)
    return jnp.concatenate(rows, axis=0)


def column_of(row, length):
    wide = jnp.broadcast_to(row, (length, length))
    here = lax.broadcasted_iota(jnp.int32, (length, length), 0) == lax.broadcasted_iota(
        jnp.int32, (length, length), 1
    )
    return jnp.broadcast_to(
        jnp.sum(jnp.where(here, wide, 0.0), axis=1, keepdims=True), (length, 128)
    )


def main_kernel(
    vel_hbm, below_hbm, above_hbm, before_hbm, behind_hbm, section_hbm, moved_ref, count_ref,
    cell_ref, near_ref, far_ref, scale_ref, tip_ref, part_ref, out_hbm, tips_ref,
    pad_ref, before_ref, behind_ref, section_ref, new_ref, bf_ref, table_ref, got_ref, deposit_ref,
    coef_ref, sems,
):
    copies = [
        pltpu.make_async_copy(vel_hbm, pad_ref.at[:, :, 8 : 8 + ROWS, :], sems.at[0]),
        pltpu.make_async_copy(below_hbm, pad_ref.at[:, :, 6:8, :], sems.at[1]),
        pltpu.make_async_copy(above_hbm, pad_ref.at[:, :, 8 + ROWS : 10 + ROWS, :], sems.at[2]),
        pltpu.make_async_copy(before_hbm, before_ref, sems.at[3]),
        pltpu.make_async_copy(behind_hbm, behind_ref, sems.at[4]),
        pltpu.make_async_copy(section_hbm, section_ref, sems.at[5]),
    ]
    for copy in copies:
        copy.start()
    coef_ref[0] = column_of(near_ref[...], ROWS)
    coef_ref[1] = column_of(far_ref[...], ROWS)
    left = lax.broadcasted_iota(jnp.int32, (1, 128), 1) < SLOTS
    lane = lax.broadcasted_iota(jnp.int32, (1, 128), 1)
    for r in range(PEERS // 2):
        lanes = slice(128 * r, 128 * r + 128)
        for n in range(2):
            one = moved_ref[2 * r, n : n + 1, :]
            two = moved_ref[2 * r + 1, n : n + 1, :]
            got_ref[2 * n : 2 * n + 1, lanes] = jnp.where(left, one, pltpu.roll(two, SLOTS, 1))
            got_ref[2 * n + 1 : 2 * n + 2, lanes] = jnp.where(left, pltpu.roll(one, SLOTS, 1), two)
        limit = jnp.where(left, count_ref[0, 2 * r], count_ref[0, 2 * r + 1])
        got_ref[4:5, lanes] = ((lane & (SLOTS - 1)) < limit).astype(F32)
    copies[0].wait()
    for c in range(3):
        for x in range(CX):
            top = c * PLANES + x * ROWS
            bf_ref[top : top + ROWS, :] = pad_ref[c, x, 8 : 8 + ROWS, :].astype(BF16)

    for step in range(TOTAL // CHUNK):
        lanes = slice(step * CHUNK, (step + 1) * CHUNK)
        plane, high, low = halves(cell_ref[:, lanes])
        table_ref[...] = span_table(high, low)
        at = jnp.dot(bf_ref[...], table_ref[...], preferred_element_type=F32)
        mask = lax.broadcasted_iota(jnp.int32, (PLANES, CHUNK), 0) == plane
        mask_bf = mask.astype(F32).astype(BF16)
        live = got_ref[4:5, lanes] > 0.5
        rate = got_ref[3:4, lanes]
        spread = []
        for n in range(3):
            fluid = jnp.sum(
                jnp.where(mask, at[n * PLANES : (n + 1) * PLANES], 0.0), axis=0, keepdims=True
            )
            old = got_ref[n : n + 1, lanes]
            relative = fluid - old
            part_ref[n : n + 1, lanes] = jnp.where(live, old + TIME_STEP * rate * relative, 0.0)
            push = jnp.where(live, -rate * relative, 0.0).astype(BF16)
            spread.append(mask_bf * push)
        new = lax.dot_general(
            jnp.concatenate(spread, axis=0), table_ref[...], (((1,), (1,)), ((), ())),
            preferred_element_type=F32,
        )
        if step == 0:
            deposit_ref[...] = new
        else:
            deposit_ref[...] += new

    for copy in copies[1:]:
        copy.wait()

    def tiled(column):
        return jnp.concatenate([column] * 8, axis=1)

    def stored(c):
        return pltpu.make_async_copy(new_ref.at[c], out_hbm.at[c], sems.at[6 + c])

    for c in range(3):
        for x in range(CX):
            def layer(i, top):
                if i < 0:
                    return before_ref[c, 2 + i, top : top + 8, :]
                if i >= CX:
                    return behind_ref[c, i - CX, top : top + 8, :]
                return pad_ref[c, i, 8 + top : 16 + top, :]

            tips = [None] * 4
            for t in range(ROWS // 8):
                top = 8 * t
                here = layer(x, top)
                ddx = (8.0 / 12.0) * (layer(x + 1, top) - layer(x - 1, top)) - (1.0 / 12.0) * (
                    layer(x + 2, top) - layer(x - 2, top)
                )
                rolled = {k: pltpu.roll(here, (-k) % CZ, 1) for k in (1, -1, 2, -2)}
                ddz = (8.0 / 12.0) * (rolled[1] - rolled[-1]) - (1.0 / 12.0) * (
                    rolled[2] - rolled[-2]
                )

                def shifted(k):
                    return pad_ref[c, x, 8 + top + k : 16 + top + k, :]

                near = tiled(coef_ref[0, top : top + 8, :])
                far = tiled(coef_ref[1, top : top + 8, :])
                ddy = near * (shifted(1) - shifted(-1)) + far * (shifted(2) - shifted(-2))
                moved = (
                    pad_ref[0, x, 8 + top : 16 + top, :] * ddx
                    + pad_ref[1, x, 8 + top : 16 + top, :] * ddy
                    + pad_ref[2, x, 8 + top : 16 + top, :] * ddz
                )
                base = c * PLANES + x * ROWS + top
                rhs = deposit_ref[base : base + 8, :] - moved
                new = SECTION_KEEP * section_ref[c, x, top : top + 8, :] + TIME_STEP * rhs
                new_ref[c, x, top : top + 8, :] = new
                scaled = new * tiled(scale_ref[top : top + 8, :])
                for r in range(4):
                    weighted = scaled * tiled(tip_ref[r, top : top + 8, :])
                    tips[r] = weighted if t == 0 else tips[r] + weighted
            for r in range(4):
                total = jnp.sum(tips[r], axis=0, keepdims=True)
                for t in range(CZ // 128):
                    tips_ref[8 * x + t, c, r : r + 1, :] = total[:, 128 * t : 128 * t + 128]
        stored(c).start()
    for c in range(3):
        stored(c).wait()


def main_part(*operands):
    return pl.pallas_call(
        main_kernel,
        out_shape=(
            shaped(3, TOTAL),
            shaped(3, CX, ROWS, CZ),
            shaped(SLABS, 3, 4, 128),
        ),
        in_specs=[ANY] * 6 + [VMEM, SMEM] + [VMEM] * 5,
        out_specs=(VMEM, ANY, VMEM),
        scratch_shapes=[
            pltpu.VMEM((3, CX, ROWS + 16, CZ), F32),
            pltpu.VMEM((3, 2, ROWS, CZ), F32),
            pltpu.VMEM((3, 2, ROWS, CZ), F32),
            pltpu.VMEM((3, CX, ROWS, CZ), F32),
            pltpu.VMEM((3, CX, ROWS, CZ), F32),
            pltpu.VMEM((3 * PLANES, CZ), BF16),
            pltpu.VMEM((CZ, CHUNK), BF16),
            pltpu.VMEM((8, TOTAL), F32),
            pltpu.VMEM((3 * PLANES, CZ), F32),
            pltpu.VMEM((2, ROWS, 128), F32),
            pltpu.SemaphoreType.DMA((9,)),
        ],
        compiler_params=params(),
        name="main_part",
    )(*operands)


WIDTH = 3 * CX * CZ // SLABS


def solve_kernel(tips_ref, green_ref, out_ref, all_ref):
    for s in range(SLABS):
        for c in range(3):
            all_ref[4 * s : 4 * s + 4, 128 * c : 128 * c + 128] = tips_ref[s, c]
    found = jnp.dot(green_ref[...], all_ref[...], precision=HIGH, preferred_element_type=F32)
    for s in range(SLABS):
        for c in range(3):
            out_ref[s, c] = found[4 * s : 4 * s + 4, 128 * c : 128 * c + 128]


def solved(tips, green):
    return pl.pallas_call(
        solve_kernel,
        out_shape=shaped(SLABS, 3, 4, 128),
        in_specs=[VMEM, VMEM],
        out_specs=VMEM,
        scratch_shapes=[pltpu.VMEM((4 * SLABS, WIDTH), F32)],
        name="solve",
    )(tips, green)


def local_kernel(vel_ref, section_ref, scale_ref, solve_ref, out_ref):
    whole = solve_ref[:, 0:ROWS]
    head = whole.astype(BF16)
    rest = (whole - head.astype(F32)).astype(BF16)
    left = jnp.concatenate([head, rest, head], axis=1)
    scale = jnp.concatenate([scale_ref[...]] * 8, axis=1)
    for x in range(CX):
        value = section_ref[0, x] * scale
        high = value.astype(BF16)
        low = (value - high.astype(F32)).astype(BF16)
        right = jnp.concatenate([high, high, low], axis=0)
        out_ref[0, x] = vel_ref[0, x] + jnp.dot(left, right, preferred_element_type=F32)


BLOCK = pl.BlockSpec((1, CX, ROWS, CZ), lambda c: (c, 0, 0, 0))


def local_solve(velocity, section_new, scale, solve):
    return pl.pallas_call(
        local_kernel,
        grid=(3,),
        out_shape=shaped(3, CX, ROWS, CZ),
        in_specs=[BLOCK, BLOCK, VMEM, VMEM],
        out_specs=BLOCK,
        compiler_params=params(),
        name="local_solve",
    )(velocity, section_new, scale, solve)


def final_kernel(partial_ref, edge_ref, fix_ref, out_ref):
    c = pl.program_id(0)
    for x in range(CX):
        for t in range(CZ // 128):
            lanes = slice(128 * t, 128 * t + 128)
            edge = edge_ref[8 * x + t, c]
            value = partial_ref[0, x, :, lanes]
            for r in range(4):
                value = value - fix_ref[r] * edge[r : r + 1, :]
            out_ref[0, x, :, lanes] = value


def finished(partial, edges, fix):
    return pl.pallas_call(
        final_kernel,
        grid=(3,),
        out_shape=shaped(3, CX, ROWS, CZ),
        in_specs=[BLOCK, VMEM, VMEM],
        out_specs=BLOCK,
        compiler_params=params(),
        name="finish",
    )(partial, edges, fix)


def local(velocity, section, diffusion, rhs_near, rhs_far, part_vel, part_rate, counts, cell_slot):
    n_gx, n_gy = lax.axis_size("gx"), lax.axis_size("gy")
    up_x = [(i, (i + 1) % n_gx) for i in range(n_gx)]
    down_x = [(t, s) for s, t in up_x]
    up_y = [(i, i + 1) for i in range(n_gy - 1)]
    down_y = [(t, s) for s, t in up_y]
    before = lax.ppermute(velocity[:, CX - 2 :], "gx", up_x)
    behind = lax.ppermute(velocity[:, :2], "gx", down_x)
    moved = lax.all_to_all(
        packed(part_vel, part_rate.reshape(1, TOTAL)),
        ("gx", "gy"), split_axis=0, concat_axis=0, tiled=True,
    )
    below = lax.ppermute(velocity[:, :, ROWS - 2 :], "gy", up_y)
    above = lax.ppermute(velocity[:, :, :2], "gy", down_y)
    place = lax.axis_index("gy").astype(jnp.int32).reshape(1)
    scale, tip, fix, solve = own_factors(place, diffusion.reshape(8, 128))
    part_new, section_new, tips = main_part(
        velocity, below, above, before, behind, section, moved, counts, cell_slot,
        rhs_near.reshape(1, ROWS), rhs_far.reshape(1, ROWS), scale, tip,
    )
    tips, diffusion = lax.optimization_barrier((tips, diffusion))
    all_tips = lax.all_to_all(tips, "gy", split_axis=0, concat_axis=0, tiled=True)
    rate = jnp.pad(
        diffusion.reshape(SLABS, ROWS).T, ((0, 0), (0, 128 - SLABS)), constant_values=1000.0
    )
    reply = solved(all_tips, green_operator(rate))
    reply, section_done = lax.optimization_barrier((reply, section_new))
    edges = lax.all_to_all(reply, "gy", split_axis=0, concat_axis=0, tiled=True)
    velocity_new = finished(local_solve(velocity, section_done, scale, solve), edges, fix)
    return (velocity_new, section_new, part_new)


def solution(mesh):
    return jax.shard_map(
        local,
        mesh=mesh,
        in_specs=(
            P(None, "gx", "gy", None),
            P(None, "gx", "gy", None),
            P(),
            P("gy"),
            P("gy"),
            P(None, ("gx", "gy")),
            P(("gx", "gy")),
            P(("gx", "gy"), None),
            P(("gx", "gy"), None),
        ),
        out_specs=(P(None, "gx", "gy", None), P(None, "gx", "gy", None), P(None, ("gx", "gy"))),
        check_vma=False,
    )
```

time: 99.5 us -> 87.4 us (0.88)
  blocking collectives: 17.3 us -> 0 us
  Pallas kernels: 45.8 us -> 37.1 us
  starting transfers between devices: 24.2 us -> 32.8 us
  waiting for transfers between devices: 4.86 us -> 10.3 us
    all_to_all x1 -> x0, blocking collectives: 17.3 us -> none  [local(): lax.all_to_all(spread_tips(tips), 'gy', split_axis=0, concat_axis=0, tile...]
    pallas_call x8 -> x6, Pallas kernels: 43.9 us -> 35.2 us  [the longest x1 20.8 us: main_part(): pl.pallas_call(main_kernel, out_shape=(shaped(3, TOTAL), shaped(3, CX, RO...]
    all_to_all x1 -> x2, starting transfers between devices: 3.8 us -> 12.4 us  [the longest x1 8.6 us: local(): lax.all_to_all(tips, 'gy', split_axis=0, concat_axis=0, tiled=True)]
    all_to_all x1 -> x2, waiting for transfers between devices: 4.84 us -> 8.93 us  [the longest x1 4.92 us: local(): lax.all_to_all(tips, 'gy', split_axis=0, concat_axis=0, tiled=True)]
    all_to_all x1, waiting for transfers between devices: 0.01 us -> 1.31 us  [local(): lax.all_to_all(packed(part_vel, part_rate.reshape(1, TOTAL)), ('gx', 'gy'...]
    unnamed x10 -> x12, local copies, waits for them, and re-layouts: 2.48 us -> 2.53 us
  transfers between devices with their start and end apart: 6 -> 7, of which waited for: 1 -> 3; matrix products, arithmetic and copies ran while one was open for 2% -> 2% of each run, Pallas kernels for 31% -> 12%
where the time goes in v2:
time: 87.4 us; the launch traced here: 86.8 us
  Pallas kernels  37.1 us (42%)
  starting transfers between devices  32.8 us (38%)
  waiting for transfers between devices  10.3 us (12%)
  local copies, waits for them, and re-layouts  5.96 us (7%)
    pallas_call x1, Pallas kernels, main_part(): pl.pallas_call(main_kernel, out_shape=(shaped(3, TOTAL), shaped(3, CX, RO...  20.8 us
    all_to_all x1, starting transfers between devices, local(): lax.all_to_all(packed(part_vel, part_rate.reshape(1, TOTAL)), ('gx', 'gy'...  10.1 us
    all_to_all x1, starting transfers between devices, local(): lax.all_to_all(tips, 'gy', split_axis=0, concat_axis=0, tiled=True)  8.6 us
    all_to_all x1, waiting for transfers between devices, local(): lax.all_to_all(tips, 'gy', split_axis=0, concat_axis=0, tiled=True)  4.92 us
    ppermute x1, starting transfers between devices, local(): behind = lax.ppermute(velocity[:, :2], 'gx', down_x)  4.66 us
    pallas_call x1, Pallas kernels, local_solve(): pl.pallas_call(local_kernel, grid=(3,), out_shape=shaped(3, CX, ROWS, CZ)...  4.26 us
    all_to_all x1, waiting for transfers between devices, local(): edges = lax.all_to_all(reply, 'gy', split_axis=0, concat_axis=0, tiled=True)  4.01 us
    all_to_all x1, starting transfers between devices, local(): edges = lax.all_to_all(reply, 'gy', split_axis=0, concat_axis=0, tiled=True)  3.8 us
  transfers between devices with their start and end apart: 7, of which 3 were waited for; matrix products, arithmetic and copies ran while one was open for 2% of the time, Pallas kernels for 12%

profile of v2, /device:TPU:1, one launch (start us, length us, event | category | flops | bytes accessed | tf_op | source)
XLA Modules:
  0.0 86.8 jit_solution(4598399236708711401)
XLA Ops:
  0.6 1.5 %fusion = (f32[3,2,32,1024]{3,2,1,0:T(8,128)S(1)}, f32[3,2,32,1024]{3,2,1,0:T(8,128)S(1)}) fusion(f32[3,4,32,1024]{3,2,1,0:T(8,128)} %vel_ref.3), kind=kLoop, calls=%fused_computation | loop fusion | bytes 3145728 | tf_op jit(solution)/shard_map/slice | solution.py:550
  2.1 4.7 %collective-permute-start.3 = (f32[3,2,32,1024]{3,2,1,0:T(8,128)S(1)}, f32[3,2,32,1024]{3,2,1,0:T(8,128)S(1)}, u32[]{:S(2)}, u32[]{:S(2)}) collective-permute-start(f32[3,2,32,1024]{3,2,1,0:T(8,128)S(1)} %get-tuple-element.25), channel_id=1, source_target_pairs={{32,0},{64,32},{96,64},{0,96},{33,1},{65,33},{97,65},{1,97},{34,2}... | collective-permute-start | bytes 2359304 | tf_op jit(solution)/shard_map/ppermute | solution.py:550
  6.8 0.0 collective-permute-start.2
  6.8 1.9 %pack.1 = f32[128,2,128]{2,1,0:T(2,128)} custom-call(f32[3,8192]{1,0:T(4,128)} %vel_ref.2, f32[1,8192]{1,0:T(1,128)} %bitcast.7), custom_call_target="tpu_custom_call" | custom-call | tf_op jit(solution)/shard_map/pack/pallas_call | solution.py:281
  8.7 10.1 %all-to-all-start = ((f32[128,2,128]{2,1,0:T(2,128)}), f32[128,2,128]{2,1,0:T(2,128)S(1)}, u32[]{:S(2)}, u32[]{:S(2)}) async-start(f32[128,2,128]{2,1,0:T(2,128)} %pack.1), calls=%async_computation | async-start | bytes 262144 | tf_op jit(solution)/shard_map/all_to_all | solution.py:551
  18.8 1.2 %fusion.1 = (f32[3,4,2,1024]{3,2,1,0:T(2,128)S(1)}, f32[3,4,2,1024]{3,2,1,0:T(2,128)S(1)}) fusion(f32[3,4,32,1024]{3,2,1,0:T(8,128)} %vel_ref.3), kind=kLoop, calls=%fused_computation.1 | loop fusion | bytes 393216 | tf_op jit(solution)/shard_map/slice | solution.py:556
  20.0 3.0 %collective-permute-start.1 = (f32[3,4,2,1024]{3,2,1,0:T(2,128)S(1)}, f32[3,4,2,1024]{3,2,1,0:T(2,128)}, u32[]{:S(2)}, u32[]{:S(2)}) collective-permute-start(f32[3,4,2,1024]{3,2,1,0:T(2,128)S(1)} %get-tuple-element.27), channel_id=1, source_target_pairs={{1,0},{2,1},{3,2},{4,3},{5,4},{6,5},{7,6},{8,7},{9,8},{10,9},{11,1... | collective-permute-start | bytes 294920 | tf_op jit(solution)/shard_map/ppermute | solution.py:556
  23.0 2.6 %collective-permute-start = (f32[3,4,2,1024]{3,2,1,0:T(2,128)S(1)}, f32[3,4,2,1024]{3,2,1,0:T(2,128)}, u32[]{:S(2)}, u32[]{:S(2)}) collective-permute-start(f32[3,4,2,1024]{3,2,1,0:T(2,128)S(1)} %get-tuple-element.28), channel_id=1, source_target_pairs={{0,1},{1,2},{2,3},{3,4},{4,5},{5,6},{6,7},{7,8},{8,9},{9,10},{10,1... | collective-permute-start | bytes 294920 | tf_op jit(solution)/shard_map/ppermute | solution.py:555
  25.6 2.0 %own_factors.1 = (f32[32,128]{1,0:T(8,128)}, f32[4,32,128]{2,1,0:T(8,128)}, f32[4,32,128]{2,1,0:T(8,128)}, f32[32,128]{1,0:T(8,128)}) custom-call(s32[1]{0:T(128)} %bitcast.3.place_ref, f32[8,128]{1,0:T(8,128)} %bitcast.8), custom_call_target="tpu_custom_call" | custom-call | tf_op jit(solution)/shard_map/own_factors/pallas_call | solution.py:133
  27.6 0.0 collective-permute-done.1.above_hbm
  27.6 0.0 collective-permute-done.below_hbm
  27.6 1.3 %all-to-all-done.moved_ref = f32[128,2,128]{2,1,0:T(2,128)S(1)} async-done(((f32[128,2,128]{2,1,0:T(2,128)}), f32[128,2,128]{2,1,0:T(2,128)S(1)}, u32[]{:S(2)}, u32[]{:S(2)}) %all-to-all-start) | async-done | bytes 131104 | tf_op jit(solution)/shard_map/all_to_all | solution.py:551
  28.9 0.0 collective-permute-done.3.behind_hbm
  28.9 0.0 collective-permute-done.2.before_hbm
  28.9 0.0 copy-start.2
  29.0 0.6 copy-done.4
  29.6 0.3 copy-done.1
  29.9 0.2 copy-done.2
  30.1 20.8 %main_part.1 = (f32[3,8192]{1,0:T(4,128)}, f32[3,4,32,1024]{3,2,1,0:T(8,128)}, f32[32,3,4,128]{3,2,1,0:T(4,128)}) custom-call(f32[3,4,32,1024]{3,2,1,0:T(8,128)} %vel_ref.3, f32[3,4,2,1024]{3,2,1,0:T(2,128)} %collective-permute-done.below_hbm, f32[3,4,2,1024]{3,2,1,0:T(2,128)} %collective-permute-done.1.above_hbm, f32[3,2,32,1024]{3,2,1,0:T(8,128)} %copy-done.2, ...), custom_call_target="tpu_custom_call" | custom-call | tf_op jit(solution)/shard_map/main_part/pallas_call | solution.py:439
  50.9 8.6 %all-to-all-start.1 = ((f32[32,3,4,128]{3,2,1,0:T(4,128)}), f32[32,3,4,128]{3,2,1,0:T(4,128)S(1)}, u32[]{:S(2)}, u32[]{:S(2)}) async-start(f32[32,3,4,128]{3,2,1,0:T(4,128)} %get-tuple-element.17), calls=%async_computation.1 | async-start | bytes 393216 | tf_op jit(solution)/shard_map/all_to_all | solution.py:564
  59.5 0.1 reshape.29
  59.6 0.1 copy.12
  59.6 0.6 pad.4.rate_ref
  60.3 2.6 %green_operator.1.green_ref = f32[128,128]{1,0:T(8,128)} custom-call(f32[32,128]{1,0:T(8,128)} %pad.4.rate_ref), custom_call_target="tpu_custom_call" | custom-call | tf_op jit(solution)/shard_map/green_operator/pallas_call | solution.py:259
  62.8 4.9 %all-to-all-done.1.tips_ref = f32[32,3,4,128]{3,2,1,0:T(4,128)S(1)} async-done(((f32[32,3,4,128]{3,2,1,0:T(4,128)}), f32[32,3,4,128]{3,2,1,0:T(4,128)S(1)}, u32[]{:S(2)}, u32[]{:S(2)}) %all-to-all-start.1) | async-done | bytes 196640 | tf_op jit(solution)/shard_map/all_to_all | solution.py:564
  67.7 0.7 copy-done
  68.4 2.0 %solve.1 = f32[32,3,4,128]{3,2,1,0:T(4,128)} custom-call(f32[32,3,4,128]{3,2,1,0:T(4,128)} %copy-done, f32[128,128]{1,0:T(8,128)} %green_operator.1.green_ref), custom_call_target="tpu_custom_call" | custom-call | tf_op jit(solution)/shard_map/solve/pallas_call | solution.py:480
  70.4 3.8 %all-to-all-start.2 = ((f32[32,3,4,128]{3,2,1,0:T(4,128)}), f32[32,3,4,128]{3,2,1,0:T(4,128)S(1)}, u32[]{:S(2)}, u32[]{:S(2)}) async-start(f32[32,3,4,128]{3,2,1,0:T(4,128)} %solve.1), calls=%async_computation.2 | async-start | bytes 393216 | tf_op jit(solution)/shard_map/all_to_all | solution.py:570
  74.2 4.3 %local_solve.1.partial_ref = f32[3,4,32,1024]{3,2,1,0:T(8,128)} custom-call(f32[3,4,32,1024]{3,2,1,0:T(8,128)} %vel_ref.3, f32[3,4,32,1024]{3,2,1,0:T(8,128)} %get-tuple-element.20.section_ref, f32[32,128]{1,0:T(8,128)} %get-tuple-element.14.scale_ref, f32[32,128]{1,0:T(8,128)} %get-tuple-element.21.solve_ref), custom_call_target="tpu_custom_call" | custom-call | tf_op jit(solution)/shard_map/local_solve/pallas_call | solution.py:508
  78.5 4.0 %all-to-all-done.2.edge_ref = f32[32,3,4,128]{3,2,1,0:T(4,128)S(1)} async-done(((f32[32,3,4,128]{3,2,1,0:T(4,128)}), f32[32,3,4,128]{3,2,1,0:T(4,128)S(1)}, u32[]{:S(2)}, u32[]{:S(2)}) %all-to-all-start.2) | async-done | bytes 196640 | tf_op jit(solution)/shard_map/all_to_all | solution.py:570
  82.5 0.7 copy-done.3
  83.2 3.6 %finish.1 = f32[3,4,32,1024]{3,2,1,0:T(8,128)} custom-call(f32[3,4,32,1024]{3,2,1,0:T(8,128)} %local_solve.1.partial_ref, f32[32,3,4,128]{3,2,1,0:T(4,128)} %copy-done.3, f32[4,32,128]{2,1,0:T(8,128)} %get-tuple-element.23.fix_ref), custom_call_target="tpu_custom_call" | custom-call | tf_op jit(solution)/shard_map/finish/pallas_call | solution.py:532
  (6 shorter events, 0.0 us)
Async XLA Ops:
  2.1 26.8 %collective-permute-start.3 = (f32[3,2,32,1024]{3,2,1,0:T(8,128)S(1)}, f32[3,2,32,1024]{3,2,1,0:T(8,128)S(1)}, u32[]{:S(2)}, u32[]{:S(2)}) collective-permute-start(f32[3,2,32,1024]{3,2,1,0:T(8,128)S(1)} %get-tuple-element.25), channel_id=1, source_target_pairs={{32,0},{64,32},{96,64},{0,96},{33,1},{65,33},{97,65},{1,97},{34,2}... | collective-permute-start | bytes 2359304 | tf_op jit(solution)/shard_map/ppermute | solution.py:550
  6.8 22.2 %collective-permute-start.2 = (f32[3,2,32,1024]{3,2,1,0:T(8,128)S(1)}, f32[3,2,32,1024]{3,2,1,0:T(8,128)S(1)}, u32[]{:S(2)}, u32[]{:S(2)}) collective-permute-start(f32[3,2,32,1024]{3,2,1,0:T(8,128)S(1)} %get-tuple-element.26), channel_id=1, source_target_pairs={{0,32},{32,64},{64,96},{96,0},{1,33},{33,65},{65,97},{97,1},{2,34}... | collective-permute-start | bytes 2359304 | tf_op jit(solution)/shard_map/ppermute | solution.py:549
  8.7 20.3 %all-to-all-start = ((f32[128,2,128]{2,1,0:T(2,128)}), f32[128,2,128]{2,1,0:T(2,128)S(1)}, u32[]{:S(2)}, u32[]{:S(2)}) async-start(f32[128,2,128]{2,1,0:T(2,128)} %pack.1), calls=%async_computation | async-start | bytes 262144 | tf_op jit(solution)/shard_map/all_to_all | solution.py:551
  20.0 7.6 %collective-permute-start.1 = (f32[3,4,2,1024]{3,2,1,0:T(2,128)S(1)}, f32[3,4,2,1024]{3,2,1,0:T(2,128)}, u32[]{:S(2)}, u32[]{:S(2)}) collective-permute-start(f32[3,4,2,1024]{3,2,1,0:T(2,128)S(1)} %get-tuple-element.27), channel_id=1, source_target_pairs={{1,0},{2,1},{3,2},{4,3},{5,4},{6,5},{7,6},{8,7},{9,8},{10,9},{11,1... | collective-permute-start | bytes 294920 | tf_op jit(solution)/shard_map/ppermute | solution.py:556
  23.0 4.6 %collective-permute-start = (f32[3,4,2,1024]{3,2,1,0:T(2,128)S(1)}, f32[3,4,2,1024]{3,2,1,0:T(2,128)}, u32[]{:S(2)}, u32[]{:S(2)}) collective-permute-start(f32[3,4,2,1024]{3,2,1,0:T(2,128)S(1)} %get-tuple-element.28), channel_id=1, source_target_pairs={{0,1},{1,2},{2,3},{3,4},{4,5},{5,6},{6,7},{7,8},{8,9},{9,10},{10,1... | collective-permute-start | bytes 294920 | tf_op jit(solution)/shard_map/ppermute | solution.py:555
  28.9 0.6 copy-start.4
  28.9 0.9 %copy-start.1 = (f32[3,2,32,1024]{3,2,1,0:T(8,128)}, f32[3,2,32,1024]{3,2,1,0:T(8,128)S(1)}, u32[]{:S(2)}) copy-start(f32[3,2,32,1024]{3,2,1,0:T(8,128)S(1)} %collective-permute-done.3.behind_hbm) | copy-start | bytes 2359300
  28.9 1.2 %copy-start.2 = (f32[3,2,32,1024]{3,2,1,0:T(8,128)}, f32[3,2,32,1024]{3,2,1,0:T(8,128)S(1)}, u32[]{:S(2)}) copy-start(f32[3,2,32,1024]{3,2,1,0:T(8,128)S(1)} %collective-permute-done.2.before_hbm) | copy-start | bytes 2359300
  30.1 29.4 %copy-start.5 = (f32[1024]{0:T(1024)S(1)}, f32[1024]{0:T(1024)}, u32[]{:S(2)}) copy-start(f32[1024]{0:T(1024)} %param.11) | copy-start | bytes 12292
  50.9 16.9 %all-to-all-start.1 = ((f32[32,3,4,128]{3,2,1,0:T(4,128)}), f32[32,3,4,128]{3,2,1,0:T(4,128)S(1)}, u32[]{:S(2)}, u32[]{:S(2)}) async-start(f32[32,3,4,128]{3,2,1,0:T(4,128)} %get-tuple-element.17), calls=%async_computation.1 | async-start | bytes 393216 | tf_op jit(solution)/shard_map/all_to_all | solution.py:564
  67.7 0.7 copy-start
  70.4 12.1 %all-to-all-start.2 = ((f32[32,3,4,128]{3,2,1,0:T(4,128)}), f32[32,3,4,128]{3,2,1,0:T(4,128)S(1)}, u32[]{:S(2)}, u32[]{:S(2)}) async-start(f32[32,3,4,128]{3,2,1,0:T(4,128)} %solve.1), calls=%async_computation.2 | async-start | bytes 393216 | tf_op jit(solution)/shard_map/all_to_all | solution.py:570
  82.5 0.7 copy-start.3

commit v3 on v2

--- a/solution.py
+++ b/solution.py
@@ -31,11 +31,23 @@
 
 VMEM = pl.BlockSpec(memory_space=pltpu.MemorySpace.VMEM)
 SMEM = pl.BlockSpec(memory_space=pltpu.MemorySpace.SMEM)
-ANY = pl.BlockSpec(memory_space=pl.ANY)
+ANY = pl.BlockSpec(memory_space=pltpu.MemorySpace.HBM)
+
+
+def held(shape, dtype=F32):
+    return pltpu.MemorySpace.VMEM(shape, dtype)
 
 
 def shaped(*shape):
     return jax.ShapeDtypeStruct(shape, F32)
+
+
+def far_out(*shape):
+    return pltpu.MemorySpace.HBM(shape, F32)
+
+
+def far_in(*arrays):
+    return [pltpu.with_memory_space_constraint(a, pltpu.MemorySpace.HBM) for a in arrays]
 
 
 def mm(a, b):
@@ -103,8 +115,7 @@
 ENDS = (0, 1, ROWS - 2, ROWS - 1)
 
 
-def own_kernel(place_ref, rate_ref, scale_ref, tip_ref, fix_ref, solve_ref, wide_ref):
-    slab = place_ref[0]
+def own_factors(slab, rate_ref, scale_ref, tip_ref, fix_ref, solve_ref, wide_ref):
     lane8 = lax.broadcasted_iota(jnp.int32, (8, 128), 1)
     row = rate_ref[pl.ds(slab // 4, 1), :]
     row = pltpu.roll(jnp.broadcast_to(row, (8, 128)), 128 - ROWS * (slab % 4), 1)
@@ -127,22 +138,6 @@
     fix_ref[1] = (NEAR * cols[0] + FAR * cols[1]) * has_low
     fix_ref[2] = (FAR * cols[2] + NEAR * cols[3]) * has_high
     fix_ref[3] = FAR * cols[3] * has_high
-
-
-def own_factors(place, rate):
-    return pl.pallas_call(
-        own_kernel,
-        out_shape=(
-            shaped(ROWS, 128),
-            shaped(4, ROWS, 128),
-            shaped(4, ROWS, 128),
-            shaped(ROWS, 128),
-        ),
-        in_specs=[SMEM, VMEM],
-        out_specs=(VMEM,) * 4,
-        scratch_shapes=[pltpu.VMEM((ROWS, 128), F32)],
-        name="own_factors",
-    )(place, rate)
 
 
 def green_kernel(rate_ref, green_ref, wide_ref, coef_ref):
@@ -262,29 +257,73 @@
         in_specs=[VMEM],
         out_specs=VMEM,
         scratch_shapes=[pltpu.VMEM((ROWS, 128), F32), pltpu.VMEM((SLABS, 24, 128), F32)],
+        compiler_params=params(4),
         name="green_operator",
     )(rate)
 
 
-def pack_kernel(vel_ref, rate_ref, out_ref):
+def pre_kernel(
+    vel_hbm, part_hbm, rate_hbm, high_hbm, low_hbm, below_hbm, above_hbm, packed_hbm, vel_ref,
+    part_ref, rate_ref, out_ref, sems,
+):
+    into = [
+        pltpu.make_async_copy(vel_hbm.at[:, 2:4], vel_ref.at[:, 2:4], sems.at[0]),
+        pltpu.make_async_copy(vel_hbm.at[:, 0:2], vel_ref.at[:, 0:2], sems.at[1]),
+        pltpu.make_async_copy(part_hbm, part_ref, sems.at[2]),
+        pltpu.make_async_copy(rate_hbm, rate_ref, sems.at[3]),
+    ]
+    for copy in into:
+        copy.start()
+    out = [
+        pltpu.make_async_copy(vel_ref.at[:, 2:4], high_hbm, sems.at[4]),
+        pltpu.make_async_copy(vel_ref.at[:, 0:2], low_hbm, sems.at[5]),
+        pltpu.make_async_copy(vel_ref.at[:, :, ROWS - 2 : ROWS], below_hbm, sems.at[6]),
+        pltpu.make_async_copy(vel_ref.at[:, :, 0:2], above_hbm, sems.at[7]),
+        pltpu.make_async_copy(out_ref, packed_hbm, sems.at[8]),
+    ]
+    into[2].wait()
+    into[3].wait()
     left = lax.broadcasted_iota(jnp.int32, (1, 128), 1) < SLOTS
     for r in range(PEERS // 2):
-        part = [vel_ref[i : i + 1, 128 * r : 128 * r + 128] for i in range(3)]
+        part = [part_ref[i : i + 1, 128 * r : 128 * r + 128] for i in range(3)]
         part.append(rate_ref[0:1, 128 * r : 128 * r + 128])
         for n in range(2):
             one, two = part[2 * n], part[2 * n + 1]
             out_ref[2 * r, n : n + 1, :] = jnp.where(left, one, pltpu.roll(two, SLOTS, 1))
             out_ref[2 * r + 1, n : n + 1, :] = jnp.where(left, pltpu.roll(one, SLOTS, 1), two)
-
-
-def packed(part_vel, part_rate):
+    out[4].start()
+    into[0].wait()
+    out[0].start()
+    into[1].wait()
+    out[1].start()
+    out[2].start()
+    out[3].start()
+    for copy in out:
+        copy.wait()
+
+
+def prepared(velocity, part_vel, part_rate):
     return pl.pallas_call(
-        pack_kernel,
-        out_shape=shaped(PEERS, 2, 128),
-        in_specs=[VMEM, VMEM],
-        out_specs=VMEM,
-        name="pack",
-    )(part_vel, part_rate)
+        pre_kernel,
+        out_shape=(
+            far_out(3, 2, ROWS, CZ),
+            far_out(3, 2, ROWS, CZ),
+            far_out(3, CX, 2, CZ),
+            far_out(3, CX, 2, CZ),
+            far_out(PEERS, 2, 128),
+            held((3, CX, ROWS, CZ)),
+        ),
+        in_specs=[ANY] * 3,
+        out_specs=(ANY,) * 5 + (VMEM,),
+        scratch_shapes=[
+            pltpu.VMEM((3, TOTAL), F32),
+            pltpu.VMEM((1, TOTAL), F32),
+            pltpu.VMEM((PEERS, 2, 128), F32),
+            pltpu.SemaphoreType.DMA((9,)),
+        ],
+        compiler_params=params(16),
+        name="prepare",
+    )(*far_in(velocity, part_vel, part_rate))
 
 
 def halves(cells):
@@ -314,153 +353,251 @@
     )
 
 
-def main_kernel(
-    vel_hbm, below_hbm, above_hbm, before_hbm, behind_hbm, section_hbm, moved_ref, count_ref,
-    cell_ref, near_ref, far_ref, scale_ref, tip_ref, part_ref, out_hbm, tips_ref,
-    pad_ref, before_ref, behind_ref, section_ref, new_ref, bf_ref, table_ref, got_ref, deposit_ref,
-    coef_ref, sems,
+def find_kernel(
+    place_ref, vel_ref, cell_hbm, rate_hbm, fluid_ref, scale_ref, tip_ref, fix_ref, solve_ref,
+    bf_ref, table_ref, cell_ref, rate_ref, wide_ref, sems,
 ):
     copies = [
-        pltpu.make_async_copy(vel_hbm, pad_ref.at[:, :, 8 : 8 + ROWS, :], sems.at[0]),
-        pltpu.make_async_copy(below_hbm, pad_ref.at[:, :, 6:8, :], sems.at[1]),
-        pltpu.make_async_copy(above_hbm, pad_ref.at[:, :, 8 + ROWS : 10 + ROWS, :], sems.at[2]),
-        pltpu.make_async_copy(before_hbm, before_ref, sems.at[3]),
-        pltpu.make_async_copy(behind_hbm, behind_ref, sems.at[4]),
-        pltpu.make_async_copy(section_hbm, section_ref, sems.at[5]),
+        pltpu.make_async_copy(cell_hbm, cell_ref, sems.at[0]),
+        pltpu.make_async_copy(rate_hbm, rate_ref, sems.at[1]),
     ]
     for copy in copies:
         copy.start()
-    coef_ref[0] = column_of(near_ref[...], ROWS)
-    coef_ref[1] = column_of(far_ref[...], ROWS)
-    left = lax.broadcasted_iota(jnp.int32, (1, 128), 1) < SLOTS
-    lane = lax.broadcasted_iota(jnp.int32, (1, 128), 1)
-    for r in range(PEERS // 2):
-        lanes = slice(128 * r, 128 * r + 128)
-        for n in range(2):
-            one = moved_ref[2 * r, n : n + 1, :]
-            two = moved_ref[2 * r + 1, n : n + 1, :]
-            got_ref[2 * n : 2 * n + 1, lanes] = jnp.where(left, one, pltpu.roll(two, SLOTS, 1))
-            got_ref[2 * n + 1 : 2 * n + 2, lanes] = jnp.where(left, pltpu.roll(one, SLOTS, 1), two)
-        limit = jnp.where(left, count_ref[0, 2 * r], count_ref[0, 2 * r + 1])
-        got_ref[4:5, lanes] = ((lane & (SLOTS - 1)) < limit).astype(F32)
-    copies[0].wait()
     for c in range(3):
         for x in range(CX):
             top = c * PLANES + x * ROWS
-            bf_ref[top : top + ROWS, :] = pad_ref[c, x, 8 : 8 + ROWS, :].astype(BF16)
-
+            bf_ref[top : top + ROWS, :] = vel_ref[c, x].astype(BF16)
+    for copy in copies:
+        copy.wait()
+    own_factors(place_ref[0], rate_ref, scale_ref, tip_ref, fix_ref, solve_ref, wide_ref)
     for step in range(TOTAL // CHUNK):
         lanes = slice(step * CHUNK, (step + 1) * CHUNK)
         plane, high, low = halves(cell_ref[:, lanes])
         table_ref[...] = span_table(high, low)
         at = jnp.dot(bf_ref[...], table_ref[...], preferred_element_type=F32)
         mask = lax.broadcasted_iota(jnp.int32, (PLANES, CHUNK), 0) == plane
-        mask_bf = mask.astype(F32).astype(BF16)
+        for n in range(3):
+            fluid_ref[n : n + 1, lanes] = jnp.sum(
+                jnp.where(mask, at[n * PLANES : (n + 1) * PLANES], 0.0), axis=0, keepdims=True
+            )
+
+
+def find(place, vel_held, cells, rate):
+    return pl.pallas_call(
+        find_kernel,
+        out_shape=(
+            far_out(3, TOTAL),
+            far_out(ROWS, 128),
+            far_out(4, ROWS, 128),
+            far_out(4, ROWS, 128),
+            far_out(ROWS, 128),
+        ),
+        in_specs=[SMEM, VMEM, ANY, ANY],
+        out_specs=(VMEM,) * 5,
+        scratch_shapes=[
+            pltpu.VMEM((3 * PLANES, CZ), BF16),
+            pltpu.VMEM((CZ, CHUNK), BF16),
+            pltpu.VMEM((1, TOTAL), jnp.int32),
+            pltpu.VMEM((8, 128), F32),
+            pltpu.VMEM((ROWS, 128), F32),
+            pltpu.SemaphoreType.DMA((2,)),
+        ],
+        compiler_params=params(28),
+        name="find",
+    )(place, vel_held, *far_in(cells, rate))
+
+
+def main_kernel(
+    below_hbm, above_hbm, before_hbm, behind_hbm, moved_hbm,
+    fluid_hbm, scale_hbm, tip_hbm, vel_hbm, section_hbm, count_hbm, cell_hbm, near_hbm, far_hbm,
+    part_hbm, tips_hbm, new_ref,
+    pad_ref, before_ref, behind_ref, section_ref, table_ref, got_ref, deposit_ref, moved_ref,
+    count_ref, cell_ref, near_ref, far_ref, part_ref, tips_ref, coef_ref,
+    fluid_ref, scale_ref, tip_ref, sems,
+):
+    sources = [
+        (cell_hbm, cell_ref),
+        (moved_hbm, moved_ref),
+        (count_hbm, count_ref),
+        (fluid_hbm, fluid_ref),
+        (scale_hbm, scale_ref),
+        (tip_hbm, tip_ref),
+        (near_hbm, near_ref),
+        (far_hbm, far_ref),
+        (vel_hbm, pad_ref.at[:, :, 8 : 8 + ROWS, :]),
+        (below_hbm, pad_ref.at[:, :, 6:8, :]),
+        (above_hbm, pad_ref.at[:, :, 8 + ROWS : 10 + ROWS, :]),
+        (before_hbm, before_ref),
+        (behind_hbm, behind_ref),
+        (section_hbm, section_ref),
+    ]
+    copies = [pltpu.make_async_copy(a, b, sems.at[n]) for n, (a, b) in enumerate(sources)]
+    for copy in copies:
+        copy.start()
+    steps = TOTAL // CHUNK
+
+    def lanes_of(step):
+        return slice(step * CHUNK, (step + 1) * CHUNK)
+
+    def spread_of(step):
+        lanes = lanes_of(step)
+        plane, high, low = halves(cell_ref[:, lanes])
+        table_ref[...] = span_table(high, low)
+        mask = lax.broadcasted_iota(jnp.int32, (PLANES, CHUNK), 0) == plane
+        mask = mask.astype(F32).astype(BF16)
         live = got_ref[4:5, lanes] > 0.5
         rate = got_ref[3:4, lanes]
         spread = []
         for n in range(3):
-            fluid = jnp.sum(
-                jnp.where(mask, at[n * PLANES : (n + 1) * PLANES], 0.0), axis=0, keepdims=True
-            )
             old = got_ref[n : n + 1, lanes]
-            relative = fluid - old
+            relative = fluid_ref[n : n + 1, lanes] - old
             part_ref[n : n + 1, lanes] = jnp.where(live, old + TIME_STEP * rate * relative, 0.0)
             push = jnp.where(live, -rate * relative, 0.0).astype(BF16)
-            spread.append(mask_bf * push)
-        new = lax.dot_general(
-            jnp.concatenate(spread, axis=0), table_ref[...], (((1,), (1,)), ((), ())),
-            preferred_element_type=F32,
-        )
+            spread.append(mask * push)
+        return jnp.concatenate(spread, axis=0)
+
+    def unpack():
+        left = lax.broadcasted_iota(jnp.int32, (1, 128), 1) < SLOTS
+        lane = lax.broadcasted_iota(jnp.int32, (1, 128), 1)
+        for r in range(PEERS // 2):
+            lanes = slice(128 * r, 128 * r + 128)
+            for n in range(2):
+                one = moved_ref[2 * r, n : n + 1, :]
+                two = moved_ref[2 * r + 1, n : n + 1, :]
+                got_ref[2 * n : 2 * n + 1, lanes] = jnp.where(left, one, pltpu.roll(two, SLOTS, 1))
+                got_ref[2 * n + 1 : 2 * n + 2, lanes] = jnp.where(
+                    left, pltpu.roll(one, SLOTS, 1), two
+                )
+            limit = jnp.where(left, count_ref[0, 2 * r], count_ref[0, 2 * r + 1])
+            got_ref[4:5, lanes] = ((lane & (SLOTS - 1)) < limit).astype(F32)
+
+    def tiled(column, times):
+        return jnp.concatenate([column] * times, axis=1)
+
+    def stencil(c, x):
+        def layer(i, top):
+            if i < 0:
+                return before_ref[c, 2 + i, top : top + 8, :]
+            if i >= CX:
+                return behind_ref[c, i - CX, top : top + 8, :]
+            return pad_ref[c, i, 8 + top : 16 + top, :]
+
+        for t in range(ROWS // 8):
+            top = 8 * t
+            here = layer(x, top)
+            ddx = (8.0 / 12.0) * (layer(x + 1, top) - layer(x - 1, top)) - (1.0 / 12.0) * (
+                layer(x + 2, top) - layer(x - 2, top)
+            )
+            rolled = {k: pltpu.roll(here, (-k) % CZ, 1) for k in (1, -1, 2, -2)}
+            ddz = (8.0 / 12.0) * (rolled[1] - rolled[-1]) - (1.0 / 12.0) * (rolled[2] - rolled[-2])
+
+            def shifted(k):
+                return pad_ref[c, x, 8 + top + k : 16 + top + k, :]
+
+            near = tiled(coef_ref[0, top : top + 8, :], 8)
+            far = tiled(coef_ref[1, top : top + 8, :], 8)
+            ddy = near * (shifted(1) - shifted(-1)) + far * (shifted(2) - shifted(-2))
+            moved = (
+                pad_ref[0, x, 8 + top : 16 + top, :] * ddx
+                + pad_ref[1, x, 8 + top : 16 + top, :] * ddy
+                + pad_ref[2, x, 8 + top : 16 + top, :] * ddz
+            )
+            new_ref[c, x, top : top + 8, :] = (
+                SECTION_KEEP * section_ref[c, x, top : top + 8, :] - TIME_STEP * moved
+            )
+
+    planes = [(c, x) for c in range(3) for x in range(CX)]
+    share = len(planes) // (steps - 1)
+    for copy in copies[:4]:
+        copy.wait()
+    unpack()
+    for step in range(steps):
+        spread = spread_of(step)
+        if step > 0:
+            for c, x in planes[share * (step - 1) : share * step]:
+                stencil(c, x)
+        last = step == steps - 1
+        wide = CZ // 4 if last else CZ
+        for z in range(0, CZ, wide):
+            new = lax.dot_general(
+                spread, table_ref[z : z + wide, :], (((1,), (1,)), ((), ())),
+                preferred_element_type=F32,
+            )
+            if step == 0:
+                deposit_ref[...] = new
+                continue
+            if not last:
+                deposit_ref[...] += new
+                continue
+            for c, x in planes:
+                base = c * PLANES + x * ROWS
+                total = [None] * 4
+                for t in range(ROWS // 8):
+                    top = 8 * t
+                    full = new_ref[c, x, top : top + 8, z : z + wide] + TIME_STEP * (
+                        deposit_ref[base + top : base + top + 8, z : z + wide]
+                        + new[base + top : base + top + 8]
+                    )
+                    new_ref[c, x, top : top + 8, z : z + wide] = full
+                    scaled = full * tiled(scale_ref[top : top + 8, :], wide // 128)
+                    for r in range(4):
+                        weighted = scaled * tiled(tip_ref[r, top : top + 8, :], wide // 128)
+                        total[r] = weighted if t == 0 else total[r] + weighted
+                for r in range(4):
+                    summed = jnp.sum(total[r], axis=0, keepdims=True)
+                    for k in range(wide // 128):
+                        tips_ref[8 * x + z // 128 + k, c, r : r + 1, :] = summed[
+                            :, 128 * k : 128 * k + 128
+                        ]
         if step == 0:
-            deposit_ref[...] = new
-        else:
-            deposit_ref[...] += new
-
-    for copy in copies[1:]:
+            for copy in copies[4:]:
+                copy.wait()
+            coef_ref[0] = column_of(near_ref[...], ROWS)
+            coef_ref[1] = column_of(far_ref[...], ROWS)
+    stores = [
+        pltpu.make_async_copy(tips_ref, tips_hbm, sems.at[14]),
+        pltpu.make_async_copy(part_ref, part_hbm, sems.at[15]),
+    ]
+    for copy in stores:
+        copy.start()
+    for copy in stores:
         copy.wait()
 
-    def tiled(column):
-        return jnp.concatenate([column] * 8, axis=1)
-
-    def stored(c):
-        return pltpu.make_async_copy(new_ref.at[c], out_hbm.at[c], sems.at[6 + c])
-
-    for c in range(3):
-        for x in range(CX):
-            def layer(i, top):
-                if i < 0:
-                    return before_ref[c, 2 + i, top : top + 8, :]
-                if i >= CX:
-                    return behind_ref[c, i - CX, top : top + 8, :]
-                return pad_ref[c, i, 8 + top : 16 + top, :]
-
-            tips = [None] * 4
-            for t in range(ROWS // 8):
-                top = 8 * t
-                here = layer(x, top)
-                ddx = (8.0 / 12.0) * (layer(x + 1, top) - layer(x - 1, top)) - (1.0 / 12.0) * (
-                    layer(x + 2, top) - layer(x - 2, top)
-                )
-                rolled = {k: pltpu.roll(here, (-k) % CZ, 1) for k in (1, -1, 2, -2)}
-                ddz = (8.0 / 12.0) * (rolled[1] - rolled[-1]) - (1.0 / 12.0) * (
-                    rolled[2] - rolled[-2]
-                )
-
-                def shifted(k):
-                    return pad_ref[c, x, 8 + top + k : 16 + top + k, :]
-
-                near = tiled(coef_ref[0, top : top + 8, :])
-                far = tiled(coef_ref[1, top : top + 8, :])
-                ddy = near * (shifted(1) - shifted(-1)) + far * (shifted(2) - shifted(-2))
-                moved = (
-                    pad_ref[0, x, 8 + top : 16 + top, :] * ddx
-                    + pad_ref[1, x, 8 + top : 16 + top, :] * ddy
-                    + pad_ref[2, x, 8 + top : 16 + top, :] * ddz
-                )
-                base = c * PLANES + x * ROWS + top
-                rhs = deposit_ref[base : base + 8, :] - moved
-                new = SECTION_KEEP * section_ref[c, x, top : top + 8, :] + TIME_STEP * rhs
-                new_ref[c, x, top : top + 8, :] = new
-                scaled = new * tiled(scale_ref[top : top + 8, :])
-                for r in range(4):
-                    weighted = scaled * tiled(tip_ref[r, top : top + 8, :])
-                    tips[r] = weighted if t == 0 else tips[r] + weighted
-            for r in range(4):
-                total = jnp.sum(tips[r], axis=0, keepdims=True)
-                for t in range(CZ // 128):
-                    tips_ref[8 * x + t, c, r : r + 1, :] = total[:, 128 * t : 128 * t + 128]
-        stored(c).start()
-    for c in range(3):
-        stored(c).wait()
-
-
-def main_part(*operands):
+
+def main_part(halos, moved, others):
     return pl.pallas_call(
         main_kernel,
         out_shape=(
-            shaped(3, TOTAL),
-            shaped(3, CX, ROWS, CZ),
-            shaped(SLABS, 3, 4, 128),
+            far_out(3, TOTAL),
+            far_out(SLABS, 3, 4, 128),
+            held((3, CX, ROWS, CZ)),
         ),
-        in_specs=[ANY] * 6 + [VMEM, SMEM] + [VMEM] * 5,
-        out_specs=(VMEM, ANY, VMEM),
+        in_specs=[ANY] * 14,
+        out_specs=(ANY, ANY, VMEM),
         scratch_shapes=[
             pltpu.VMEM((3, CX, ROWS + 16, CZ), F32),
             pltpu.VMEM((3, 2, ROWS, CZ), F32),
             pltpu.VMEM((3, 2, ROWS, CZ), F32),
             pltpu.VMEM((3, CX, ROWS, CZ), F32),
-            pltpu.VMEM((3, CX, ROWS, CZ), F32),
-            pltpu.VMEM((3 * PLANES, CZ), BF16),
             pltpu.VMEM((CZ, CHUNK), BF16),
             pltpu.VMEM((8, TOTAL), F32),
             pltpu.VMEM((3 * PLANES, CZ), F32),
+            pltpu.VMEM((PEERS, 2, 128), F32),
+            pltpu.SMEM((1, PEERS), jnp.int32),
+            pltpu.VMEM((1, TOTAL), jnp.int32),
+            pltpu.VMEM((1, ROWS), F32),
+            pltpu.VMEM((1, ROWS), F32),
+            pltpu.VMEM((3, TOTAL), F32),
+            pltpu.VMEM((SLABS, 3, 4, 128), F32),
             pltpu.VMEM((2, ROWS, 128), F32),
-            pltpu.SemaphoreType.DMA((9,)),
+            pltpu.VMEM((3, TOTAL), F32),
+            pltpu.VMEM((ROWS, 128), F32),
+            pltpu.VMEM((4, ROWS, 128), F32),
+            pltpu.SemaphoreType.DMA((16,)),
         ],
-        compiler_params=params(),
+        compiler_params=params(36),
         name="main_part",
-    )(*operands)
+    )(*halos, moved, *far_in(*others))
 
 
 WIDTH = 3 * CX * CZ // SLABS
@@ -483,59 +620,76 @@
         in_specs=[VMEM, VMEM],
         out_specs=VMEM,
         scratch_shapes=[pltpu.VMEM((4 * SLABS, WIDTH), F32)],
+        compiler_params=params(4),
         name="solve",
     )(tips, green)
 
 
-def local_kernel(vel_ref, section_ref, scale_ref, solve_ref, out_ref):
+def local_kernel(vel_hbm, section_ref, scale_ref, solve_ref, section_hbm, out_ref, sems):
+    loads = [pltpu.make_async_copy(vel_hbm.at[c], out_ref.at[c], sems.at[c]) for c in range(3)]
+    for load in loads:
+        load.start()
+    store = pltpu.make_async_copy(section_ref, section_hbm, sems.at[3])
+    store.start()
     whole = solve_ref[:, 0:ROWS]
     head = whole.astype(BF16)
     rest = (whole - head.astype(F32)).astype(BF16)
     left = jnp.concatenate([head, rest, head], axis=1)
     scale = jnp.concatenate([scale_ref[...]] * 8, axis=1)
-    for x in range(CX):
-        value = section_ref[0, x] * scale
-        high = value.astype(BF16)
-        low = (value - high.astype(F32)).astype(BF16)
-        right = jnp.concatenate([high, high, low], axis=0)
-        out_ref[0, x] = vel_ref[0, x] + jnp.dot(left, right, preferred_element_type=F32)
-
-
-BLOCK = pl.BlockSpec((1, CX, ROWS, CZ), lambda c: (c, 0, 0, 0))
+    for c in range(3):
+        loads[c].wait()
+        for x in range(CX):
+            value = section_ref[c, x] * scale
+            high = value.astype(BF16)
+            low = (value - high.astype(F32)).astype(BF16)
+            right = jnp.concatenate([high, high, low], axis=0)
+            out_ref[c, x] += jnp.dot(left, right, preferred_element_type=F32)
+    store.wait()
 
 
 def local_solve(velocity, section_new, scale, solve):
     return pl.pallas_call(
         local_kernel,
-        grid=(3,),
-        out_shape=shaped(3, CX, ROWS, CZ),
-        in_specs=[BLOCK, BLOCK, VMEM, VMEM],
-        out_specs=BLOCK,
-        compiler_params=params(),
+        out_shape=(far_out(3, CX, ROWS, CZ), held((3, CX, ROWS, CZ))),
+        in_specs=[ANY, VMEM, VMEM, VMEM],
+        out_specs=(ANY, VMEM),
+        scratch_shapes=[pltpu.SemaphoreType.DMA((4,))],
+        compiler_params=params(16),
         name="local_solve",
-    )(velocity, section_new, scale, solve)
-
-
-def final_kernel(partial_ref, edge_ref, fix_ref, out_ref):
-    c = pl.program_id(0)
-    for x in range(CX):
-        for t in range(CZ // 128):
-            lanes = slice(128 * t, 128 * t + 128)
-            edge = edge_ref[8 * x + t, c]
-            value = partial_ref[0, x, :, lanes]
-            for r in range(4):
-                value = value - fix_ref[r] * edge[r : r + 1, :]
-            out_ref[0, x, :, lanes] = value
+    )(*far_in(velocity), section_new, scale, solve)
+
+
+def final_kernel(partial_ref, edge_ref, fix_ref, out_hbm, out_ref, sems):
+    stores = []
+    for c in range(3):
+        for x in range(CX):
+            for t in range(CZ // 128):
+                lanes = slice(128 * t, 128 * t + 128)
+                edge = edge_ref[8 * x + t, c]
+                value = partial_ref[c, x, :, lanes]
+                for r in range(4):
+                    value = value - fix_ref[r] * edge[r : r + 1, :]
+                out_ref[c, x, :, lanes] = value
+            if x % 2 == 1:
+                span = pl.ds(x - 1, 2)
+                stores.append(
+                    pltpu.make_async_copy(
+                        out_ref.at[c, span], out_hbm.at[c, span], sems.at[len(stores)]
+                    )
+                )
+                stores[-1].start()
+    for copy in stores:
+        copy.wait()
 
 
 def finished(partial, edges, fix):
     return pl.pallas_call(
         final_kernel,
-        grid=(3,),
-        out_shape=shaped(3, CX, ROWS, CZ),
-        in_specs=[BLOCK, VMEM, VMEM],
-        out_specs=BLOCK,
-        compiler_params=params(),
+        out_shape=far_out(3, CX, ROWS, CZ),
+        in_specs=[VMEM] * 3,
+        out_specs=ANY,
+        scratch_shapes=[pltpu.VMEM((3, CX, ROWS, CZ), F32), pltpu.SemaphoreType.DMA((6,))],
+        compiler_params=params(16),
         name="finish",
     )(partial, edges, fix)
 
@@ -546,19 +700,19 @@
     down_x = [(t, s) for s, t in up_x]
     up_y = [(i, i + 1) for i in range(n_gy - 1)]
     down_y = [(t, s) for s, t in up_y]
-    before = lax.ppermute(velocity[:, CX - 2 :], "gx", up_x)
-    behind = lax.ppermute(velocity[:, :2], "gx", down_x)
-    moved = lax.all_to_all(
-        packed(part_vel, part_rate.reshape(1, TOTAL)),
-        ("gx", "gy"), split_axis=0, concat_axis=0, tiled=True,
+    high, low, top, bottom, packed, vel_held = prepared(
+        velocity, part_vel, part_rate.reshape(1, TOTAL)
     )
-    below = lax.ppermute(velocity[:, :, ROWS - 2 :], "gy", up_y)
-    above = lax.ppermute(velocity[:, :, :2], "gy", down_y)
+    before = lax.ppermute(high, "gx", up_x)
+    behind = lax.ppermute(low, "gx", down_x)
+    below = lax.ppermute(top, "gy", up_y)
+    above = lax.ppermute(bottom, "gy", down_y)
+    moved = lax.all_to_all(packed, ("gx", "gy"), split_axis=0, concat_axis=0, tiled=True)
     place = lax.axis_index("gy").astype(jnp.int32).reshape(1)
-    scale, tip, fix, solve = own_factors(place, diffusion.reshape(8, 128))
-    part_new, section_new, tips = main_part(
-        velocity, below, above, before, behind, section, moved, counts, cell_slot,
-        rhs_near.reshape(1, ROWS), rhs_far.reshape(1, ROWS), scale, tip,
+    fluid, scale, tip, fix, solve = find(place, vel_held, cell_slot, diffusion.reshape(8, 128))
+    part_new, tips, new_held = main_part(
+        (below, above, before, behind), moved,
+        (fluid, scale, tip, velocity, section, counts, cell_slot, rhs_near.reshape(1, ROWS), rhs_far.reshape(1, ROWS)),
     )
     tips, diffusion = lax.optimization_barrier((tips, diffusion))
     all_tips = lax.all_to_all(tips, "gy", split_axis=0, concat_axis=0, tiled=True)
@@ -566,9 +720,10 @@
         diffusion.reshape(SLABS, ROWS).T, ((0, 0), (0, 128 - SLABS)), constant_values=1000.0
     )
     reply = solved(all_tips, green_operator(rate))
-    reply, section_done = lax.optimization_barrier((reply, section_new))
+    reply, solve = lax.optimization_barrier((reply, solve))
     edges = lax.all_to_all(reply, "gy", split_axis=0, concat_axis=0, tiled=True)
-    velocity_new = finished(local_solve(velocity, section_done, scale, solve), edges, fix)
+    section_new, partial = local_solve(velocity, new_held, scale, solve)
+    velocity_new = finished(partial, edges, fix)
     return (velocity_new, section_new, part_new)
 
 

time: 87.4 us -> 73.1 us (0.84)
  Pallas kernels: 37.1 us -> 28.3 us
  local copies, waits for them, and re-layouts: 5.96 us -> 0.17 us
  waiting for transfers between devices: 10.3 us -> 12.8 us
  starting transfers between devices: 32.8 us -> 30.4 us
    pallas_call x5, Pallas kernels: 32.5 us -> 26 us  [the longest x1 10.9 us: main_part(): pl.pallas_call(main_kernel, out_shape=(far_out(3, TOTAL), far_out(SLABS,...]
    slice x2 -> x0, local copies, waits for them, and re-layouts: 2.67 us -> none  [the longest x1 1.48 us: local(): behind = lax.ppermute(velocity[:, :2], 'gx', down_x)]
    unnamed x12 -> x8, local copies, waits for them, and re-layouts: 2.53 us -> 0.02 us
    all_to_all x1, waiting for transfers between devices: 4.92 us -> 6.85 us  [local(): lax.all_to_all(tips, 'gy', split_axis=0, concat_axis=0, tiled=True)]
    all_to_all x1, waiting for transfers between devices: 4.01 us -> 5.9 us  [local(): edges = lax.all_to_all(reply, 'gy', split_axis=0, concat_axis=0, tiled=True)]
    pallas_call x1, Pallas kernels: 2.57 us -> 1.25 us  [green_operator(): pl.pallas_call(green_kernel, out_shape=shaped(128, 128), in_specs=[VMEM],...]
    all_to_all x1, waiting for transfers between devices: 1.31 us -> 0.01 us  [local(): lax.all_to_all(packed, ('gx', 'gy'), split_axis=0, concat_axis=0, tiled=T...]
    all_to_all x1, starting transfers between devices: 10.1 us -> 8.85 us  [local(): lax.all_to_all(packed, ('gx', 'gy'), split_axis=0, concat_axis=0, tiled=T...]
  transfers between devices with their start and end apart: 7 -> 7, of which waited for: 3 -> 2; matrix products, arithmetic and copies ran while one was open for 2% -> 0% of each run, Pallas kernels for 12% -> 17%
where the time goes in v3:
time: 73.1 us; the launch traced here: 72.6 us
  starting transfers between devices  30.4 us (42%)
  Pallas kernels  28.3 us (39%)
  waiting for transfers between devices  12.8 us (18%)
  between operations  0.97 us (1%)
    pallas_call x1, Pallas kernels, main_part(): pl.pallas_call(main_kernel, out_shape=(far_out(3, TOTAL), far_out(SLABS,...  10.9 us
    all_to_all x1, starting transfers between devices, local(): lax.all_to_all(packed, ('gx', 'gy'), split_axis=0, concat_axis=0, tiled=T...  8.85 us
    pallas_call x1, Pallas kernels, find(): pl.pallas_call(find_kernel, out_shape=(far_out(3, TOTAL), far_out(ROWS, 1...  8.56 us
    all_to_all x1, starting transfers between devices, local(): lax.all_to_all(tips, 'gy', split_axis=0, concat_axis=0, tiled=True)  7.5 us
    all_to_all x1, waiting for transfers between devices, local(): lax.all_to_all(tips, 'gy', split_axis=0, concat_axis=0, tiled=True)  6.85 us
    all_to_all x1, waiting for transfers between devices, local(): edges = lax.all_to_all(reply, 'gy', split_axis=0, concat_axis=0, tiled=True)  5.9 us
    all_to_all x1, starting transfers between devices, local(): edges = lax.all_to_all(reply, 'gy', split_axis=0, concat_axis=0, tiled=True)  3.8 us
    ppermute x1, starting transfers between devices, local(): below = lax.ppermute(top, 'gy', up_y)  3.54 us
  transfers between devices with their start and end apart: 7, of which 2 were waited for; matrix products, arithmetic and copies ran while one was open for 0% of the time, Pallas kernels for 17%

profile of v3, /device:TPU:1, one launch (start us, length us, event | category | flops | bytes accessed | tf_op | source)
XLA Modules:
  0.0 72.6 jit_solution(13905303978173330356)
XLA Ops:
  0.6 3.0 %prepare.1 = (f32[3,2,32,1024]{3,2,1,0:T(8,128)}, f32[3,2,32,1024]{3,2,1,0:T(8,128)}, f32[3,4,2,1024]{3,2,1,0:T(2,128)}, f32[3,4,2,1024]{3,2,1,0:T(2,128)}, f32[...) custom-call(f32[3,4,32,1024]{3,2,1,0:T(8,128)} %vel_hbm.5, f32[3,8192]{1,0:T(4,128)} %part_hbm.1, f32[1,8192]{1,0:T(1,128)} %bitcast.7), custom_call_target="tpu_custom_call" | custom-call | tf_op jit(solution)/shard_map/prepare/pallas_call | solution.py:306
  3.7 2.5 %collective-permute-start.2 = (f32[3,2,32,1024]{3,2,1,0:T(8,128)}, f32[3,2,32,1024]{3,2,1,0:T(8,128)S(1)}, u32[]{:S(2)}, u32[]{:S(2)}) collective-permute-start(f32[3,2,32,1024]{3,2,1,0:T(8,128)} %get-tuple-element.25), channel_id=1, source_target_pairs={{0,32},{32,64},{64,96},{96,0},{1,33},{33,65},{65,97},{97,1},{2,34}... | collective-permute-start | bytes 2359304 | tf_op jit(solution)/shard_map/ppermute | solution.py:706
  6.2 2.2 %collective-permute-start.3 = (f32[3,2,32,1024]{3,2,1,0:T(8,128)}, f32[3,2,32,1024]{3,2,1,0:T(8,128)S(1)}, u32[]{:S(2)}, u32[]{:S(2)}) collective-permute-start(f32[3,2,32,1024]{3,2,1,0:T(8,128)} %get-tuple-element.26), channel_id=1, source_target_pairs={{32,0},{64,32},{96,64},{0,96},{33,1},{65,33},{97,65},{1,97},{34,2}... | collective-permute-start | bytes 2359304 | tf_op jit(solution)/shard_map/ppermute | solution.py:707
  8.4 8.9 %all-to-all-start = ((f32[128,2,128]{2,1,0:T(2,128)}), f32[128,2,128]{2,1,0:T(2,128)S(1)}, u32[]{:S(2)}, u32[]{:S(2)}) async-start(f32[128,2,128]{2,1,0:T(2,128)} %get-tuple-element.27), calls=%async_computation | async-start | bytes 262144 | tf_op jit(solution)/shard_map/all_to_all | solution.py:710
  17.3 3.5 %collective-permute-start = (f32[3,4,2,1024]{3,2,1,0:T(2,128)}, f32[3,4,2,1024]{3,2,1,0:T(2,128)S(1)}, u32[]{:S(2)}, u32[]{:S(2)}) collective-permute-start(f32[3,4,2,1024]{3,2,1,0:T(2,128)} %get-tuple-element.23), channel_id=1, source_target_pairs={{0,1},{1,2},{2,3},{3,4},{4,5},{5,6},{6,7},{7,8},{8,9},{9,10},{10,1... | collective-permute-start | bytes 294920 | tf_op jit(solution)/shard_map/ppermute | solution.py:708
  20.8 1.9 %collective-permute-start.1 = (f32[3,4,2,1024]{3,2,1,0:T(2,128)}, f32[3,4,2,1024]{3,2,1,0:T(2,128)S(1)}, u32[]{:S(2)}, u32[]{:S(2)}) collective-permute-start(f32[3,4,2,1024]{3,2,1,0:T(2,128)} %get-tuple-element.24), channel_id=1, source_target_pairs={{1,0},{2,1},{3,2},{4,3},{5,4},{6,5},{7,6},{8,7},{9,8},{10,9},{11,1... | collective-permute-start | bytes 294920 | tf_op jit(solution)/shard_map/ppermute | solution.py:709
  22.7 8.6 %find.1 = (f32[3,8192]{1,0:T(4,128)}, f32[32,128]{1,0:T(8,128)}, f32[4,32,128]{2,1,0:T(8,128)}, f32[4,32,128]{2,1,0:T(8,128)}, f32[32,128]{1,0:T(8,128)}) custom-call(s32[1]{0:T(128)} %bitcast.1.place_ref, f32[3,4,32,1024]{3,2,1,0:T(8,128)S(1)} %get-tuple-element.28.vel_ref, s32[1,8192]{1,0:T(1,128)} %cell_hbm.3, f32[8,128]{1,0:T(8,128)} %bitcast.8), custom_call_target="tpu_custom_call" | custom-call | tf_op jit(solution)/shard_map/find/pallas_call | solution.py:386
  31.3 0.0 collective-permute-done.below_hbm
  31.3 0.0 collective-permute-done.1.above_hbm
  31.3 0.0 all-to-all-done.moved_hbm
  31.3 0.0 collective-permute-done.2.before_hbm
  31.4 0.0 collective-permute-done.3.behind_hbm
  31.4 0.0 copy-start.3
  31.4 0.0 copy-start
  31.4 0.0 copy-start.2
  31.4 10.9 %main_part.1 = (f32[3,8192]{1,0:T(4,128)}, f32[32,3,4,128]{3,2,1,0:T(4,128)}, f32[3,4,32,1024]{3,2,1,0:T(8,128)S(1)}) custom-call(f32[3,4,2,1024]{3,2,1,0:T(2,128)S(1)} %collective-permute-done.below_hbm, f32[3,4,2,1024]{3,2,1,0:T(2,128)S(1)} %collective-permute-done.1.above_hbm, f32[3,2,32,1024]{3,2,1,0:T(8,128)S(1)} %collective-permute-done.2.before_hbm, ...), custom_call_target="tpu_custom_call" | custom-call | tf_op jit(solution)/shard_map/main_part/pallas_call | solution.py:568
  42.3 7.5 %all-to-all-start.1 = ((f32[32,3,4,128]{3,2,1,0:T(4,128)}), f32[32,3,4,128]{3,2,1,0:T(4,128)S(1)}, u32[]{:S(2)}, u32[]{:S(2)}) async-start(f32[32,3,4,128]{3,2,1,0:T(4,128)} %get-tuple-element.34), calls=%async_computation.1 | async-start | bytes 393216 | tf_op jit(solution)/shard_map/all_to_all | solution.py:718
  49.8 0.0 copy-done.3
  49.8 0.1 reshape.29
  49.8 0.1 copy.12
  49.9 1.2 %green_operator.1.green_ref = f32[128,128]{1,0:T(8,128)S(1)} custom-call(f32[32,128]{1,0:T(8,128)S(1)} %pad.4.rate_ref), custom_call_target="tpu_custom_call" | custom-call | tf_op jit(solution)/shard_map/green_operator/pallas_call | solution.py:254
  51.2 6.8 %all-to-all-done.1.tips_ref = f32[32,3,4,128]{3,2,1,0:T(4,128)S(1)} async-done(((f32[32,3,4,128]{3,2,1,0:T(4,128)}), f32[32,3,4,128]{3,2,1,0:T(4,128)S(1)}, u32[]{:S(2)}, u32[]{:S(2)}) %all-to-all-start.1) | async-done | bytes 196640 | tf_op jit(solution)/shard_map/all_to_all | solution.py:718
  58.0 1.0 %solve.1 = f32[32,3,4,128]{3,2,1,0:T(4,128)} custom-call(f32[32,3,4,128]{3,2,1,0:T(4,128)S(1)} %all-to-all-done.1.tips_ref, f32[128,128]{1,0:T(8,128)S(1)} %green_operator.1.green_ref), custom_call_target="tpu_custom_call" | custom-call | tf_op jit(solution)/shard_map/solve/pallas_call | solution.py:617
  59.1 3.8 %all-to-all-start.2 = ((f32[32,3,4,128]{3,2,1,0:T(4,128)}), f32[32,3,4,128]{3,2,1,0:T(4,128)S(1)}, u32[]{:S(2)}, u32[]{:S(2)}) async-start(f32[32,3,4,128]{3,2,1,0:T(4,128)} %solve.1), calls=%async_computation.2 | async-start | bytes 393216 | tf_op jit(solution)/shard_map/all_to_all | solution.py:724
  62.9 0.0 copy-done
  62.9 0.0 copy-done.2
  62.9 0.0 copy-start.1
  62.9 2.3 %local_solve.1 = (f32[3,4,32,1024]{3,2,1,0:T(8,128)}, f32[3,4,32,1024]{3,2,1,0:T(8,128)S(1)}) custom-call(f32[3,4,32,1024]{3,2,1,0:T(8,128)} %vel_hbm.5, f32[3,4,32,1024]{3,2,1,0:T(8,128)S(1)} %get-tuple-element.32.section_ref, f32[32,128]{1,0:T(8,128)S(1)} %copy-done, f32[32,128]{1,0:T(8,128)S(1)} %copy-done.2), custom_call_target="tpu_custom_call" | custom-call | tf_op jit(solution)/shard_map/local_solve/pallas_call | solution.py:651
  65.2 5.9 %all-to-all-done.2.edge_ref = f32[32,3,4,128]{3,2,1,0:T(4,128)S(1)} async-done(((f32[32,3,4,128]{3,2,1,0:T(4,128)}), f32[32,3,4,128]{3,2,1,0:T(4,128)S(1)}, u32[]{:S(2)}, u32[]{:S(2)}) %all-to-all-start.2) | async-done | bytes 196640 | tf_op jit(solution)/shard_map/all_to_all | solution.py:724
  71.1 0.0 copy-done.1
  71.1 1.3 %finish.1 = f32[3,4,32,1024]{3,2,1,0:T(8,128)} custom-call(f32[3,4,32,1024]{3,2,1,0:T(8,128)S(1)} %get-tuple-element.38.partial_ref, f32[32,3,4,128]{3,2,1,0:T(4,128)S(1)} %all-to-all-done.2.edge_ref, f32[4,32,128]{2,1,0:T(8,128)S(1)} %copy-done.1), custom_call_target="tpu_custom_call" | custom-call | tf_op jit(solution)/shard_map/finish/pallas_call | solution.py:686
  (1 shorter events, 0.0 us)
Async XLA Ops:
  3.7 27.7 %collective-permute-start.2 = (f32[3,2,32,1024]{3,2,1,0:T(8,128)}, f32[3,2,32,1024]{3,2,1,0:T(8,128)S(1)}, u32[]{:S(2)}, u32[]{:S(2)}) collective-permute-start(f32[3,2,32,1024]{3,2,1,0:T(8,128)} %get-tuple-element.25), channel_id=1, source_target_pairs={{0,32},{32,64},{64,96},{96,0},{1,33},{33,65},{65,97},{97,1},{2,34}... | collective-permute-start | bytes 2359304 | tf_op jit(solution)/shard_map/ppermute | solution.py:706
  6.2 25.2 %collective-permute-start.3 = (f32[3,2,32,1024]{3,2,1,0:T(8,128)}, f32[3,2,32,1024]{3,2,1,0:T(8,128)S(1)}, u32[]{:S(2)}, u32[]{:S(2)}) collective-permute-start(f32[3,2,32,1024]{3,2,1,0:T(8,128)} %get-tuple-element.26), channel_id=1, source_target_pairs={{32,0},{64,32},{96,64},{0,96},{33,1},{65,33},{97,65},{1,97},{34,2}... | collective-permute-start | bytes 2359304 | tf_op jit(solution)/shard_map/ppermute | solution.py:707
  8.4 22.9 %all-to-all-start = ((f32[128,2,128]{2,1,0:T(2,128)}), f32[128,2,128]{2,1,0:T(2,128)S(1)}, u32[]{:S(2)}, u32[]{:S(2)}) async-start(f32[128,2,128]{2,1,0:T(2,128)} %get-tuple-element.27), calls=%async_computation | async-start | bytes 262144 | tf_op jit(solution)/shard_map/all_to_all | solution.py:710
  17.3 14.1 %collective-permute-start = (f32[3,4,2,1024]{3,2,1,0:T(2,128)}, f32[3,4,2,1024]{3,2,1,0:T(2,128)S(1)}, u32[]{:S(2)}, u32[]{:S(2)}) collective-permute-start(f32[3,4,2,1024]{3,2,1,0:T(2,128)} %get-tuple-element.23), channel_id=1, source_target_pairs={{0,1},{1,2},{2,3},{3,4},{4,5},{5,6},{6,7},{7,8},{8,9},{9,10},{10,1... | collective-permute-start | bytes 294920 | tf_op jit(solution)/shard_map/ppermute | solution.py:708
  20.8 10.5 %collective-permute-start.1 = (f32[3,4,2,1024]{3,2,1,0:T(2,128)}, f32[3,4,2,1024]{3,2,1,0:T(2,128)S(1)}, u32[]{:S(2)}, u32[]{:S(2)}) collective-permute-start(f32[3,4,2,1024]{3,2,1,0:T(2,128)} %get-tuple-element.24), channel_id=1, source_target_pairs={{1,0},{2,1},{3,2},{4,3},{5,4},{6,5},{7,6},{8,7},{9,8},{10,9},{11,1... | collective-permute-start | bytes 294920 | tf_op jit(solution)/shard_map/ppermute | solution.py:709
  31.4 18.4 %copy-start.3 = (f32[1024]{0:T(1024)S(1)}, f32[1024]{0:T(1024)}, u32[]{:S(2)}) copy-start(f32[1024]{0:T(1024)} %param.11) | copy-start | bytes 12292
  31.4 31.5 %copy-start = (f32[32,128]{1,0:T(8,128)S(1)}, f32[32,128]{1,0:T(8,128)}, u32[]{:S(2)}) copy-start(f32[32,128]{1,0:T(8,128)} %get-tuple-element.30.scale_hbm.scale_ref) | copy-start | bytes 49156
  31.4 31.5 %copy-start.2 = (f32[32,128]{1,0:T(8,128)S(1)}, f32[32,128]{1,0:T(8,128)}, u32[]{:S(2)}) copy-start(f32[32,128]{1,0:T(8,128)} %get-tuple-element.37.solve_ref) | copy-start | bytes 49156
  42.3 15.8 %all-to-all-start.1 = ((f32[32,3,4,128]{3,2,1,0:T(4,128)}), f32[32,3,4,128]{3,2,1,0:T(4,128)S(1)}, u32[]{:S(2)}, u32[]{:S(2)}) async-start(f32[32,3,4,128]{3,2,1,0:T(4,128)} %get-tuple-element.34), calls=%async_computation.1 | async-start | bytes 393216 | tf_op jit(solution)/shard_map/all_to_all | solution.py:718
  59.1 12.1 %all-to-all-start.2 = ((f32[32,3,4,128]{3,2,1,0:T(4,128)}), f32[32,3,4,128]{3,2,1,0:T(4,128)S(1)}, u32[]{:S(2)}, u32[]{:S(2)}) async-start(f32[32,3,4,128]{3,2,1,0:T(4,128)} %solve.1), calls=%async_computation.2 | async-start | bytes 393216 | tf_op jit(solution)/shard_map/all_to_all | solution.py:724
  62.9 8.2 %copy-start.1 = (f32[4,32,128]{2,1,0:T(8,128)S(1)}, f32[4,32,128]{2,1,0:T(8,128)}, u32[]{:S(2)}) copy-start(f32[4,32,128]{2,1,0:T(8,128)} %get-tuple-element.40.fix_ref) | copy-start | bytes 196612

commit v4 on v3

--- a/solution.py
+++ b/solution.py
@@ -263,9 +263,10 @@
 
 
 def pre_kernel(
-    vel_hbm, part_hbm, rate_hbm, high_hbm, low_hbm, below_hbm, above_hbm, packed_hbm, vel_ref,
-    part_ref, rate_ref, out_ref, sems,
+    place_ref, vel_hbm, part_hbm, rate_hbm, high_hbm, low_hbm, inner_hbm, outer_hbm, packed_hbm,
+    vel_ref, part_ref, rate_ref, out_ref, sems,
 ):
+    even = place_ref[0] % 2 == 0
     into = [
         pltpu.make_async_copy(vel_hbm.at[:, 2:4], vel_ref.at[:, 2:4], sems.at[0]),
         pltpu.make_async_copy(vel_hbm.at[:, 0:2], vel_ref.at[:, 0:2], sems.at[1]),
@@ -277,8 +278,8 @@
     out = [
         pltpu.make_async_copy(vel_ref.at[:, 2:4], high_hbm, sems.at[4]),
         pltpu.make_async_copy(vel_ref.at[:, 0:2], low_hbm, sems.at[5]),
-        pltpu.make_async_copy(vel_ref.at[:, :, ROWS - 2 : ROWS], below_hbm, sems.at[6]),
-        pltpu.make_async_copy(vel_ref.at[:, :, 0:2], above_hbm, sems.at[7]),
+        pltpu.make_async_copy(vel_ref.at[:, :, ROWS - 2 : ROWS], inner_hbm, sems.at[6]),
+        pltpu.make_async_copy(vel_ref.at[:, :, 0:2], outer_hbm, sems.at[7]),
         pltpu.make_async_copy(out_ref, packed_hbm, sems.at[8]),
     ]
     into[2].wait()
@@ -296,13 +297,22 @@
     out[0].start()
     into[1].wait()
     out[1].start()
-    out[2].start()
-    out[3].start()
+
+    @pl.when(even)
+    def _():
+        out[2].start()
+        out[3].start()
+
+    @pl.when(jnp.logical_not(even))
+    def _():
+        pltpu.make_async_copy(vel_ref.at[:, :, 0:2], inner_hbm, sems.at[6]).start()
+        pltpu.make_async_copy(vel_ref.at[:, :, ROWS - 2 : ROWS], outer_hbm, sems.at[7]).start()
+
     for copy in out:
         copy.wait()
 
 
-def prepared(velocity, part_vel, part_rate):
+def prepared(place, velocity, part_vel, part_rate):
     return pl.pallas_call(
         pre_kernel,
         out_shape=(
@@ -313,7 +323,7 @@
             far_out(PEERS, 2, 128),
             held((3, CX, ROWS, CZ)),
         ),
-        in_specs=[ANY] * 3,
+        in_specs=[SMEM] + [ANY] * 3,
         out_specs=(ANY,) * 5 + (VMEM,),
         scratch_shapes=[
             pltpu.VMEM((3, TOTAL), F32),
@@ -323,7 +333,7 @@
         ],
         compiler_params=params(16),
         name="prepare",
-    )(*far_in(velocity, part_vel, part_rate))
+    )(place, *far_in(velocity, part_vel, part_rate))
 
 
 def halves(cells):
@@ -354,9 +364,11 @@
 
 
 def find_kernel(
-    place_ref, vel_ref, cell_hbm, rate_hbm, fluid_ref, scale_ref, tip_ref, fix_ref, solve_ref,
-    bf_ref, table_ref, cell_ref, rate_ref, wide_ref, sems,
+    place_ref, vel_ref, cell_hbm, rate_hbm, *refs,
 ):
+    outs, held_refs = refs[:5], refs[5:10]
+    fluid_ref, scale_ref, tip_ref, fix_ref, solve_ref = held_refs
+    bf_ref, table_ref, cell_ref, rate_ref, wide_ref, sems = refs[10:]
     copies = [
         pltpu.make_async_copy(cell_hbm, cell_ref, sems.at[0]),
         pltpu.make_async_copy(rate_hbm, rate_ref, sems.at[1]),
@@ -370,6 +382,11 @@
     for copy in copies:
         copy.wait()
     own_factors(place_ref[0], rate_ref, scale_ref, tip_ref, fix_ref, solve_ref, wide_ref)
+    stores = [
+        pltpu.make_async_copy(held_refs[n], outs[n], sems.at[1 + n]) for n in range(1, 5)
+    ]
+    for store in stores:
+        store.start()
     for step in range(TOTAL // CHUNK):
         lanes = slice(step * CHUNK, (step + 1) * CHUNK)
         plane, high, low = halves(cell_ref[:, lanes])
@@ -380,6 +397,14 @@
             fluid_ref[n : n + 1, lanes] = jnp.sum(
                 jnp.where(mask, at[n * PLANES : (n + 1) * PLANES], 0.0), axis=0, keepdims=True
             )
+        stores.append(
+            pltpu.make_async_copy(
+                fluid_ref.at[:, lanes], outs[0].at[:, lanes], sems.at[6 + step]
+            )
+        )
+        stores[-1].start()
+    for store in stores:
+        store.wait()
 
 
 def find(place, vel_held, cells, rate):
@@ -393,14 +418,19 @@
             far_out(ROWS, 128),
         ),
         in_specs=[SMEM, VMEM, ANY, ANY],
-        out_specs=(VMEM,) * 5,
+        out_specs=(ANY,) * 5,
         scratch_shapes=[
+            pltpu.VMEM((3, TOTAL), F32),
+            pltpu.VMEM((ROWS, 128), F32),
+            pltpu.VMEM((4, ROWS, 128), F32),
+            pltpu.VMEM((4, ROWS, 128), F32),
+            pltpu.VMEM((ROWS, 128), F32),
             pltpu.VMEM((3 * PLANES, CZ), BF16),
             pltpu.VMEM((CZ, CHUNK), BF16),
             pltpu.VMEM((1, TOTAL), jnp.int32),
             pltpu.VMEM((8, 128), F32),
             pltpu.VMEM((ROWS, 128), F32),
-            pltpu.SemaphoreType.DMA((2,)),
+            pltpu.SemaphoreType.DMA((6 + TOTAL // CHUNK,)),
         ],
         compiler_params=params(28),
         name="find",
@@ -408,7 +438,7 @@
 
 
 def main_kernel(
-    below_hbm, above_hbm, before_hbm, behind_hbm, moved_hbm,
+    place_ref, inner_hbm, outer_hbm, before_hbm, behind_hbm, moved_hbm,
     fluid_hbm, scale_hbm, tip_hbm, vel_hbm, section_hbm, count_hbm, cell_hbm, near_hbm, far_hbm,
     part_hbm, tips_hbm, new_ref,
     pad_ref, before_ref, behind_ref, section_ref, table_ref, got_ref, deposit_ref, moved_ref,
@@ -425,15 +455,29 @@
         (near_hbm, near_ref),
         (far_hbm, far_ref),
         (vel_hbm, pad_ref.at[:, :, 8 : 8 + ROWS, :]),
-        (below_hbm, pad_ref.at[:, :, 6:8, :]),
-        (above_hbm, pad_ref.at[:, :, 8 + ROWS : 10 + ROWS, :]),
+        (inner_hbm, pad_ref.at[:, :, 6:8, :]),
+        (outer_hbm, pad_ref.at[:, :, 8 + ROWS : 10 + ROWS, :]),
         (before_hbm, before_ref),
         (behind_hbm, behind_ref),
         (section_hbm, section_ref),
     ]
     copies = [pltpu.make_async_copy(a, b, sems.at[n]) for n, (a, b) in enumerate(sources)]
-    for copy in copies:
-        copy.start()
+    swaps = [n for n, (a, b) in enumerate(sources) if a is inner_hbm or a is outer_hbm]
+    for n, copy in enumerate(copies):
+        if n not in swaps:
+            copy.start()
+    even = place_ref[0] % 2 == 0
+
+    @pl.when(even)
+    def _():
+        for n, source in zip(swaps, (outer_hbm, inner_hbm)):
+            pltpu.make_async_copy(source, sources[n][1], sems.at[n]).start()
+
+    @pl.when(jnp.logical_not(even))
+    def _():
+        for n in swaps:
+            copies[n].start()
+
     steps = TOTAL // CHUNK
 
     def lanes_of(step):
@@ -517,6 +561,9 @@
             for c, x in planes[share * (step - 1) : share * step]:
                 stencil(c, x)
         last = step == steps - 1
+        if last:
+            stores = [pltpu.make_async_copy(part_ref, part_hbm, sems.at[14])]
+            stores[0].start()
         wide = CZ // 4 if last else CZ
         for z in range(0, CZ, wide):
             new = lax.dot_general(
@@ -549,22 +596,24 @@
                         tips_ref[8 * x + z // 128 + k, c, r : r + 1, :] = summed[
                             :, 128 * k : 128 * k + 128
                         ]
+            for x in range(CX if last else 0):
+                span = pl.ds(8 * x + z // 128, wide // 128)
+                stores.append(
+                    pltpu.make_async_copy(
+                        tips_ref.at[span], tips_hbm.at[span], sems.at[14 + len(stores)]
+                    )
+                )
+                stores[-1].start()
         if step == 0:
             for copy in copies[4:]:
                 copy.wait()
             coef_ref[0] = column_of(near_ref[...], ROWS)
             coef_ref[1] = column_of(far_ref[...], ROWS)
-    stores = [
-        pltpu.make_async_copy(tips_ref, tips_hbm, sems.at[14]),
-        pltpu.make_async_copy(part_ref, part_hbm, sems.at[15]),
-    ]
-    for copy in stores:
-        copy.start()
-    for copy in stores:
-        copy.wait()
-
-
-def main_part(halos, moved, others):
+    for store in stores:
+        store.wait()
+
+
+def main_part(place, halos, moved, others):
     return pl.pallas_call(
         main_kernel,
         out_shape=(
@@ -572,7 +621,7 @@
             far_out(SLABS, 3, 4, 128),
             held((3, CX, ROWS, CZ)),
         ),
-        in_specs=[ANY] * 14,
+        in_specs=[SMEM] + [ANY] * 14,
         out_specs=(ANY, ANY, VMEM),
         scratch_shapes=[
             pltpu.VMEM((3, CX, ROWS + 16, CZ), F32),
@@ -593,11 +642,11 @@
             pltpu.VMEM((3, TOTAL), F32),
             pltpu.VMEM((ROWS, 128), F32),
             pltpu.VMEM((4, ROWS, 128), F32),
-            pltpu.SemaphoreType.DMA((16,)),
+            pltpu.SemaphoreType.DMA((31,)),
         ],
         compiler_params=params(36),
         name="main_part",
-    )(*halos, moved, *far_in(*others))
+    )(place, *halos, moved, *far_in(*others))
 
 
 WIDTH = 3 * CX * CZ // SLABS
@@ -698,20 +747,20 @@
     n_gx, n_gy = lax.axis_size("gx"), lax.axis_size("gy")
     up_x = [(i, (i + 1) % n_gx) for i in range(n_gx)]
     down_x = [(t, s) for s, t in up_x]
-    up_y = [(i, i + 1) for i in range(n_gy - 1)]
-    down_y = [(t, s) for s, t in up_y]
-    high, low, top, bottom, packed, vel_held = prepared(
-        velocity, part_vel, part_rate.reshape(1, TOTAL)
+    place = lax.axis_index("gy").astype(jnp.int32).reshape(1)
+    high, low, inner, outer, packed, vel_held = prepared(
+        place, velocity, part_vel, part_rate.reshape(1, TOTAL)
     )
     before = lax.ppermute(high, "gx", up_x)
     behind = lax.ppermute(low, "gx", down_x)
-    below = lax.ppermute(top, "gy", up_y)
-    above = lax.ppermute(bottom, "gy", down_y)
+    inner = lax.ppermute(inner, "gy", [(i, i ^ 1) for i in range(n_gy)])
+    outer = lax.ppermute(
+        outer, "gy", [pair for i in range(1, n_gy - 1, 2) for pair in ((i, i + 1), (i + 1, i))]
+    )
     moved = lax.all_to_all(packed, ("gx", "gy"), split_axis=0, concat_axis=0, tiled=True)
-    place = lax.axis_index("gy").astype(jnp.int32).reshape(1)
     fluid, scale, tip, fix, solve = find(place, vel_held, cell_slot, diffusion.reshape(8, 128))
     part_new, tips, new_held = main_part(
-        (below, above, before, behind), moved,
+        place, (inner, outer, before, behind), moved,
         (fluid, scale, tip, velocity, section, counts, cell_slot, rhs_near.reshape(1, ROWS), rhs_far.reshape(1, ROWS)),
     )
     tips, diffusion = lax.optimization_barrier((tips, diffusion))

time: 73.1 us -> 70.7 us (0.967)
  starting transfers between devices: 30.4 us -> 28.1 us
    ppermute x2, starting transfers between devices: 5.46 us -> 3.76 us  [the longest x1 2.61 us: local(): lax.ppermute(outer, 'gy', [pair for i in range(1, n_gy - 1, 2) for pair i...]
where the time goes in v4:
time: 70.7 us; the launch traced here: 70.2 us
  Pallas kernels  28.2 us (40%)
  starting transfers between devices  28.1 us (40%)
  waiting for transfers between devices  12.8 us (18%)
  between operations  0.97 us (1%)
    pallas_call x1, Pallas kernels, main_part(): pl.pallas_call(main_kernel, out_shape=(far_out(3, TOTAL), far_out(SLABS,...  10.7 us
    all_to_all x1, starting transfers between devices, local(): lax.all_to_all(packed, ('gx', 'gy'), split_axis=0, concat_axis=0, tiled=T...  8.85 us
    pallas_call x1, Pallas kernels, find(): pl.pallas_call(find_kernel, out_shape=(far_out(3, TOTAL), far_out(ROWS, 1...  8.64 us
    all_to_all x1, starting transfers between devices, local(): lax.all_to_all(tips, 'gy', split_axis=0, concat_axis=0, tiled=True)  6.95 us
    all_to_all x1, waiting for transfers between devices, local(): lax.all_to_all(tips, 'gy', split_axis=0, concat_axis=0, tiled=True)  6.85 us
    all_to_all x1, waiting for transfers between devices, local(): edges = lax.all_to_all(reply, 'gy', split_axis=0, concat_axis=0, tiled=True)  5.9 us
    all_to_all x1, starting transfers between devices, local(): edges = lax.all_to_all(reply, 'gy', split_axis=0, concat_axis=0, tiled=True)  3.8 us
    pallas_call x1, Pallas kernels, prepared(): pl.pallas_call(pre_kernel, out_shape=(far_out(3, 2, ROWS, CZ), far_out(3,...  3.03 us
  transfers between devices with their start and end apart: 7, of which 2 were waited for; matrix products, arithmetic and copies ran while one was open for 0% of the time, Pallas kernels for 17%

profile of v4, /device:TPU:1, one launch (start us, length us, event | category | flops | bytes accessed | tf_op | source)
XLA Modules:
  0.0 70.2 jit_solution(16090320454512984840)
XLA Ops:
  0.6 3.0 %prepare.1 = (f32[3,2,32,1024]{3,2,1,0:T(8,128)}, f32[3,2,32,1024]{3,2,1,0:T(8,128)}, f32[3,4,2,1024]{3,2,1,0:T(2,128)}, f32[3,4,2,1024]{3,2,1,0:T(2,128)}, f32[...) custom-call(s32[1]{0:T(128)} %bitcast.place_ref, f32[3,4,32,1024]{3,2,1,0:T(8,128)} %vel_hbm.5, f32[3,8192]{1,0:T(4,128)} %part_hbm.1, ...), custom_call_target="tpu_custom_call" | custom-call | tf_op jit(solution)/shard_map/prepare/pallas_call | solution.py:316
  3.7 2.5 %collective-permute-start.2 = (f32[3,2,32,1024]{3,2,1,0:T(8,128)}, f32[3,2,32,1024]{3,2,1,0:T(8,128)S(1)}, u32[]{:S(2)}, u32[]{:S(2)}) collective-permute-start(f32[3,2,32,1024]{3,2,1,0:T(8,128)} %get-tuple-element.25), channel_id=1, source_target_pairs={{0,32},{32,64},{64,96},{96,0},{1,33},{33,65},{65,97},{97,1},{2,34}... | collective-permute-start | bytes 2359304 | tf_op jit(solution)/shard_map/ppermute | solution.py:754
  6.2 2.2 %collective-permute-start.3 = (f32[3,2,32,1024]{3,2,1,0:T(8,128)}, f32[3,2,32,1024]{3,2,1,0:T(8,128)S(1)}, u32[]{:S(2)}, u32[]{:S(2)}) collective-permute-start(f32[3,2,32,1024]{3,2,1,0:T(8,128)} %get-tuple-element.26), channel_id=1, source_target_pairs={{32,0},{64,32},{96,64},{0,96},{33,1},{65,33},{97,65},{1,97},{34,2}... | collective-permute-start | bytes 2359304 | tf_op jit(solution)/shard_map/ppermute | solution.py:755
  8.4 8.9 %all-to-all-start = ((f32[128,2,128]{2,1,0:T(2,128)}), f32[128,2,128]{2,1,0:T(2,128)S(1)}, u32[]{:S(2)}, u32[]{:S(2)}) async-start(f32[128,2,128]{2,1,0:T(2,128)} %get-tuple-element.27), calls=%async_computation | async-start | bytes 262144 | tf_op jit(solution)/shard_map/all_to_all | solution.py:760
  17.3 1.1 %collective-permute-start = (f32[3,4,2,1024]{3,2,1,0:T(2,128)}, f32[3,4,2,1024]{3,2,1,0:T(2,128)S(1)}, u32[]{:S(2)}, u32[]{:S(2)}) collective-permute-start(f32[3,4,2,1024]{3,2,1,0:T(2,128)} %get-tuple-element.23), channel_id=1, source_target_pairs={{0,1},{1,0},{2,3},{3,2},{4,5},{5,4},{6,7},{7,6},{8,9},{9,8},{10,11... | collective-permute-start | bytes 294920 | tf_op jit(solution)/shard_map/ppermute | solution.py:756
  18.4 2.6 %collective-permute-start.1 = (f32[3,4,2,1024]{3,2,1,0:T(2,128)}, f32[3,4,2,1024]{3,2,1,0:T(2,128)S(1)}, u32[]{:S(2)}, u32[]{:S(2)}) collective-permute-start(f32[3,4,2,1024]{3,2,1,0:T(2,128)} %get-tuple-element.24), channel_id=1, source_target_pairs={{1,2},{2,1},{3,4},{4,3},{5,6},{6,5},{7,8},{8,7},{9,10},{10,9},{11,... | collective-permute-start | bytes 294920 | tf_op jit(solution)/shard_map/ppermute | solution.py:757
  21.0 8.6 %find.1 = (f32[3,8192]{1,0:T(4,128)}, f32[32,128]{1,0:T(8,128)}, f32[4,32,128]{2,1,0:T(8,128)}, f32[4,32,128]{2,1,0:T(8,128)}, f32[32,128]{1,0:T(8,128)}) custom-call(s32[1]{0:T(128)} %bitcast.place_ref, f32[3,4,32,1024]{3,2,1,0:T(8,128)S(1)} %get-tuple-element.28.vel_ref, s32[1,8192]{1,0:T(1,128)} %cell_hbm.3, f32[8,128]{1,0:T(8,128)} %bitcast.8), custom_call_target="tpu_custom_call" | custom-call | tf_op jit(solution)/shard_map/find/pallas_call | solution.py:411
  29.7 0.0 collective-permute-done.inner_hbm
  29.7 0.0 collective-permute-done.1.outer_hbm
  29.7 0.0 all-to-all-done.moved_hbm
  29.7 0.0 collective-permute-done.2.before_hbm
  29.7 0.0 collective-permute-done.3.behind_hbm
  29.7 0.0 copy-start.3
  29.7 0.0 copy-start
  29.8 0.0 copy-start.2
  29.8 10.7 %main_part.1 = (f32[3,8192]{1,0:T(4,128)}, f32[32,3,4,128]{3,2,1,0:T(4,128)}, f32[3,4,32,1024]{3,2,1,0:T(8,128)S(1)}) custom-call(s32[1]{0:T(128)} %bitcast.place_ref, f32[3,4,2,1024]{3,2,1,0:T(2,128)S(1)} %collective-permute-done.inner_hbm, f32[3,4,2,1024]{3,2,1,0:T(2,128)S(1)} %collective-permute-done.1.outer_hbm, ...), custom_call_target="tpu_custom_call" | custom-call | tf_op jit(solution)/shard_map/main_part/pallas_call | solution.py:617
  40.5 6.9 %all-to-all-start.1 = ((f32[32,3,4,128]{3,2,1,0:T(4,128)}), f32[32,3,4,128]{3,2,1,0:T(4,128)S(1)}, u32[]{:S(2)}, u32[]{:S(2)}) async-start(f32[32,3,4,128]{3,2,1,0:T(4,128)} %get-tuple-element.34), calls=%async_computation.1 | async-start | bytes 393216 | tf_op jit(solution)/shard_map/all_to_all | solution.py:767
  47.4 0.0 copy-done.3
  47.4 0.1 reshape.29
  47.5 0.1 copy.12
  47.6 1.2 %green_operator.1.green_ref = f32[128,128]{1,0:T(8,128)S(1)} custom-call(f32[32,128]{1,0:T(8,128)S(1)} %pad.4.rate_ref), custom_call_target="tpu_custom_call" | custom-call | tf_op jit(solution)/shard_map/green_operator/pallas_call | solution.py:254
  48.8 6.8 %all-to-all-done.1.tips_ref = f32[32,3,4,128]{3,2,1,0:T(4,128)S(1)} async-done(((f32[32,3,4,128]{3,2,1,0:T(4,128)}), f32[32,3,4,128]{3,2,1,0:T(4,128)S(1)}, u32[]{:S(2)}, u32[]{:S(2)}) %all-to-all-start.1) | async-done | bytes 196640 | tf_op jit(solution)/shard_map/all_to_all | solution.py:767
  55.7 1.0 %solve.1 = f32[32,3,4,128]{3,2,1,0:T(4,128)} custom-call(f32[32,3,4,128]{3,2,1,0:T(4,128)S(1)} %all-to-all-done.1.tips_ref, f32[128,128]{1,0:T(8,128)S(1)} %green_operator.1.green_ref), custom_call_target="tpu_custom_call" | custom-call | tf_op jit(solution)/shard_map/solve/pallas_call | solution.py:666
  56.7 3.8 %all-to-all-start.2 = ((f32[32,3,4,128]{3,2,1,0:T(4,128)}), f32[32,3,4,128]{3,2,1,0:T(4,128)S(1)}, u32[]{:S(2)}, u32[]{:S(2)}) async-start(f32[32,3,4,128]{3,2,1,0:T(4,128)} %solve.1), calls=%async_computation.2 | async-start | bytes 393216 | tf_op jit(solution)/shard_map/all_to_all | solution.py:773
  60.5 0.0 copy-done
  60.5 0.0 copy-done.2
  60.5 0.0 copy-start.1
  60.5 2.3 %local_solve.1 = (f32[3,4,32,1024]{3,2,1,0:T(8,128)}, f32[3,4,32,1024]{3,2,1,0:T(8,128)S(1)}) custom-call(f32[3,4,32,1024]{3,2,1,0:T(8,128)} %vel_hbm.5, f32[3,4,32,1024]{3,2,1,0:T(8,128)S(1)} %get-tuple-element.32.section_ref, f32[32,128]{1,0:T(8,128)S(1)} %copy-done, f32[32,128]{1,0:T(8,128)S(1)} %copy-done.2), custom_call_target="tpu_custom_call" | custom-call | tf_op jit(solution)/shard_map/local_solve/pallas_call | solution.py:700
  62.9 5.9 %all-to-all-done.2.edge_ref = f32[32,3,4,128]{3,2,1,0:T(4,128)S(1)} async-done(((f32[32,3,4,128]{3,2,1,0:T(4,128)}), f32[32,3,4,128]{3,2,1,0:T(4,128)S(1)}, u32[]{:S(2)}, u32[]{:S(2)}) %all-to-all-start.2) | async-done | bytes 196640 | tf_op jit(solution)/shard_map/all_to_all | solution.py:773
  68.8 0.0 copy-done.1
  68.8 1.3 %finish.1 = f32[3,4,32,1024]{3,2,1,0:T(8,128)} custom-call(f32[3,4,32,1024]{3,2,1,0:T(8,128)S(1)} %get-tuple-element.38.partial_ref, f32[32,3,4,128]{3,2,1,0:T(4,128)S(1)} %all-to-all-done.2.edge_ref, f32[4,32,128]{2,1,0:T(8,128)S(1)} %copy-done.1), custom_call_target="tpu_custom_call" | custom-call | tf_op jit(solution)/shard_map/finish/pallas_call | solution.py:735
  (1 shorter events, 0.0 us)
Async XLA Ops:
  3.7 26.0 %collective-permute-start.2 = (f32[3,2,32,1024]{3,2,1,0:T(8,128)}, f32[3,2,32,1024]{3,2,1,0:T(8,128)S(1)}, u32[]{:S(2)}, u32[]{:S(2)}) collective-permute-start(f32[3,2,32,1024]{3,2,1,0:T(8,128)} %get-tuple-element.25), channel_id=1, source_target_pairs={{0,32},{32,64},{64,96},{96,0},{1,33},{33,65},{65,97},{97,1},{2,34}... | collective-permute-start | bytes 2359304 | tf_op jit(solution)/shard_map/ppermute | solution.py:754
  6.2 23.5 %collective-permute-start.3 = (f32[3,2,32,1024]{3,2,1,0:T(8,128)}, f32[3,2,32,1024]{3,2,1,0:T(8,128)S(1)}, u32[]{:S(2)}, u32[]{:S(2)}) collective-permute-start(f32[3,2,32,1024]{3,2,1,0:T(8,128)} %get-tuple-element.26), channel_id=1, source_target_pairs={{32,0},{64,32},{96,64},{0,96},{33,1},{65,33},{97,65},{1,97},{34,2}... | collective-permute-start | bytes 2359304 | tf_op jit(solution)/shard_map/ppermute | solution.py:755
  8.4 21.3 %all-to-all-start = ((f32[128,2,128]{2,1,0:T(2,128)}), f32[128,2,128]{2,1,0:T(2,128)S(1)}, u32[]{:S(2)}, u32[]{:S(2)}) async-start(f32[128,2,128]{2,1,0:T(2,128)} %get-tuple-element.27), calls=%async_computation | async-start | bytes 262144 | tf_op jit(solution)/shard_map/all_to_all | solution.py:760
  17.3 12.4 %collective-permute-start = (f32[3,4,2,1024]{3,2,1,0:T(2,128)}, f32[3,4,2,1024]{3,2,1,0:T(2,128)S(1)}, u32[]{:S(2)}, u32[]{:S(2)}) collective-permute-start(f32[3,4,2,1024]{3,2,1,0:T(2,128)} %get-tuple-element.23), channel_id=1, source_target_pairs={{0,1},{1,0},{2,3},{3,2},{4,5},{5,4},{6,7},{7,6},{8,9},{9,8},{10,11... | collective-permute-start | bytes 294920 | tf_op jit(solution)/shard_map/ppermute | solution.py:756
  18.4 11.3 %collective-permute-start.1 = (f32[3,4,2,1024]{3,2,1,0:T(2,128)}, f32[3,4,2,1024]{3,2,1,0:T(2,128)S(1)}, u32[]{:S(2)}, u32[]{:S(2)}) collective-permute-start(f32[3,4,2,1024]{3,2,1,0:T(2,128)} %get-tuple-element.24), channel_id=1, source_target_pairs={{1,2},{2,1},{3,4},{4,3},{5,6},{6,5},{7,8},{8,7},{9,10},{10,9},{11,... | collective-permute-start | bytes 294920 | tf_op jit(solution)/shard_map/ppermute | solution.py:757
  29.7 17.7 %copy-start.3 = (f32[1024]{0:T(1024)S(1)}, f32[1024]{0:T(1024)}, u32[]{:S(2)}) copy-start(f32[1024]{0:T(1024)} %param.11) | copy-start | bytes 12292
  29.7 30.8 %copy-start = (f32[32,128]{1,0:T(8,128)S(1)}, f32[32,128]{1,0:T(8,128)}, u32[]{:S(2)}) copy-start(f32[32,128]{1,0:T(8,128)} %get-tuple-element.30.scale_hbm.scale_ref) | copy-start | bytes 49156
  29.8 30.8 %copy-start.2 = (f32[32,128]{1,0:T(8,128)S(1)}, f32[32,128]{1,0:T(8,128)}, u32[]{:S(2)}) copy-start(f32[32,128]{1,0:T(8,128)} %get-tuple-element.37.solve_ref) | copy-start | bytes 49156
  40.5 15.2 %all-to-all-start.1 = ((f32[32,3,4,128]{3,2,1,0:T(4,128)}), f32[32,3,4,128]{3,2,1,0:T(4,128)S(1)}, u32[]{:S(2)}, u32[]{:S(2)}) async-start(f32[32,3,4,128]{3,2,1,0:T(4,128)} %get-tuple-element.34), calls=%async_computation.1 | async-start | bytes 393216 | tf_op jit(solution)/shard_map/all_to_all | solution.py:767
  56.7 12.1 %all-to-all-start.2 = ((f32[32,3,4,128]{3,2,1,0:T(4,128)}), f32[32,3,4,128]{3,2,1,0:T(4,128)S(1)}, u32[]{:S(2)}, u32[]{:S(2)}) async-start(f32[32,3,4,128]{3,2,1,0:T(4,128)} %solve.1), calls=%async_computation.2 | async-start | bytes 393216 | tf_op jit(solution)/shard_map/all_to_all | solution.py:773
  60.5 8.2 %copy-start.1 = (f32[4,32,128]{2,1,0:T(8,128)S(1)}, f32[4,32,128]{2,1,0:T(8,128)}, u32[]{:S(2)}) copy-start(f32[4,32,128]{2,1,0:T(8,128)} %get-tuple-element.40.fix_ref) | copy-start | bytes 196612

commit v5 on v4

--- a/solution.py
+++ b/solution.py
@@ -263,56 +263,64 @@
 
 
 def pre_kernel(
-    place_ref, vel_hbm, part_hbm, rate_hbm, high_hbm, low_hbm, inner_hbm, outer_hbm, packed_hbm,
-    vel_ref, part_ref, rate_ref, out_ref, sems,
+    place_ref, vel_hbm, part_hbm, rate_hbm, cell_hbm, high_hbm, low_hbm, inner_hbm, outer_hbm,
+    packed_hbm, vel_ref, cell_ref, part_ref, rate_ref, out_ref, sems,
 ):
     even = place_ref[0] % 2 == 0
+    order = (2, 3, 0, 1)
     into = [
-        pltpu.make_async_copy(vel_hbm.at[:, 2:4], vel_ref.at[:, 2:4], sems.at[0]),
-        pltpu.make_async_copy(vel_hbm.at[:, 0:2], vel_ref.at[:, 0:2], sems.at[1]),
-        pltpu.make_async_copy(part_hbm, part_ref, sems.at[2]),
-        pltpu.make_async_copy(rate_hbm, rate_ref, sems.at[3]),
+        pltpu.make_async_copy(part_hbm, part_ref, sems.at[0]),
+        pltpu.make_async_copy(rate_hbm, rate_ref, sems.at[1]),
     ]
+    layers = [
+        pltpu.make_async_copy(vel_hbm.at[:, x], vel_ref.at[:, x], sems.at[2 + x]) for x in order
+    ]
+    cells = pltpu.make_async_copy(cell_hbm, cell_ref, sems.at[6])
+    for copy in into + layers + [cells]:
+        copy.start()
     for copy in into:
-        copy.start()
-    out = [
-        pltpu.make_async_copy(vel_ref.at[:, 2:4], high_hbm, sems.at[4]),
-        pltpu.make_async_copy(vel_ref.at[:, 0:2], low_hbm, sems.at[5]),
-        pltpu.make_async_copy(vel_ref.at[:, :, ROWS - 2 : ROWS], inner_hbm, sems.at[6]),
-        pltpu.make_async_copy(vel_ref.at[:, :, 0:2], outer_hbm, sems.at[7]),
-        pltpu.make_async_copy(out_ref, packed_hbm, sems.at[8]),
-    ]
-    into[2].wait()
-    into[3].wait()
+        copy.wait()
     left = lax.broadcasted_iota(jnp.int32, (1, 128), 1) < SLOTS
-    for r in range(PEERS // 2):
-        part = [part_ref[i : i + 1, 128 * r : 128 * r + 128] for i in range(3)]
-        part.append(rate_ref[0:1, 128 * r : 128 * r + 128])
-        for n in range(2):
-            one, two = part[2 * n], part[2 * n + 1]
-            out_ref[2 * r, n : n + 1, :] = jnp.where(left, one, pltpu.roll(two, SLOTS, 1))
-            out_ref[2 * r + 1, n : n + 1, :] = jnp.where(left, pltpu.roll(one, SLOTS, 1), two)
-    out[4].start()
-    into[0].wait()
-    out[0].start()
-    into[1].wait()
-    out[1].start()
-
-    @pl.when(even)
-    def _():
-        out[2].start()
-        out[3].start()
-
-    @pl.when(jnp.logical_not(even))
-    def _():
-        pltpu.make_async_copy(vel_ref.at[:, :, 0:2], inner_hbm, sems.at[6]).start()
-        pltpu.make_async_copy(vel_ref.at[:, :, ROWS - 2 : ROWS], outer_hbm, sems.at[7]).start()
-
+
+    def pack(first, last):
+        for r in range(first, last):
+            part = [part_ref[i : i + 1, 128 * r : 128 * r + 128] for i in range(3)]
+            part.append(rate_ref[0:1, 128 * r : 128 * r + 128])
+            for n in range(2):
+                one, two = part[2 * n], part[2 * n + 1]
+                out_ref[2 * r, n : n + 1, :] = jnp.where(left, one, pltpu.roll(two, SLOTS, 1))
+                out_ref[2 * r + 1, n : n + 1, :] = jnp.where(left, pltpu.roll(one, SLOTS, 1), two)
+
+    out = []
+    for n, x in enumerate(order):
+        pack(16 * n, 16 * n + 16)
+        layers[n].wait()
+        target = high_hbm.at[:, x - 2] if x >= 2 else low_hbm.at[:, x]
+        flat = pltpu.make_async_copy(vel_ref.at[:, x], target, sems.at[7 + n])
+        flat.start()
+        out.append(flat)
+        bottom, top = vel_ref.at[:, x, 0:2], vel_ref.at[:, x, ROWS - 2 : ROWS]
+        out.append(pltpu.make_async_copy(top, inner_hbm.at[:, x], sems.at[11 + n]))
+        out.append(pltpu.make_async_copy(bottom, outer_hbm.at[:, x], sems.at[15 + n]))
+
+        @pl.when(even)
+        def _():
+            out[-2].start()
+            out[-1].start()
+
+        @pl.when(jnp.logical_not(even))
+        def _():
+            pltpu.make_async_copy(bottom, inner_hbm.at[:, x], sems.at[11 + n]).start()
+            pltpu.make_async_copy(top, outer_hbm.at[:, x], sems.at[15 + n]).start()
+
+    out.append(pltpu.make_async_copy(out_ref, packed_hbm, sems.at[19]))
+    out[-1].start()
+    cells.wait()
     for copy in out:
         copy.wait()
 
 
-def prepared(place, velocity, part_vel, part_rate):
+def prepared(place, velocity, part_vel, part_rate, cells):
     return pl.pallas_call(
         pre_kernel,
         out_shape=(
@@ -322,18 +330,19 @@
             far_out(3, CX, 2, CZ),
             far_out(PEERS, 2, 128),
             held((3, CX, ROWS, CZ)),
+            held((1, TOTAL), jnp.int32),
         ),
-        in_specs=[SMEM] + [ANY] * 3,
-        out_specs=(ANY,) * 5 + (VMEM,),
+        in_specs=[SMEM] + [ANY] * 4,
+        out_specs=(ANY,) * 5 + (VMEM,) * 2,
         scratch_shapes=[
             pltpu.VMEM((3, TOTAL), F32),
             pltpu.VMEM((1, TOTAL), F32),
             pltpu.VMEM((PEERS, 2, 128), F32),
-            pltpu.SemaphoreType.DMA((9,)),
+            pltpu.SemaphoreType.DMA((20,)),
         ],
         compiler_params=params(16),
         name="prepare",
-    )(place, *far_in(velocity, part_vel, part_rate))
+    )(place, *far_in(velocity, part_vel, part_rate, cells))
 
 
 def halves(cells):
@@ -364,14 +373,13 @@
 
 
 def find_kernel(
-    place_ref, vel_ref, cell_hbm, rate_hbm, *refs,
+    place_ref, vel_ref, cell_ref, rate_hbm, *refs,
 ):
     outs, held_refs = refs[:5], refs[5:10]
     fluid_ref, scale_ref, tip_ref, fix_ref, solve_ref = held_refs
-    bf_ref, table_ref, cell_ref, rate_ref, wide_ref, sems = refs[10:]
+    bf_ref, table_ref, rate_ref, wide_ref, sems = refs[10:]
     copies = [
-        pltpu.make_async_copy(cell_hbm, cell_ref, sems.at[0]),
-        pltpu.make_async_copy(rate_hbm, rate_ref, sems.at[1]),
+        pltpu.make_async_copy(rate_hbm, rate_ref, sems.at[0]),
     ]
     for copy in copies:
         copy.start()
@@ -417,7 +425,7 @@
             far_out(4, ROWS, 128),
             far_out(ROWS, 128),
         ),
-        in_specs=[SMEM, VMEM, ANY, ANY],
+        in_specs=[SMEM, VMEM, VMEM, ANY],
         out_specs=(ANY,) * 5,
         scratch_shapes=[
             pltpu.VMEM((3, TOTAL), F32),
@@ -427,26 +435,24 @@
             pltpu.VMEM((ROWS, 128), F32),
             pltpu.VMEM((3 * PLANES, CZ), BF16),
             pltpu.VMEM((CZ, CHUNK), BF16),
-            pltpu.VMEM((1, TOTAL), jnp.int32),
             pltpu.VMEM((8, 128), F32),
             pltpu.VMEM((ROWS, 128), F32),
             pltpu.SemaphoreType.DMA((6 + TOTAL // CHUNK,)),
         ],
         compiler_params=params(28),
         name="find",
-    )(place, vel_held, *far_in(cells, rate))
+    )(place, vel_held, cells, *far_in(rate))
 
 
 def main_kernel(
-    place_ref, inner_hbm, outer_hbm, before_hbm, behind_hbm, moved_hbm,
-    fluid_hbm, scale_hbm, tip_hbm, vel_hbm, section_hbm, count_hbm, cell_hbm, near_hbm, far_hbm,
+    place_ref, cell_ref, inner_hbm, outer_hbm, before_hbm, behind_hbm, moved_hbm,
+    fluid_hbm, scale_hbm, tip_hbm, vel_hbm, section_hbm, count_hbm, near_hbm, far_hbm,
     part_hbm, tips_hbm, new_ref,
     pad_ref, before_ref, behind_ref, section_ref, table_ref, got_ref, deposit_ref, moved_ref,
-    count_ref, cell_ref, near_ref, far_ref, part_ref, tips_ref, coef_ref,
+    count_ref, near_ref, far_ref, part_ref, tips_ref, coef_ref,
     fluid_ref, scale_ref, tip_ref, sems,
 ):
     sources = [
-        (cell_hbm, cell_ref),
         (moved_hbm, moved_ref),
         (count_hbm, count_ref),
         (fluid_hbm, fluid_ref),
@@ -529,11 +535,15 @@
         for t in range(ROWS // 8):
             top = 8 * t
             here = layer(x, top)
-            ddx = (8.0 / 12.0) * (layer(x + 1, top) - layer(x - 1, top)) - (1.0 / 12.0) * (
+            ddx = (TIME_STEP * 8.0 / 12.0) * (layer(x + 1, top) - layer(x - 1, top)) - (
+                TIME_STEP / 12.0
+            ) * (
                 layer(x + 2, top) - layer(x - 2, top)
             )
             rolled = {k: pltpu.roll(here, (-k) % CZ, 1) for k in (1, -1, 2, -2)}
-            ddz = (8.0 / 12.0) * (rolled[1] - rolled[-1]) - (1.0 / 12.0) * (rolled[2] - rolled[-2])
+            ddz = (TIME_STEP * 8.0 / 12.0) * (rolled[1] - rolled[-1]) - (TIME_STEP / 12.0) * (
+                rolled[2] - rolled[-2]
+            )
 
             def shifted(k):
                 return pad_ref[c, x, 8 + top + k : 16 + top + k, :]
@@ -547,24 +557,28 @@
                 + pad_ref[2, x, 8 + top : 16 + top, :] * ddz
             )
             new_ref[c, x, top : top + 8, :] = (
-                SECTION_KEEP * section_ref[c, x, top : top + 8, :] - TIME_STEP * moved
+                SECTION_KEEP * section_ref[c, x, top : top + 8, :] - moved
             )
 
     planes = [(c, x) for c in range(3) for x in range(CX)]
-    share = len(planes) // (steps - 1)
-    for copy in copies[:4]:
+    share = len(planes) // steps
+    for copy in copies[:3]:
         copy.wait()
     unpack()
     for step in range(steps):
         spread = spread_of(step)
-        if step > 0:
-            for c, x in planes[share * (step - 1) : share * step]:
-                stencil(c, x)
+        if step == 0:
+            for copy in copies[3:]:
+                copy.wait()
+            coef_ref[0] = TIME_STEP * column_of(near_ref[...], ROWS)
+            coef_ref[1] = TIME_STEP * column_of(far_ref[...], ROWS)
+        for c, x in planes[share * step : share * (step + 1)]:
+            stencil(c, x)
         last = step == steps - 1
         if last:
             stores = [pltpu.make_async_copy(part_ref, part_hbm, sems.at[14])]
             stores[0].start()
-        wide = CZ // 4 if last else CZ
+        wide = CZ // 2 if last else CZ
         for z in range(0, CZ, wide):
             new = lax.dot_general(
                 spread, table_ref[z : z + wide, :], (((1,), (1,)), ((), ())),
@@ -590,12 +604,17 @@
                     for r in range(4):
                         weighted = scaled * tiled(tip_ref[r, top : top + 8, :], wide // 128)
                         total[r] = weighted if t == 0 else total[r] + weighted
-                for r in range(4):
-                    summed = jnp.sum(total[r], axis=0, keepdims=True)
+                for r in (0, 2):
+                    one, two = total[r], total[r + 1]
+                    upper = lax.broadcasted_iota(jnp.int32, one.shape, 0) < 4
+                    both = jnp.where(upper, one, two) + pltpu.roll(jnp.where(upper, two, one), 4, 0)
+                    both = both + pltpu.roll(both, 6, 0)
+                    both = both + pltpu.roll(both, 7, 0)
                     for k in range(wide // 128):
-                        tips_ref[8 * x + z // 128 + k, c, r : r + 1, :] = summed[
-                            :, 128 * k : 128 * k + 128
-                        ]
+                        at = 8 * x + z // 128 + k
+                        lanes = slice(128 * k, 128 * k + 128)
+                        tips_ref[at, c, r : r + 1, :] = both[0:1, lanes]
+                        tips_ref[at, c, r + 1 : r + 2, :] = both[4:5, lanes]
             for x in range(CX if last else 0):
                 span = pl.ds(8 * x + z // 128, wide // 128)
                 stores.append(
@@ -604,16 +623,11 @@
                     )
                 )
                 stores[-1].start()
-        if step == 0:
-            for copy in copies[4:]:
-                copy.wait()
-            coef_ref[0] = column_of(near_ref[...], ROWS)
-            coef_ref[1] = column_of(far_ref[...], ROWS)
     for store in stores:
         store.wait()
 
 
-def main_part(place, halos, moved, others):
+def main_part(place, cells, halos, moved, others):
     return pl.pallas_call(
         main_kernel,
         out_shape=(
@@ -621,7 +635,7 @@
             far_out(SLABS, 3, 4, 128),
             held((3, CX, ROWS, CZ)),
         ),
-        in_specs=[SMEM] + [ANY] * 14,
+        in_specs=[SMEM, VMEM] + [ANY] * 13,
         out_specs=(ANY, ANY, VMEM),
         scratch_shapes=[
             pltpu.VMEM((3, CX, ROWS + 16, CZ), F32),
@@ -633,7 +647,6 @@
             pltpu.VMEM((3 * PLANES, CZ), F32),
             pltpu.VMEM((PEERS, 2, 128), F32),
             pltpu.SMEM((1, PEERS), jnp.int32),
-            pltpu.VMEM((1, TOTAL), jnp.int32),
             pltpu.VMEM((1, ROWS), F32),
             pltpu.VMEM((1, ROWS), F32),
             pltpu.VMEM((3, TOTAL), F32),
@@ -646,7 +659,7 @@
         ],
         compiler_params=params(36),
         name="main_part",
-    )(place, *halos, moved, *far_in(*others))
+    )(place, cells, *halos, moved, *far_in(*others))
 
 
 WIDTH = 3 * CX * CZ // SLABS
@@ -748,8 +761,8 @@
     up_x = [(i, (i + 1) % n_gx) for i in range(n_gx)]
     down_x = [(t, s) for s, t in up_x]
     place = lax.axis_index("gy").astype(jnp.int32).reshape(1)
-    high, low, inner, outer, packed, vel_held = prepared(
-        place, velocity, part_vel, part_rate.reshape(1, TOTAL)
+    high, low, inner, outer, packed, vel_held, cells = prepared(
+        place, velocity, part_vel, part_rate.reshape(1, TOTAL), cell_slot
     )
     before = lax.ppermute(high, "gx", up_x)
     behind = lax.ppermute(low, "gx", down_x)
@@ -758,10 +771,10 @@
         outer, "gy", [pair for i in range(1, n_gy - 1, 2) for pair in ((i, i + 1), (i + 1, i))]
     )
     moved = lax.all_to_all(packed, ("gx", "gy"), split_axis=0, concat_axis=0, tiled=True)
-    fluid, scale, tip, fix, solve = find(place, vel_held, cell_slot, diffusion.reshape(8, 128))
+    fluid, scale, tip, fix, solve = find(place, vel_held, cells, diffusion.reshape(8, 128))
     part_new, tips, new_held = main_part(
-        place, (inner, outer, before, behind), moved,
-        (fluid, scale, tip, velocity, section, counts, cell_slot, rhs_near.reshape(1, ROWS), rhs_far.reshape(1, ROWS)),
+        place, cells, (inner, outer, before, behind), moved,
+        (fluid, scale, tip, velocity, section, counts, rhs_near.reshape(1, ROWS), rhs_far.reshape(1, ROWS)),
     )
     tips, diffusion = lax.optimization_barrier((tips, diffusion))
     all_tips = lax.all_to_all(tips, "gy", split_axis=0, concat_axis=0, tiled=True)

time: 70.7 us -> 71.3 us (level)
    pallas_call x1, Pallas kernels: 10.7 us -> 11.9 us  [main_part(): pl.pallas_call(main_kernel, out_shape=(far_out(3, TOTAL), far_out(SLABS,...]
where the time goes in v5:
time: 71.3 us; the launch traced here: 70.9 us
  Pallas kernels  28.8 us (40%)
  starting transfers between devices  28.2 us (40%)
  waiting for transfers between devices  12.8 us (18%)
  between operations  0.97 us (1%)
    pallas_call x1, Pallas kernels, main_part(): pl.pallas_call(main_kernel, out_shape=(far_out(3, TOTAL), far_out(SLABS,...  11.9 us
    all_to_all x1, starting transfers between devices, local(): lax.all_to_all(packed, ('gx', 'gy'), split_axis=0, concat_axis=0, tiled=T...  8.85 us
    pallas_call x1, Pallas kernels, find(): pl.pallas_call(find_kernel, out_shape=(far_out(3, TOTAL), far_out(ROWS, 1...  8.56 us
    all_to_all x1, starting transfers between devices, local(): lax.all_to_all(tips, 'gy', split_axis=0, concat_axis=0, tiled=True)  7.05 us
    all_to_all x1, waiting for transfers between devices, local(): lax.all_to_all(tips, 'gy', split_axis=0, concat_axis=0, tiled=True)  6.85 us
    all_to_all x1, waiting for transfers between devices, local(): edges = lax.all_to_all(reply, 'gy', split_axis=0, concat_axis=0, tiled=True)  5.9 us
    all_to_all x1, starting transfers between devices, local(): edges = lax.all_to_all(reply, 'gy', split_axis=0, concat_axis=0, tiled=True)  3.8 us
    ppermute x1, starting transfers between devices, local(): lax.ppermute(outer, 'gy', [pair for i in range(1, n_gy - 1, 2) for pair i...  2.61 us
  transfers between devices with their start and end apart: 7, of which 2 were waited for; matrix products, arithmetic and copies ran while one was open for 0% of the time, Pallas kernels for 17%

profile of v5, /device:TPU:1, one launch (start us, length us, event | category | flops | bytes accessed | tf_op | source)
XLA Modules:
  0.0 70.9 jit_solution(6265520575356143217)
XLA Ops:
  0.6 2.5 %prepare.1 = (f32[3,2,32,1024]{3,2,1,0:T(8,128)}, f32[3,2,32,1024]{3,2,1,0:T(8,128)}, f32[3,4,2,1024]{3,2,1,0:T(2,128)}, f32[3,4,2,1024]{3,2,1,0:T(2,128)}, f32[...) custom-call(s32[1]{0:T(128)} %bitcast.place_ref, f32[3,4,32,1024]{3,2,1,0:T(8,128)} %vel_hbm.5, ...), custom_call_target="tpu_custom_call" | custom-call | tf_op jit(solution)/shard_map/prepare/pallas_call | solution.py:324
  3.1 2.5 %collective-permute-start.2 = (f32[3,2,32,1024]{3,2,1,0:T(8,128)}, f32[3,2,32,1024]{3,2,1,0:T(8,128)S(1)}, u32[]{:S(2)}, u32[]{:S(2)}) collective-permute-start(f32[3,2,32,1024]{3,2,1,0:T(8,128)} %get-tuple-element.27), channel_id=1, source_target_pairs={{0,32},{32,64},{64,96},{96,0},{1,33},{33,65},{65,97},{97,1},{2,34}... | collective-permute-start | bytes 2359304 | tf_op jit(solution)/shard_map/ppermute | solution.py:767
  5.7 2.2 %collective-permute-start.3 = (f32[3,2,32,1024]{3,2,1,0:T(8,128)}, f32[3,2,32,1024]{3,2,1,0:T(8,128)S(1)}, u32[]{:S(2)}, u32[]{:S(2)}) collective-permute-start(f32[3,2,32,1024]{3,2,1,0:T(8,128)} %get-tuple-element.28), channel_id=1, source_target_pairs={{32,0},{64,32},{96,64},{0,96},{33,1},{65,33},{97,65},{1,97},{34,2}... | collective-permute-start | bytes 2359304 | tf_op jit(solution)/shard_map/ppermute | solution.py:768
  7.9 8.9 %all-to-all-start = ((f32[128,2,128]{2,1,0:T(2,128)}), f32[128,2,128]{2,1,0:T(2,128)S(1)}, u32[]{:S(2)}, u32[]{:S(2)}) async-start(f32[128,2,128]{2,1,0:T(2,128)} %get-tuple-element.29), calls=%async_computation | async-start | bytes 262144 | tf_op jit(solution)/shard_map/all_to_all | solution.py:773
  16.7 1.1 %collective-permute-start = (f32[3,4,2,1024]{3,2,1,0:T(2,128)}, f32[3,4,2,1024]{3,2,1,0:T(2,128)S(1)}, u32[]{:S(2)}, u32[]{:S(2)}) collective-permute-start(f32[3,4,2,1024]{3,2,1,0:T(2,128)} %get-tuple-element.25), channel_id=1, source_target_pairs={{0,1},{1,0},{2,3},{3,2},{4,5},{5,4},{6,7},{7,6},{8,9},{9,8},{10,11... | collective-permute-start | bytes 294920 | tf_op jit(solution)/shard_map/ppermute | solution.py:769
  17.9 2.6 %collective-permute-start.1 = (f32[3,4,2,1024]{3,2,1,0:T(2,128)}, f32[3,4,2,1024]{3,2,1,0:T(2,128)S(1)}, u32[]{:S(2)}, u32[]{:S(2)}) collective-permute-start(f32[3,4,2,1024]{3,2,1,0:T(2,128)} %get-tuple-element.26), channel_id=1, source_target_pairs={{1,2},{2,1},{3,4},{4,3},{5,6},{6,5},{7,8},{8,7},{9,10},{10,9},{11,... | collective-permute-start | bytes 294920 | tf_op jit(solution)/shard_map/ppermute | solution.py:770
  20.5 8.6 %find.1 = (f32[3,8192]{1,0:T(4,128)}, f32[32,128]{1,0:T(8,128)}, f32[4,32,128]{2,1,0:T(8,128)}, f32[4,32,128]{2,1,0:T(8,128)}, f32[32,128]{1,0:T(8,128)}) custom-call(s32[1]{0:T(128)} %bitcast.place_ref, f32[3,4,32,1024]{3,2,1,0:T(8,128)S(1)} %get-tuple-element.30.vel_ref, s32[1,8192]{1,0:T(1,128)S(1)} %get-tuple-element.24.cell_ref, f32[8,128]{1,0:T(8,128)} %bitcast.8), custom_call_target="tpu_custom_call" | custom-call | tf_op jit(solution)/shard_map/find/pallas_call | solution.py:419
  29.1 0.0 collective-permute-done.inner_hbm
  29.1 0.0 collective-permute-done.1.outer_hbm
  29.1 0.0 all-to-all-done.moved_hbm
  29.1 0.0 collective-permute-done.2.before_hbm
  29.1 0.0 collective-permute-done.3.behind_hbm
  29.1 0.0 copy-start.3
  29.1 0.0 copy-start
  29.1 0.0 copy-start.2
  29.2 11.9 %main_part.1 = (f32[3,8192]{1,0:T(4,128)}, f32[32,3,4,128]{3,2,1,0:T(4,128)}, f32[3,4,32,1024]{3,2,1,0:T(8,128)S(1)}) custom-call(s32[1]{0:T(128)} %bitcast.place_ref, s32[1,8192]{1,0:T(1,128)S(1)} %get-tuple-element.24.cell_ref, f32[3,4,2,1024]{3,2,1,0:T(2,128)S(1)} %collective-permute-done.inner_hbm, ...), custom_call_target="tpu_custom_call" | custom-call | tf_op jit(solution)/shard_map/main_part/pallas_call | solution.py:631
  41.1 7.1 %all-to-all-start.1 = ((f32[32,3,4,128]{3,2,1,0:T(4,128)}), f32[32,3,4,128]{3,2,1,0:T(4,128)S(1)}, u32[]{:S(2)}, u32[]{:S(2)}) async-start(f32[32,3,4,128]{3,2,1,0:T(4,128)} %get-tuple-element.36), calls=%async_computation.1 | async-start | bytes 393216 | tf_op jit(solution)/shard_map/all_to_all | solution.py:780
  48.1 0.0 copy-done.3
  48.1 0.1 reshape.29
  48.2 0.1 copy.12
  48.3 1.2 %green_operator.1.green_ref = f32[128,128]{1,0:T(8,128)S(1)} custom-call(f32[32,128]{1,0:T(8,128)S(1)} %pad.4.rate_ref), custom_call_target="tpu_custom_call" | custom-call | tf_op jit(solution)/shard_map/green_operator/pallas_call | solution.py:254
  49.5 6.8 %all-to-all-done.1.tips_ref = f32[32,3,4,128]{3,2,1,0:T(4,128)S(1)} async-done(((f32[32,3,4,128]{3,2,1,0:T(4,128)}), f32[32,3,4,128]{3,2,1,0:T(4,128)S(1)}, u32[]{:S(2)}, u32[]{:S(2)}) %all-to-all-start.1) | async-done | bytes 196640 | tf_op jit(solution)/shard_map/all_to_all | solution.py:780
  56.4 1.0 %solve.1 = f32[32,3,4,128]{3,2,1,0:T(4,128)} custom-call(f32[32,3,4,128]{3,2,1,0:T(4,128)S(1)} %all-to-all-done.1.tips_ref, f32[128,128]{1,0:T(8,128)S(1)} %green_operator.1.green_ref), custom_call_target="tpu_custom_call" | custom-call | tf_op jit(solution)/shard_map/solve/pallas_call | solution.py:679
  57.4 3.8 %all-to-all-start.2 = ((f32[32,3,4,128]{3,2,1,0:T(4,128)}), f32[32,3,4,128]{3,2,1,0:T(4,128)S(1)}, u32[]{:S(2)}, u32[]{:S(2)}) async-start(f32[32,3,4,128]{3,2,1,0:T(4,128)} %solve.1), calls=%async_computation.2 | async-start | bytes 393216 | tf_op jit(solution)/shard_map/all_to_all | solution.py:786
  61.2 0.0 copy-done
  61.2 0.0 copy-done.2
  61.2 0.0 copy-start.1
  61.2 2.3 %local_solve.1 = (f32[3,4,32,1024]{3,2,1,0:T(8,128)}, f32[3,4,32,1024]{3,2,1,0:T(8,128)S(1)}) custom-call(f32[3,4,32,1024]{3,2,1,0:T(8,128)} %vel_hbm.5, f32[3,4,32,1024]{3,2,1,0:T(8,128)S(1)} %get-tuple-element.34.section_ref, f32[32,128]{1,0:T(8,128)S(1)} %copy-done, f32[32,128]{1,0:T(8,128)S(1)} %copy-done.2), custom_call_target="tpu_custom_call" | custom-call | tf_op jit(solution)/shard_map/local_solve/pallas_call | solution.py:713
  63.6 5.9 %all-to-all-done.2.edge_ref = f32[32,3,4,128]{3,2,1,0:T(4,128)S(1)} async-done(((f32[32,3,4,128]{3,2,1,0:T(4,128)}), f32[32,3,4,128]{3,2,1,0:T(4,128)S(1)}, u32[]{:S(2)}, u32[]{:S(2)}) %all-to-all-start.2) | async-done | bytes 196640 | tf_op jit(solution)/shard_map/all_to_all | solution.py:786
  69.5 0.0 copy-done.1
  69.5 1.3 %finish.1 = f32[3,4,32,1024]{3,2,1,0:T(8,128)} custom-call(f32[3,4,32,1024]{3,2,1,0:T(8,128)S(1)} %get-tuple-element.40.partial_ref, f32[32,3,4,128]{3,2,1,0:T(4,128)S(1)} %all-to-all-done.2.edge_ref, f32[4,32,128]{2,1,0:T(8,128)S(1)} %copy-done.1), custom_call_target="tpu_custom_call" | custom-call | tf_op jit(solution)/shard_map/finish/pallas_call | solution.py:748
  (1 shorter events, 0.0 us)
Async XLA Ops:
  3.1 26.0 %collective-permute-start.2 = (f32[3,2,32,1024]{3,2,1,0:T(8,128)}, f32[3,2,32,1024]{3,2,1,0:T(8,128)S(1)}, u32[]{:S(2)}, u32[]{:S(2)}) collective-permute-start(f32[3,2,32,1024]{3,2,1,0:T(8,128)} %get-tuple-element.27), channel_id=1, source_target_pairs={{0,32},{32,64},{64,96},{96,0},{1,33},{33,65},{65,97},{97,1},{2,34}... | collective-permute-start | bytes 2359304 | tf_op jit(solution)/shard_map/ppermute | solution.py:767
  5.7 23.4 %collective-permute-start.3 = (f32[3,2,32,1024]{3,2,1,0:T(8,128)}, f32[3,2,32,1024]{3,2,1,0:T(8,128)S(1)}, u32[]{:S(2)}, u32[]{:S(2)}) collective-permute-start(f32[3,2,32,1024]{3,2,1,0:T(8,128)} %get-tuple-element.28), channel_id=1, source_target_pairs={{32,0},{64,32},{96,64},{0,96},{33,1},{65,33},{97,65},{1,97},{34,2}... | collective-permute-start | bytes 2359304 | tf_op jit(solution)/shard_map/ppermute | solution.py:768
  7.9 21.2 %all-to-all-start = ((f32[128,2,128]{2,1,0:T(2,128)}), f32[128,2,128]{2,1,0:T(2,128)S(1)}, u32[]{:S(2)}, u32[]{:S(2)}) async-start(f32[128,2,128]{2,1,0:T(2,128)} %get-tuple-element.29), calls=%async_computation | async-start | bytes 262144 | tf_op jit(solution)/shard_map/all_to_all | solution.py:773
  16.7 12.3 %collective-permute-start = (f32[3,4,2,1024]{3,2,1,0:T(2,128)}, f32[3,4,2,1024]{3,2,1,0:T(2,128)S(1)}, u32[]{:S(2)}, u32[]{:S(2)}) collective-permute-start(f32[3,4,2,1024]{3,2,1,0:T(2,128)} %get-tuple-element.25), channel_id=1, source_target_pairs={{0,1},{1,0},{2,3},{3,2},{4,5},{5,4},{6,7},{7,6},{8,9},{9,8},{10,11... | collective-permute-start | bytes 294920 | tf_op jit(solution)/shard_map/ppermute | solution.py:769
  17.9 11.2 %collective-permute-start.1 = (f32[3,4,2,1024]{3,2,1,0:T(2,128)}, f32[3,4,2,1024]{3,2,1,0:T(2,128)S(1)}, u32[]{:S(2)}, u32[]{:S(2)}) collective-permute-start(f32[3,4,2,1024]{3,2,1,0:T(2,128)} %get-tuple-element.26), channel_id=1, source_target_pairs={{1,2},{2,1},{3,4},{4,3},{5,6},{6,5},{7,8},{8,7},{9,10},{10,9},{11,... | collective-permute-start | bytes 294920 | tf_op jit(solution)/shard_map/ppermute | solution.py:770
  29.1 19.0 %copy-start.3 = (f32[1024]{0:T(1024)S(1)}, f32[1024]{0:T(1024)}, u32[]{:S(2)}) copy-start(f32[1024]{0:T(1024)} %param.11) | copy-start | bytes 12292
  29.1 32.1 %copy-start = (f32[32,128]{1,0:T(8,128)S(1)}, f32[32,128]{1,0:T(8,128)}, u32[]{:S(2)}) copy-start(f32[32,128]{1,0:T(8,128)} %get-tuple-element.32.scale_hbm.scale_ref) | copy-start | bytes 49156
  29.1 32.1 %copy-start.2 = (f32[32,128]{1,0:T(8,128)S(1)}, f32[32,128]{1,0:T(8,128)}, u32[]{:S(2)}) copy-start(f32[32,128]{1,0:T(8,128)} %get-tuple-element.39.solve_ref) | copy-start | bytes 49156
  41.1 15.3 %all-to-all-start.1 = ((f32[32,3,4,128]{3,2,1,0:T(4,128)}), f32[32,3,4,128]{3,2,1,0:T(4,128)S(1)}, u32[]{:S(2)}, u32[]{:S(2)}) async-start(f32[32,3,4,128]{3,2,1,0:T(4,128)} %get-tuple-element.36), calls=%async_computation.1 | async-start | bytes 393216 | tf_op jit(solution)/shard_map/all_to_all | solution.py:780
  57.4 12.1 %all-to-all-start.2 = ((f32[32,3,4,128]{3,2,1,0:T(4,128)}), f32[32,3,4,128]{3,2,1,0:T(4,128)S(1)}, u32[]{:S(2)}, u32[]{:S(2)}) async-start(f32[32,3,4,128]{3,2,1,0:T(4,128)} %solve.1), calls=%async_computation.2 | async-start | bytes 393216 | tf_op jit(solution)/shard_map/all_to_all | solution.py:786
  61.2 8.2 %copy-start.1 = (f32[4,32,128]{2,1,0:T(8,128)S(1)}, f32[4,32,128]{2,1,0:T(8,128)}, u32[]{:S(2)}) copy-start(f32[4,32,128]{2,1,0:T(8,128)} %get-tuple-element.42.fix_ref) | copy-start | bytes 196612

commit v6 on v5

--- a/solution.py
+++ b/solution.py
@@ -373,29 +373,68 @@
 
 
 def find_kernel(
-    place_ref, vel_ref, cell_ref, rate_hbm, *refs,
+    place_ref, vel_ref, cell_ref, inner_hbm, outer_hbm, rate_hbm, section_hbm, near_hbm, far_hbm, *refs
 ):
-    outs, held_refs = refs[:5], refs[5:10]
-    fluid_ref, scale_ref, tip_ref, fix_ref, solve_ref = held_refs
-    bf_ref, table_ref, rate_ref, wide_ref, sems = refs[10:]
+    outs, held_refs = refs[:6], refs[6:12]
+    fluid_ref, scale_ref, tip_ref, fix_ref, solve_ref, base_ref = held_refs
+    bf_ref, table_ref, rate_ref, wide_ref, pad_ref, section_ref, near_ref, far_ref, coef_ref, sems = (
+        refs[12:]
+    )
+    below, above = pad_ref.at[:, :, 6:8, :], pad_ref.at[:, :, 8 + ROWS : 10 + ROWS, :]
     copies = [
         pltpu.make_async_copy(rate_hbm, rate_ref, sems.at[0]),
+        pltpu.make_async_copy(near_hbm, near_ref, sems.at[1]),
+        pltpu.make_async_copy(far_hbm, far_ref, sems.at[2]),
+        pltpu.make_async_copy(section_hbm, section_ref, sems.at[3]),
+        pltpu.make_async_copy(inner_hbm, below, sems.at[4]),
+        pltpu.make_async_copy(outer_hbm, above, sems.at[5]),
     ]
-    for copy in copies:
+    for copy in copies[:4]:
         copy.start()
+    even = place_ref[0] % 2 == 0
+
+    @pl.when(even)
+    def _():
+        pltpu.make_async_copy(outer_hbm, below, sems.at[4]).start()
+        pltpu.make_async_copy(inner_hbm, above, sems.at[5]).start()
+
+    @pl.when(jnp.logical_not(even))
+    def _():
+        copies[4].start()
+        copies[5].start()
+
     for c in range(3):
         for x in range(CX):
             top = c * PLANES + x * ROWS
             bf_ref[top : top + ROWS, :] = vel_ref[c, x].astype(BF16)
-    for copy in copies:
-        copy.wait()
+    copies[0].wait()
     own_factors(place_ref[0], rate_ref, scale_ref, tip_ref, fix_ref, solve_ref, wide_ref)
-    stores = [
-        pltpu.make_async_copy(held_refs[n], outs[n], sems.at[1 + n]) for n in range(1, 5)
-    ]
+    stores = [pltpu.make_async_copy(held_refs[n], outs[n], sems.at[5 + n]) for n in range(1, 5)]
     for store in stores:
         store.start()
-    for step in range(TOTAL // CHUNK):
+
+    def stencil(c, x):
+        for top in range(0, ROWS, 8):
+            here = vel_ref[c, x, top : top + 8, :]
+            rolled = {k: pltpu.roll(here, (-k) % CZ, 1) for k in (1, -1, 2, -2)}
+            ddz = (TIME_STEP * 8.0 / 12.0) * (rolled[1] - rolled[-1]) - (TIME_STEP / 12.0) * (
+                rolled[2] - rolled[-2]
+            )
+
+            def shifted(k):
+                return pad_ref[c, x, 8 + top + k : 16 + top + k, :]
+
+            near = jnp.concatenate([coef_ref[0, top : top + 8, :]] * 8, axis=1)
+            far = jnp.concatenate([coef_ref[1, top : top + 8, :]] * 8, axis=1)
+            ddy = near * (shifted(1) - shifted(-1)) + far * (shifted(2) - shifted(-2))
+            base_ref[c, x, top : top + 8, :] = SECTION_KEEP * section_ref[c, x, top : top + 8, :] - (
+                vel_ref[1, x, top : top + 8, :] * ddy + vel_ref[2, x, top : top + 8, :] * ddz
+            )
+
+    steps = TOTAL // CHUNK
+    planes = [(c, x) for c in range(3) for x in range(CX)]
+    share = len(planes) // (steps - 1)
+    for step in range(steps):
         lanes = slice(step * CHUNK, (step + 1) * CHUNK)
         plane, high, low = halves(cell_ref[:, lanes])
         table_ref[...] = span_table(high, low)
@@ -407,7 +446,23 @@
             )
         stores.append(
             pltpu.make_async_copy(
-                fluid_ref.at[:, lanes], outs[0].at[:, lanes], sems.at[6 + step]
+                fluid_ref.at[:, lanes], outs[0].at[:, lanes], sems.at[13 + step]
+            )
+        )
+        stores[-1].start()
+        if step == 0:
+            for copy in copies[1:]:
+                copy.wait()
+            coef_ref[0] = TIME_STEP * column_of(near_ref[...], ROWS)
+            coef_ref[1] = TIME_STEP * column_of(far_ref[...], ROWS)
+            for c, x in planes:
+                pad_ref[c, x, 8 : 8 + ROWS, :] = vel_ref[c, x]
+            continue
+        for c, x in planes[share * (step - 1) : share * step]:
+            stencil(c, x)
+        stores.append(
+            pltpu.make_async_copy(
+                base_ref.at[step - 1], outs[5].at[step - 1], sems.at[9 + step]
             )
         )
         stores[-1].start()
@@ -415,7 +470,7 @@
         store.wait()
 
 
-def find(place, vel_held, cells, rate):
+def find(place, vel_held, cells, inner, outer, *others):
     return pl.pallas_call(
         find_kernel,
         out_shape=(
@@ -424,32 +479,39 @@
             far_out(4, ROWS, 128),
             far_out(4, ROWS, 128),
             far_out(ROWS, 128),
+            far_out(3, CX, ROWS, CZ),
         ),
-        in_specs=[SMEM, VMEM, VMEM, ANY],
-        out_specs=(ANY,) * 5,
+        in_specs=[SMEM, VMEM, VMEM] + [ANY] * 6,
+        out_specs=(ANY,) * 6,
         scratch_shapes=[
             pltpu.VMEM((3, TOTAL), F32),
             pltpu.VMEM((ROWS, 128), F32),
             pltpu.VMEM((4, ROWS, 128), F32),
             pltpu.VMEM((4, ROWS, 128), F32),
             pltpu.VMEM((ROWS, 128), F32),
+            pltpu.VMEM((3, CX, ROWS, CZ), F32),
             pltpu.VMEM((3 * PLANES, CZ), BF16),
             pltpu.VMEM((CZ, CHUNK), BF16),
             pltpu.VMEM((8, 128), F32),
             pltpu.VMEM((ROWS, 128), F32),
-            pltpu.SemaphoreType.DMA((6 + TOTAL // CHUNK,)),
+            pltpu.VMEM((3, CX, ROWS + 16, CZ), F32),
+            pltpu.VMEM((3, CX, ROWS, CZ), F32),
+            pltpu.VMEM((1, ROWS), F32),
+            pltpu.VMEM((1, ROWS), F32),
+            pltpu.VMEM((2, ROWS, 128), F32),
+            pltpu.SemaphoreType.DMA((13 + TOTAL // CHUNK,)),
         ],
-        compiler_params=params(28),
+        compiler_params=params(36),
         name="find",
-    )(place, vel_held, cells, *far_in(rate))
+    )(place, vel_held, cells, inner, outer, *far_in(*others))
 
 
 def main_kernel(
-    place_ref, cell_ref, inner_hbm, outer_hbm, before_hbm, behind_hbm, moved_hbm,
-    fluid_hbm, scale_hbm, tip_hbm, vel_hbm, section_hbm, count_hbm, near_hbm, far_hbm,
+    cell_ref, before_hbm, behind_hbm, moved_hbm,
+    fluid_hbm, scale_hbm, tip_hbm, vel_hbm, base_hbm, count_hbm,
     part_hbm, tips_hbm, new_ref,
-    pad_ref, before_ref, behind_ref, section_ref, table_ref, got_ref, deposit_ref, moved_ref,
-    count_ref, near_ref, far_ref, part_ref, tips_ref, coef_ref,
+    vel_ref, before_ref, behind_ref, base_ref, table_ref, got_ref, deposit_ref, moved_ref,
+    count_ref, part_ref, tips_ref,
     fluid_ref, scale_ref, tip_ref, sems,
 ):
     sources = [
@@ -458,32 +520,14 @@
         (fluid_hbm, fluid_ref),
         (scale_hbm, scale_ref),
         (tip_hbm, tip_ref),
-        (near_hbm, near_ref),
-        (far_hbm, far_ref),
-        (vel_hbm, pad_ref.at[:, :, 8 : 8 + ROWS, :]),
-        (inner_hbm, pad_ref.at[:, :, 6:8, :]),
-        (outer_hbm, pad_ref.at[:, :, 8 + ROWS : 10 + ROWS, :]),
+        (vel_hbm, vel_ref),
         (before_hbm, before_ref),
         (behind_hbm, behind_ref),
-        (section_hbm, section_ref),
+        (base_hbm, base_ref),
     ]
     copies = [pltpu.make_async_copy(a, b, sems.at[n]) for n, (a, b) in enumerate(sources)]
-    swaps = [n for n, (a, b) in enumerate(sources) if a is inner_hbm or a is outer_hbm]
-    for n, copy in enumerate(copies):
-        if n not in swaps:
-            copy.start()
-    even = place_ref[0] % 2 == 0
-
-    @pl.when(even)
-    def _():
-        for n, source in zip(swaps, (outer_hbm, inner_hbm)):
-            pltpu.make_async_copy(source, sources[n][1], sems.at[n]).start()
-
-    @pl.when(jnp.logical_not(even))
-    def _():
-        for n in swaps:
-            copies[n].start()
-
+    for copy in copies:
+        copy.start()
     steps = TOTAL // CHUNK
 
     def lanes_of(step):
@@ -530,55 +574,31 @@
                 return before_ref[c, 2 + i, top : top + 8, :]
             if i >= CX:
                 return behind_ref[c, i - CX, top : top + 8, :]
-            return pad_ref[c, i, 8 + top : 16 + top, :]
-
-        for t in range(ROWS // 8):
-            top = 8 * t
-            here = layer(x, top)
+            return vel_ref[c, i, top : top + 8, :]
+
+        for top in range(0, ROWS, 8):
             ddx = (TIME_STEP * 8.0 / 12.0) * (layer(x + 1, top) - layer(x - 1, top)) - (
                 TIME_STEP / 12.0
-            ) * (
-                layer(x + 2, top) - layer(x - 2, top)
+            ) * (layer(x + 2, top) - layer(x - 2, top))
+            new_ref[c, x, top : top + 8, :] = (
+                base_ref[c, x, top : top + 8, :] - vel_ref[0, x, top : top + 8, :] * ddx
             )
-            rolled = {k: pltpu.roll(here, (-k) % CZ, 1) for k in (1, -1, 2, -2)}
-            ddz = (TIME_STEP * 8.0 / 12.0) * (rolled[1] - rolled[-1]) - (TIME_STEP / 12.0) * (
-                rolled[2] - rolled[-2]
-            )
-
-            def shifted(k):
-                return pad_ref[c, x, 8 + top + k : 16 + top + k, :]
-
-            near = tiled(coef_ref[0, top : top + 8, :], 8)
-            far = tiled(coef_ref[1, top : top + 8, :], 8)
-            ddy = near * (shifted(1) - shifted(-1)) + far * (shifted(2) - shifted(-2))
-            moved = (
-                pad_ref[0, x, 8 + top : 16 + top, :] * ddx
-                + pad_ref[1, x, 8 + top : 16 + top, :] * ddy
-                + pad_ref[2, x, 8 + top : 16 + top, :] * ddz
-            )
-            new_ref[c, x, top : top + 8, :] = (
-                SECTION_KEEP * section_ref[c, x, top : top + 8, :] - moved
-            )
 
     planes = [(c, x) for c in range(3) for x in range(CX)]
-    share = len(planes) // steps
+    share = len(planes) // (steps - 1)
     for copy in copies[:3]:
         copy.wait()
     unpack()
     for step in range(steps):
         spread = spread_of(step)
-        if step == 0:
-            for copy in copies[3:]:
-                copy.wait()
-            coef_ref[0] = TIME_STEP * column_of(near_ref[...], ROWS)
-            coef_ref[1] = TIME_STEP * column_of(far_ref[...], ROWS)
-        for c, x in planes[share * step : share * (step + 1)]:
-            stencil(c, x)
+        if step > 0:
+            for c, x in planes[share * (step - 1) : share * step]:
+                stencil(c, x)
         last = step == steps - 1
         if last:
             stores = [pltpu.make_async_copy(part_ref, part_hbm, sems.at[14])]
             stores[0].start()
-        wide = CZ // 2 if last else CZ
+        wide = CZ // 4 if last else CZ
         for z in range(0, CZ, wide):
             new = lax.dot_general(
                 spread, table_ref[z : z + wide, :], (((1,), (1,)), ((), ())),
@@ -623,11 +643,14 @@
                     )
                 )
                 stores[-1].start()
+        if step == 0:
+            for copy in copies[3:]:
+                copy.wait()
     for store in stores:
         store.wait()
 
 
-def main_part(place, cells, halos, moved, others):
+def main_part(cells, halos, moved, others):
     return pl.pallas_call(
         main_kernel,
         out_shape=(
@@ -635,10 +658,10 @@
             far_out(SLABS, 3, 4, 128),
             held((3, CX, ROWS, CZ)),
         ),
-        in_specs=[SMEM, VMEM] + [ANY] * 13,
+        in_specs=[VMEM] + [ANY] * 9,
         out_specs=(ANY, ANY, VMEM),
         scratch_shapes=[
-            pltpu.VMEM((3, CX, ROWS + 16, CZ), F32),
+            pltpu.VMEM((3, CX, ROWS, CZ), F32),
             pltpu.VMEM((3, 2, ROWS, CZ), F32),
             pltpu.VMEM((3, 2, ROWS, CZ), F32),
             pltpu.VMEM((3, CX, ROWS, CZ), F32),
@@ -647,11 +670,8 @@
             pltpu.VMEM((3 * PLANES, CZ), F32),
             pltpu.VMEM((PEERS, 2, 128), F32),
             pltpu.SMEM((1, PEERS), jnp.int32),
-            pltpu.VMEM((1, ROWS), F32),
-            pltpu.VMEM((1, ROWS), F32),
             pltpu.VMEM((3, TOTAL), F32),
             pltpu.VMEM((SLABS, 3, 4, 128), F32),
-            pltpu.VMEM((2, ROWS, 128), F32),
             pltpu.VMEM((3, TOTAL), F32),
             pltpu.VMEM((ROWS, 128), F32),
             pltpu.VMEM((4, ROWS, 128), F32),
@@ -659,7 +679,7 @@
         ],
         compiler_params=params(36),
         name="main_part",
-    )(place, cells, *halos, moved, *far_in(*others))
+    )(cells, *halos, moved, *far_in(*others))
 
 
 WIDTH = 3 * CX * CZ // SLABS
@@ -771,10 +791,12 @@
         outer, "gy", [pair for i in range(1, n_gy - 1, 2) for pair in ((i, i + 1), (i + 1, i))]
     )
     moved = lax.all_to_all(packed, ("gx", "gy"), split_axis=0, concat_axis=0, tiled=True)
-    fluid, scale, tip, fix, solve = find(place, vel_held, cells, diffusion.reshape(8, 128))
+    fluid, scale, tip, fix, solve, base = find(
+        place, vel_held, cells, inner, outer, diffusion.reshape(8, 128), section,
+        rhs_near.reshape(1, ROWS), rhs_far.reshape(1, ROWS),
+    )
     part_new, tips, new_held = main_part(
-        place, cells, (inner, outer, before, behind), moved,
-        (fluid, scale, tip, velocity, section, counts, rhs_near.reshape(1, ROWS), rhs_far.reshape(1, ROWS)),
+        cells, (before, behind), moved, (fluid, scale, tip, velocity, base, counts)
     )
     tips, diffusion = lax.optimization_barrier((tips, diffusion))
     all_tips = lax.all_to_all(tips, "gy", split_axis=0, concat_axis=0, tiled=True)

time: 71.3 us -> 75.8 us (1.063)
  waiting for transfers between devices: 12.8 us -> 16.6 us
  starting transfers between devices: 28.2 us -> 29.1 us
    ppermute x1, waiting for transfers between devices: 0.01 us -> 3.8 us  [local(): lax.ppermute(outer, 'gy', [pair for i in range(1, n_gy - 1, 2) for pair i...]
    pallas_call x1, Pallas kernels: 11.9 us -> 9.88 us  [main_part(): pl.pallas_call(main_kernel, out_shape=(far_out(3, TOTAL), far_out(SLABS,...]
    pallas_call x1, Pallas kernels: 8.56 us -> 10.4 us  [find(): pl.pallas_call(find_kernel, out_shape=(far_out(3, TOTAL), far_out(ROWS, 1...]
    all_to_all x1, starting transfers between devices: 7.05 us -> 7.98 us  [local(): lax.all_to_all(tips, 'gy', split_axis=0, concat_axis=0, tiled=True)]
  transfers between devices with their start and end apart: 7 -> 7, of which waited for: 2 -> 3; matrix products, arithmetic and copies ran while one was open for 0% -> 0% of each run, Pallas kernels for 17% -> 19%
where the time goes in v6:
time: 75.8 us; the launch traced here: 75.5 us
  starting transfers between devices  29.1 us (38%)
  Pallas kernels  28.6 us (38%)
  waiting for transfers between devices  16.6 us (22%)
  between operations  0.96 us (1%)
    pallas_call x1, Pallas kernels, find(): pl.pallas_call(find_kernel, out_shape=(far_out(3, TOTAL), far_out(ROWS, 1...  10.4 us
    pallas_call x1, Pallas kernels, main_part(): pl.pallas_call(main_kernel, out_shape=(far_out(3, TOTAL), far_out(SLABS,...  9.88 us
    all_to_all x1, starting transfers between devices, local(): lax.all_to_all(packed, ('gx', 'gy'), split_axis=0, concat_axis=0, tiled=T...  8.85 us
    all_to_all x1, starting transfers between devices, local(): lax.all_to_all(tips, 'gy', split_axis=0, concat_axis=0, tiled=True)  7.98 us
    all_to_all x1, waiting for transfers between devices, local(): lax.all_to_all(tips, 'gy', split_axis=0, concat_axis=0, tiled=True)  6.85 us
    all_to_all x1, waiting for transfers between devices, local(): edges = lax.all_to_all(reply, 'gy', split_axis=0, concat_axis=0, tiled=True)  5.9 us
    all_to_all x1, starting transfers between devices, local(): edges = lax.all_to_all(reply, 'gy', split_axis=0, concat_axis=0, tiled=True)  3.8 us
    ppermute x1, waiting for transfers between devices, local(): lax.ppermute(outer, 'gy', [pair for i in range(1, n_gy - 1, 2) for pair i...  3.8 us
  transfers between devices with their start and end apart: 7, of which 3 were waited for; matrix products, arithmetic and copies ran while one was open for 0% of the time, Pallas kernels for 19%

profile of v6, /device:TPU:1, one launch (start us, length us, event | category | flops | bytes accessed | tf_op | source)
XLA Modules:
  0.0 75.5 jit_solution(10864354635147152486)
XLA Ops:
  0.6 2.5 %prepare.1 = (f32[3,2,32,1024]{3,2,1,0:T(8,128)}, f32[3,2,32,1024]{3,2,1,0:T(8,128)}, f32[3,4,2,1024]{3,2,1,0:T(2,128)}, f32[3,4,2,1024]{3,2,1,0:T(2,128)}, f32[...) custom-call(s32[1]{0:T(128)} %bitcast.place_ref, f32[3,4,32,1024]{3,2,1,0:T(8,128)} %vel_hbm.5, ...), custom_call_target="tpu_custom_call" | custom-call | tf_op jit(solution)/shard_map/prepare/pallas_call | solution.py:324
  3.1 2.5 %collective-permute-start = (f32[3,2,32,1024]{3,2,1,0:T(8,128)}, f32[3,2,32,1024]{3,2,1,0:T(8,128)S(1)}, u32[]{:S(2)}, u32[]{:S(2)}) collective-permute-start(f32[3,2,32,1024]{3,2,1,0:T(8,128)} %get-tuple-element.26), channel_id=1, source_target_pairs={{0,32},{32,64},{64,96},{96,0},{1,33},{33,65},{65,97},{97,1},{2,34}... | collective-permute-start | bytes 2359304 | tf_op jit(solution)/shard_map/ppermute | solution.py:787
  5.7 2.2 %collective-permute-start.1 = (f32[3,2,32,1024]{3,2,1,0:T(8,128)}, f32[3,2,32,1024]{3,2,1,0:T(8,128)S(1)}, u32[]{:S(2)}, u32[]{:S(2)}) collective-permute-start(f32[3,2,32,1024]{3,2,1,0:T(8,128)} %get-tuple-element.27), channel_id=1, source_target_pairs={{32,0},{64,32},{96,64},{0,96},{33,1},{65,33},{97,65},{1,97},{34,2}... | collective-permute-start | bytes 2359304 | tf_op jit(solution)/shard_map/ppermute | solution.py:788
  7.9 8.9 %all-to-all-start = ((f32[128,2,128]{2,1,0:T(2,128)}), f32[128,2,128]{2,1,0:T(2,128)S(1)}, u32[]{:S(2)}, u32[]{:S(2)}) async-start(f32[128,2,128]{2,1,0:T(2,128)} %get-tuple-element.28), calls=%async_computation | async-start | bytes 262144 | tf_op jit(solution)/shard_map/all_to_all | solution.py:793
  16.7 1.1 %collective-permute-start.2 = (f32[3,4,2,1024]{3,2,1,0:T(2,128)}, f32[3,4,2,1024]{3,2,1,0:T(2,128)S(1)}, u32[]{:S(2)}, u32[]{:S(2)}) collective-permute-start(f32[3,4,2,1024]{3,2,1,0:T(2,128)} %get-tuple-element.30), channel_id=1, source_target_pairs={{0,1},{1,0},{2,3},{3,2},{4,5},{5,4},{6,7},{7,6},{8,9},{9,8},{10,11... | collective-permute-start | bytes 294920 | tf_op jit(solution)/shard_map/ppermute | solution.py:789
  17.9 2.6 %collective-permute-start.3 = (f32[3,4,2,1024]{3,2,1,0:T(2,128)}, f32[3,4,2,1024]{3,2,1,0:T(2,128)S(1)}, u32[]{:S(2)}, u32[]{:S(2)}) collective-permute-start(f32[3,4,2,1024]{3,2,1,0:T(2,128)} %get-tuple-element.31), channel_id=1, source_target_pairs={{1,2},{2,1},{3,4},{4,3},{5,6},{6,5},{7,8},{8,7},{9,10},{10,9},{11,... | collective-permute-start | bytes 294920 | tf_op jit(solution)/shard_map/ppermute | solution.py:790
  20.5 0.0 collective-permute-done.2.inner_hbm
  20.5 3.8 %collective-permute-done.3.outer_hbm = f32[3,4,2,1024]{3,2,1,0:T(2,128)S(1)} collective-permute-done((f32[3,4,2,1024]{3,2,1,0:T(2,128)}, f32[3,4,2,1024]{3,2,1,0:T(2,128)S(1)}, u32[]{:S(2)}, u32[]{:S(2)}) %collective-permute-start.3) | collective-permute-done | bytes 98336 | tf_op jit(solution)/shard_map/ppermute | solution.py:790
  24.3 10.4 %find.1 = (f32[3,8192]{1,0:T(4,128)}, f32[32,128]{1,0:T(8,128)}, f32[4,32,128]{2,1,0:T(8,128)}, f32[4,32,128]{2,1,0:T(8,128)}, f32[32,128]{1,0:T(8,128)}, /*index=5*/f32[3,4,32,1024]{3,2,1,0:T(8,128)}) custom-call(s32[1]{0:T(128)} %bitcast.place_ref, f32[3,4,32,1024]{3,2,1,0:T(8,128)S(1)} %get-tuple-element.29.vel_ref, ...), custom_call_target="tpu_custom_call" | custom-call | tf_op jit(solution)/shard_map/find/pallas_call | solution.py:474
  34.7 0.0 all-to-all-done.moved_hbm
  34.7 0.0 collective-permute-done.before_hbm
  34.7 0.0 collective-permute-done.1.behind_hbm
  34.7 0.0 copy-start.3
  34.8 0.0 copy-start
  34.8 0.0 copy-start.2
  34.8 9.9 %main_part.1 = (f32[3,8192]{1,0:T(4,128)}, f32[32,3,4,128]{3,2,1,0:T(4,128)}, f32[3,4,32,1024]{3,2,1,0:T(8,128)S(1)}) custom-call(s32[1,8192]{1,0:T(1,128)S(1)} %get-tuple-element.25.cell_ref, f32[3,2,32,1024]{3,2,1,0:T(8,128)S(1)} %collective-permute-done.before_hbm, f32[3,2,32,1024]{3,2,1,0:T(8,128)S(1)} %collective-permute-done.1.behind_hbm, ...), custom_call_target="tpu_custom_call" | custom-call | tf_op jit(solution)/shard_map/main_part/pallas_call | solution.py:654
  44.7 8.0 %all-to-all-start.1 = ((f32[32,3,4,128]{3,2,1,0:T(4,128)}), f32[32,3,4,128]{3,2,1,0:T(4,128)S(1)}, u32[]{:S(2)}, u32[]{:S(2)}) async-start(f32[32,3,4,128]{3,2,1,0:T(4,128)} %get-tuple-element.38), calls=%async_computation.1 | async-start | bytes 393216 | tf_op jit(solution)/shard_map/all_to_all | solution.py:802
  52.7 0.0 copy-done.3
  52.7 0.1 reshape.29
  52.7 0.1 copy.12
  52.8 1.2 %green_operator.1.green_ref = f32[128,128]{1,0:T(8,128)S(1)} custom-call(f32[32,128]{1,0:T(8,128)S(1)} %pad.4.rate_ref), custom_call_target="tpu_custom_call" | custom-call | tf_op jit(solution)/shard_map/green_operator/pallas_call | solution.py:254
  54.1 6.8 %all-to-all-done.1.tips_ref = f32[32,3,4,128]{3,2,1,0:T(4,128)S(1)} async-done(((f32[32,3,4,128]{3,2,1,0:T(4,128)}), f32[32,3,4,128]{3,2,1,0:T(4,128)S(1)}, u32[]{:S(2)}, u32[]{:S(2)}) %all-to-all-start.1) | async-done | bytes 196640 | tf_op jit(solution)/shard_map/all_to_all | solution.py:802
  60.9 1.0 %solve.1 = f32[32,3,4,128]{3,2,1,0:T(4,128)} custom-call(f32[32,3,4,128]{3,2,1,0:T(4,128)S(1)} %all-to-all-done.1.tips_ref, f32[128,128]{1,0:T(8,128)S(1)} %green_operator.1.green_ref), custom_call_target="tpu_custom_call" | custom-call | tf_op jit(solution)/shard_map/solve/pallas_call | solution.py:699
  62.0 3.8 %all-to-all-start.2 = ((f32[32,3,4,128]{3,2,1,0:T(4,128)}), f32[32,3,4,128]{3,2,1,0:T(4,128)S(1)}, u32[]{:S(2)}, u32[]{:S(2)}) async-start(f32[32,3,4,128]{3,2,1,0:T(4,128)} %solve.1), calls=%async_computation.2 | async-start | bytes 393216 | tf_op jit(solution)/shard_map/all_to_all | solution.py:808
  65.8 0.0 copy-done
  65.8 0.0 copy-done.2
  65.8 0.0 copy-start.1
  65.8 2.3 %local_solve.1 = (f32[3,4,32,1024]{3,2,1,0:T(8,128)}, f32[3,4,32,1024]{3,2,1,0:T(8,128)S(1)}) custom-call(f32[3,4,32,1024]{3,2,1,0:T(8,128)} %vel_hbm.5, f32[3,4,32,1024]{3,2,1,0:T(8,128)S(1)} %get-tuple-element.36.section_ref, f32[32,128]{1,0:T(8,128)S(1)} %copy-done, f32[32,128]{1,0:T(8,128)S(1)} %copy-done.2), custom_call_target="tpu_custom_call" | custom-call | tf_op jit(solution)/shard_map/local_solve/pallas_call | solution.py:733
  68.1 5.9 %all-to-all-done.2.edge_ref = f32[32,3,4,128]{3,2,1,0:T(4,128)S(1)} async-done(((f32[32,3,4,128]{3,2,1,0:T(4,128)}), f32[32,3,4,128]{3,2,1,0:T(4,128)S(1)}, u32[]{:S(2)}, u32[]{:S(2)}) %all-to-all-start.2) | async-done | bytes 196640 | tf_op jit(solution)/shard_map/all_to_all | solution.py:808
  74.0 0.0 copy-done.1
  74.0 1.3 %finish.1 = f32[3,4,32,1024]{3,2,1,0:T(8,128)} custom-call(f32[3,4,32,1024]{3,2,1,0:T(8,128)S(1)} %get-tuple-element.42.partial_ref, f32[32,3,4,128]{3,2,1,0:T(4,128)S(1)} %all-to-all-done.2.edge_ref, f32[4,32,128]{2,1,0:T(8,128)S(1)} %copy-done.1), custom_call_target="tpu_custom_call" | custom-call | tf_op jit(solution)/shard_map/finish/pallas_call | solution.py:768
  (1 shorter events, 0.0 us)
Async XLA Ops:
  3.1 31.6 %collective-permute-start = (f32[3,2,32,1024]{3,2,1,0:T(8,128)}, f32[3,2,32,1024]{3,2,1,0:T(8,128)S(1)}, u32[]{:S(2)}, u32[]{:S(2)}) collective-permute-start(f32[3,2,32,1024]{3,2,1,0:T(8,128)} %get-tuple-element.26), channel_id=1, source_target_pairs={{0,32},{32,64},{64,96},{96,0},{1,33},{33,65},{65,97},{97,1},{2,34}... | collective-permute-start | bytes 2359304 | tf_op jit(solution)/shard_map/ppermute | solution.py:787
  5.7 29.1 %collective-permute-start.1 = (f32[3,2,32,1024]{3,2,1,0:T(8,128)}, f32[3,2,32,1024]{3,2,1,0:T(8,128)S(1)}, u32[]{:S(2)}, u32[]{:S(2)}) collective-permute-start(f32[3,2,32,1024]{3,2,1,0:T(8,128)} %get-tuple-element.27), channel_id=1, source_target_pairs={{32,0},{64,32},{96,64},{0,96},{33,1},{65,33},{97,65},{1,97},{34,2}... | collective-permute-start | bytes 2359304 | tf_op jit(solution)/shard_map/ppermute | solution.py:788
  7.9 26.8 %all-to-all-start = ((f32[128,2,128]{2,1,0:T(2,128)}), f32[128,2,128]{2,1,0:T(2,128)S(1)}, u32[]{:S(2)}, u32[]{:S(2)}) async-start(f32[128,2,128]{2,1,0:T(2,128)} %get-tuple-element.28), calls=%async_computation | async-start | bytes 262144 | tf_op jit(solution)/shard_map/all_to_all | solution.py:793
  16.7 3.8 %collective-permute-start.2 = (f32[3,4,2,1024]{3,2,1,0:T(2,128)}, f32[3,4,2,1024]{3,2,1,0:T(2,128)S(1)}, u32[]{:S(2)}, u32[]{:S(2)}) collective-permute-start(f32[3,4,2,1024]{3,2,1,0:T(2,128)} %get-tuple-element.30), channel_id=1, source_target_pairs={{0,1},{1,0},{2,3},{3,2},{4,5},{5,4},{6,7},{7,6},{8,9},{9,8},{10,11... | collective-permute-start | bytes 294920 | tf_op jit(solution)/shard_map/ppermute | solution.py:789
  17.9 6.4 %collective-permute-start.3 = (f32[3,4,2,1024]{3,2,1,0:T(2,128)}, f32[3,4,2,1024]{3,2,1,0:T(2,128)S(1)}, u32[]{:S(2)}, u32[]{:S(2)}) collective-permute-start(f32[3,4,2,1024]{3,2,1,0:T(2,128)} %get-tuple-element.31), channel_id=1, source_target_pairs={{1,2},{2,1},{3,4},{4,3},{5,6},{6,5},{7,8},{8,7},{9,10},{10,9},{11,... | collective-permute-start | bytes 294920 | tf_op jit(solution)/shard_map/ppermute | solution.py:790
  34.7 17.9 %copy-start.3 = (f32[1024]{0:T(1024)S(1)}, f32[1024]{0:T(1024)}, u32[]{:S(2)}) copy-start(f32[1024]{0:T(1024)} %param.11) | copy-start | bytes 12292
  34.8 31.0 %copy-start = (f32[32,128]{1,0:T(8,128)S(1)}, f32[32,128]{1,0:T(8,128)}, u32[]{:S(2)}) copy-start(f32[32,128]{1,0:T(8,128)} %get-tuple-element.33.scale_hbm.scale_ref) | copy-start | bytes 49156
  34.8 31.0 %copy-start.2 = (f32[32,128]{1,0:T(8,128)S(1)}, f32[32,128]{1,0:T(8,128)}, u32[]{:S(2)}) copy-start(f32[32,128]{1,0:T(8,128)} %get-tuple-element.41.solve_ref) | copy-start | bytes 49156
  44.7 16.3 %all-to-all-start.1 = ((f32[32,3,4,128]{3,2,1,0:T(4,128)}), f32[32,3,4,128]{3,2,1,0:T(4,128)S(1)}, u32[]{:S(2)}, u32[]{:S(2)}) async-start(f32[32,3,4,128]{3,2,1,0:T(4,128)} %get-tuple-element.38), calls=%async_computation.1 | async-start | bytes 393216 | tf_op jit(solution)/shard_map/all_to_all | solution.py:802
  62.0 12.1 %all-to-all-start.2 = ((f32[32,3,4,128]{3,2,1,0:T(4,128)}), f32[32,3,4,128]{3,2,1,0:T(4,128)S(1)}, u32[]{:S(2)}, u32[]{:S(2)}) async-start(f32[32,3,4,128]{3,2,1,0:T(4,128)} %solve.1), calls=%async_computation.2 | async-start | bytes 393216 | tf_op jit(solution)/shard_map/all_to_all | solution.py:808
  65.8 8.2 %copy-start.1 = (f32[4,32,128]{2,1,0:T(8,128)S(1)}, f32[4,32,128]{2,1,0:T(8,128)}, u32[]{:S(2)}) copy-start(f32[4,32,128]{2,1,0:T(8,128)} %get-tuple-element.44.fix_ref) | copy-start | bytes 196612

commit v7 on v5

--- a/solution.py
+++ b/solution.py
@@ -561,24 +561,20 @@
             )
 
     planes = [(c, x) for c in range(3) for x in range(CX)]
-    share = len(planes) // steps
+    share = len(planes) // (steps - 1)
     for copy in copies[:3]:
         copy.wait()
     unpack()
     for step in range(steps):
         spread = spread_of(step)
-        if step == 0:
-            for copy in copies[3:]:
-                copy.wait()
-            coef_ref[0] = TIME_STEP * column_of(near_ref[...], ROWS)
-            coef_ref[1] = TIME_STEP * column_of(far_ref[...], ROWS)
-        for c, x in planes[share * step : share * (step + 1)]:
-            stencil(c, x)
+        if step > 0:
+            for c, x in planes[share * (step - 1) : share * step]:
+                stencil(c, x)
         last = step == steps - 1
         if last:
             stores = [pltpu.make_async_copy(part_ref, part_hbm, sems.at[14])]
             stores[0].start()
-        wide = CZ // 2 if last else CZ
+        wide = CZ // 4 if last else CZ
         for z in range(0, CZ, wide):
             new = lax.dot_general(
                 spread, table_ref[z : z + wide, :], (((1,), (1,)), ((), ())),
@@ -623,6 +619,11 @@
                     )
                 )
                 stores[-1].start()
+        if step == 0:
+            for copy in copies[3:]:
+                copy.wait()
+            coef_ref[0] = TIME_STEP * column_of(near_ref[...], ROWS)
+            coef_ref[1] = TIME_STEP * column_of(far_ref[...], ROWS)
     for store in stores:
         store.wait()
 

time: 71.3 us -> 70.2 us (0.985)
  Pallas kernels: 28.8 us -> 27.8 us
    pallas_call x1, Pallas kernels: 11.9 us -> 10.8 us  [main_part(): pl.pallas_call(main_kernel, out_shape=(far_out(3, TOTAL), far_out(SLABS,...]
where the time goes in v7:
time: 70.2 us; the launch traced here: 69.8 us
  starting transfers between devices  28.2 us (40%)
  Pallas kernels  27.8 us (40%)
  waiting for transfers between devices  12.8 us (18%)
  between operations  0.97 us (1%)
    pallas_call x1, Pallas kernels, main_part(): pl.pallas_call(main_kernel, out_shape=(far_out(3, TOTAL), far_out(SLABS,...  10.8 us
    all_to_all x1, starting transfers between devices, local(): lax.all_to_all(packed, ('gx', 'gy'), split_axis=0, concat_axis=0, tiled=T...  8.85 us
    pallas_call x1, Pallas kernels, find(): pl.pallas_call(find_kernel, out_shape=(far_out(3, TOTAL), far_out(ROWS, 1...  8.56 us
    all_to_all x1, starting transfers between devices, local(): lax.all_to_all(tips, 'gy', split_axis=0, concat_axis=0, tiled=True)  7.05 us
    all_to_all x1, waiting for transfers between devices, local(): lax.all_to_all(tips, 'gy', split_axis=0, concat_axis=0, tiled=True)  6.85 us
    all_to_all x1, waiting for transfers between devices, local(): edges = lax.all_to_all(reply, 'gy', split_axis=0, concat_axis=0, tiled=True)  5.9 us
    all_to_all x1, starting transfers between devices, local(): edges = lax.all_to_all(reply, 'gy', split_axis=0, concat_axis=0, tiled=True)  3.8 us
    ppermute x1, starting transfers between devices, local(): lax.ppermute(outer, 'gy', [pair for i in range(1, n_gy - 1, 2) for pair i...  2.61 us
  transfers between devices with their start and end apart: 7, of which 2 were waited for; matrix products, arithmetic and copies ran while one was open for 0% of the time, Pallas kernels for 17%

profile of v7, /device:TPU:1, one launch (start us, length us, event | category | flops | bytes accessed | tf_op | source)
XLA Modules:
  0.0 69.8 jit_solution(15471418943130027648)
XLA Ops:
  0.6 2.5 %prepare.1 = (f32[3,2,32,1024]{3,2,1,0:T(8,128)}, f32[3,2,32,1024]{3,2,1,0:T(8,128)}, f32[3,4,2,1024]{3,2,1,0:T(2,128)}, f32[3,4,2,1024]{3,2,1,0:T(2,128)}, f32[...) custom-call(s32[1]{0:T(128)} %bitcast.place_ref, f32[3,4,32,1024]{3,2,1,0:T(8,128)} %vel_hbm.5, ...), custom_call_target="tpu_custom_call" | custom-call | tf_op jit(solution)/shard_map/prepare/pallas_call | solution.py:324
  3.1 2.5 %collective-permute-start.2 = (f32[3,2,32,1024]{3,2,1,0:T(8,128)}, f32[3,2,32,1024]{3,2,1,0:T(8,128)S(1)}, u32[]{:S(2)}, u32[]{:S(2)}) collective-permute-start(f32[3,2,32,1024]{3,2,1,0:T(8,128)} %get-tuple-element.27), channel_id=1, source_target_pairs={{0,32},{32,64},{64,96},{96,0},{1,33},{33,65},{65,97},{97,1},{2,34}... | collective-permute-start | bytes 2359304 | tf_op jit(solution)/shard_map/ppermute | solution.py:768
  5.7 2.2 %collective-permute-start.3 = (f32[3,2,32,1024]{3,2,1,0:T(8,128)}, f32[3,2,32,1024]{3,2,1,0:T(8,128)S(1)}, u32[]{:S(2)}, u32[]{:S(2)}) collective-permute-start(f32[3,2,32,1024]{3,2,1,0:T(8,128)} %get-tuple-element.28), channel_id=1, source_target_pairs={{32,0},{64,32},{96,64},{0,96},{33,1},{65,33},{97,65},{1,97},{34,2}... | collective-permute-start | bytes 2359304 | tf_op jit(solution)/shard_map/ppermute | solution.py:769
  7.9 8.9 %all-to-all-start = ((f32[128,2,128]{2,1,0:T(2,128)}), f32[128,2,128]{2,1,0:T(2,128)S(1)}, u32[]{:S(2)}, u32[]{:S(2)}) async-start(f32[128,2,128]{2,1,0:T(2,128)} %get-tuple-element.29), calls=%async_computation | async-start | bytes 262144 | tf_op jit(solution)/shard_map/all_to_all | solution.py:774
  16.7 1.1 %collective-permute-start = (f32[3,4,2,1024]{3,2,1,0:T(2,128)}, f32[3,4,2,1024]{3,2,1,0:T(2,128)S(1)}, u32[]{:S(2)}, u32[]{:S(2)}) collective-permute-start(f32[3,4,2,1024]{3,2,1,0:T(2,128)} %get-tuple-element.25), channel_id=1, source_target_pairs={{0,1},{1,0},{2,3},{3,2},{4,5},{5,4},{6,7},{7,6},{8,9},{9,8},{10,11... | collective-permute-start | bytes 294920 | tf_op jit(solution)/shard_map/ppermute | solution.py:770
  17.9 2.6 %collective-permute-start.1 = (f32[3,4,2,1024]{3,2,1,0:T(2,128)}, f32[3,4,2,1024]{3,2,1,0:T(2,128)S(1)}, u32[]{:S(2)}, u32[]{:S(2)}) collective-permute-start(f32[3,4,2,1024]{3,2,1,0:T(2,128)} %get-tuple-element.26), channel_id=1, source_target_pairs={{1,2},{2,1},{3,4},{4,3},{5,6},{6,5},{7,8},{8,7},{9,10},{10,9},{11,... | collective-permute-start | bytes 294920 | tf_op jit(solution)/shard_map/ppermute | solution.py:771
  20.5 8.6 %find.1 = (f32[3,8192]{1,0:T(4,128)}, f32[32,128]{1,0:T(8,128)}, f32[4,32,128]{2,1,0:T(8,128)}, f32[4,32,128]{2,1,0:T(8,128)}, f32[32,128]{1,0:T(8,128)}) custom-call(s32[1]{0:T(128)} %bitcast.place_ref, f32[3,4,32,1024]{3,2,1,0:T(8,128)S(1)} %get-tuple-element.30.vel_ref, s32[1,8192]{1,0:T(1,128)S(1)} %get-tuple-element.24.cell_ref, f32[8,128]{1,0:T(8,128)} %bitcast.8), custom_call_target="tpu_custom_call" | custom-call | tf_op jit(solution)/shard_map/find/pallas_call | solution.py:419
  29.1 0.0 collective-permute-done.inner_hbm
  29.1 0.0 collective-permute-done.1.outer_hbm
  29.1 0.0 all-to-all-done.moved_hbm
  29.1 0.0 collective-permute-done.2.before_hbm
  29.1 0.0 collective-permute-done.3.behind_hbm
  29.1 0.0 copy-start.3
  29.1 0.0 copy-start
  29.1 0.0 copy-start.2
  29.2 10.8 %main_part.1 = (f32[3,8192]{1,0:T(4,128)}, f32[32,3,4,128]{3,2,1,0:T(4,128)}, f32[3,4,32,1024]{3,2,1,0:T(8,128)S(1)}) custom-call(s32[1]{0:T(128)} %bitcast.place_ref, s32[1,8192]{1,0:T(1,128)S(1)} %get-tuple-element.24.cell_ref, f32[3,4,2,1024]{3,2,1,0:T(2,128)S(1)} %collective-permute-done.inner_hbm, ...), custom_call_target="tpu_custom_call" | custom-call | tf_op jit(solution)/shard_map/main_part/pallas_call | solution.py:632
  40.0 7.0 %all-to-all-start.1 = ((f32[32,3,4,128]{3,2,1,0:T(4,128)}), f32[32,3,4,128]{3,2,1,0:T(4,128)S(1)}, u32[]{:S(2)}, u32[]{:S(2)}) async-start(f32[32,3,4,128]{3,2,1,0:T(4,128)} %get-tuple-element.36), calls=%async_computation.1 | async-start | bytes 393216 | tf_op jit(solution)/shard_map/all_to_all | solution.py:781
  47.0 0.0 copy-done.3
  47.1 0.1 reshape.29
  47.1 0.1 copy.12
  47.2 1.2 %green_operator.1.green_ref = f32[128,128]{1,0:T(8,128)S(1)} custom-call(f32[32,128]{1,0:T(8,128)S(1)} %pad.4.rate_ref), custom_call_target="tpu_custom_call" | custom-call | tf_op jit(solution)/shard_map/green_operator/pallas_call | solution.py:254
  48.5 6.8 %all-to-all-done.1.tips_ref = f32[32,3,4,128]{3,2,1,0:T(4,128)S(1)} async-done(((f32[32,3,4,128]{3,2,1,0:T(4,128)}), f32[32,3,4,128]{3,2,1,0:T(4,128)S(1)}, u32[]{:S(2)}, u32[]{:S(2)}) %all-to-all-start.1) | async-done | bytes 196640 | tf_op jit(solution)/shard_map/all_to_all | solution.py:781
  55.3 1.0 %solve.1 = f32[32,3,4,128]{3,2,1,0:T(4,128)} custom-call(f32[32,3,4,128]{3,2,1,0:T(4,128)S(1)} %all-to-all-done.1.tips_ref, f32[128,128]{1,0:T(8,128)S(1)} %green_operator.1.green_ref), custom_call_target="tpu_custom_call" | custom-call | tf_op jit(solution)/shard_map/solve/pallas_call | solution.py:680
  56.3 3.8 %all-to-all-start.2 = ((f32[32,3,4,128]{3,2,1,0:T(4,128)}), f32[32,3,4,128]{3,2,1,0:T(4,128)S(1)}, u32[]{:S(2)}, u32[]{:S(2)}) async-start(f32[32,3,4,128]{3,2,1,0:T(4,128)} %solve.1), calls=%async_computation.2 | async-start | bytes 393216 | tf_op jit(solution)/shard_map/all_to_all | solution.py:787
  60.1 0.0 copy-done
  60.2 0.0 copy-done.2
  60.2 0.0 copy-start.1
  60.2 2.3 %local_solve.1 = (f32[3,4,32,1024]{3,2,1,0:T(8,128)}, f32[3,4,32,1024]{3,2,1,0:T(8,128)S(1)}) custom-call(f32[3,4,32,1024]{3,2,1,0:T(8,128)} %vel_hbm.5, f32[3,4,32,1024]{3,2,1,0:T(8,128)S(1)} %get-tuple-element.34.section_ref, f32[32,128]{1,0:T(8,128)S(1)} %copy-done, f32[32,128]{1,0:T(8,128)S(1)} %copy-done.2), custom_call_target="tpu_custom_call" | custom-call | tf_op jit(solution)/shard_map/local_solve/pallas_call | solution.py:714
  62.5 5.9 %all-to-all-done.2.edge_ref = f32[32,3,4,128]{3,2,1,0:T(4,128)S(1)} async-done(((f32[32,3,4,128]{3,2,1,0:T(4,128)}), f32[32,3,4,128]{3,2,1,0:T(4,128)S(1)}, u32[]{:S(2)}, u32[]{:S(2)}) %all-to-all-start.2) | async-done | bytes 196640 | tf_op jit(solution)/shard_map/all_to_all | solution.py:787
  68.4 0.0 copy-done.1
  68.4 1.3 %finish.1 = f32[3,4,32,1024]{3,2,1,0:T(8,128)} custom-call(f32[3,4,32,1024]{3,2,1,0:T(8,128)S(1)} %get-tuple-element.40.partial_ref, f32[32,3,4,128]{3,2,1,0:T(4,128)S(1)} %all-to-all-done.2.edge_ref, f32[4,32,128]{2,1,0:T(8,128)S(1)} %copy-done.1), custom_call_target="tpu_custom_call" | custom-call | tf_op jit(solution)/shard_map/finish/pallas_call | solution.py:749
  (1 shorter events, 0.0 us)
Async XLA Ops:
  3.1 26.0 %collective-permute-start.2 = (f32[3,2,32,1024]{3,2,1,0:T(8,128)}, f32[3,2,32,1024]{3,2,1,0:T(8,128)S(1)}, u32[]{:S(2)}, u32[]{:S(2)}) collective-permute-start(f32[3,2,32,1024]{3,2,1,0:T(8,128)} %get-tuple-element.27), channel_id=1, source_target_pairs={{0,32},{32,64},{64,96},{96,0},{1,33},{33,65},{65,97},{97,1},{2,34}... | collective-permute-start | bytes 2359304 | tf_op jit(solution)/shard_map/ppermute | solution.py:768
  5.7 23.4 %collective-permute-start.3 = (f32[3,2,32,1024]{3,2,1,0:T(8,128)}, f32[3,2,32,1024]{3,2,1,0:T(8,128)S(1)}, u32[]{:S(2)}, u32[]{:S(2)}) collective-permute-start(f32[3,2,32,1024]{3,2,1,0:T(8,128)} %get-tuple-element.28), channel_id=1, source_target_pairs={{32,0},{64,32},{96,64},{0,96},{33,1},{65,33},{97,65},{1,97},{34,2}... | collective-permute-start | bytes 2359304 | tf_op jit(solution)/shard_map/ppermute | solution.py:769
  7.9 21.2 %all-to-all-start = ((f32[128,2,128]{2,1,0:T(2,128)}), f32[128,2,128]{2,1,0:T(2,128)S(1)}, u32[]{:S(2)}, u32[]{:S(2)}) async-start(f32[128,2,128]{2,1,0:T(2,128)} %get-tuple-element.29), calls=%async_computation | async-start | bytes 262144 | tf_op jit(solution)/shard_map/all_to_all | solution.py:774
  16.7 12.3 %collective-permute-start = (f32[3,4,2,1024]{3,2,1,0:T(2,128)}, f32[3,4,2,1024]{3,2,1,0:T(2,128)S(1)}, u32[]{:S(2)}, u32[]{:S(2)}) collective-permute-start(f32[3,4,2,1024]{3,2,1,0:T(2,128)} %get-tuple-element.25), channel_id=1, source_target_pairs={{0,1},{1,0},{2,3},{3,2},{4,5},{5,4},{6,7},{7,6},{8,9},{9,8},{10,11... | collective-permute-start | bytes 294920 | tf_op jit(solution)/shard_map/ppermute | solution.py:770
  17.9 11.2 %collective-permute-start.1 = (f32[3,4,2,1024]{3,2,1,0:T(2,128)}, f32[3,4,2,1024]{3,2,1,0:T(2,128)S(1)}, u32[]{:S(2)}, u32[]{:S(2)}) collective-permute-start(f32[3,4,2,1024]{3,2,1,0:T(2,128)} %get-tuple-element.26), channel_id=1, source_target_pairs={{1,2},{2,1},{3,4},{4,3},{5,6},{6,5},{7,8},{8,7},{9,10},{10,9},{11,... | collective-permute-start | bytes 294920 | tf_op jit(solution)/shard_map/ppermute | solution.py:771
  29.1 17.9 %copy-start.3 = (f32[1024]{0:T(1024)S(1)}, f32[1024]{0:T(1024)}, u32[]{:S(2)}) copy-start(f32[1024]{0:T(1024)} %param.11) | copy-start | bytes 12292
  29.1 31.0 %copy-start = (f32[32,128]{1,0:T(8,128)S(1)}, f32[32,128]{1,0:T(8,128)}, u32[]{:S(2)}) copy-start(f32[32,128]{1,0:T(8,128)} %get-tuple-element.32.scale_hbm.scale_ref) | copy-start | bytes 49156
  29.1 31.0 %copy-start.2 = (f32[32,128]{1,0:T(8,128)S(1)}, f32[32,128]{1,0:T(8,128)}, u32[]{:S(2)}) copy-start(f32[32,128]{1,0:T(8,128)} %get-tuple-element.39.solve_ref) | copy-start | bytes 49156
  40.0 15.3 %all-to-all-start.1 = ((f32[32,3,4,128]{3,2,1,0:T(4,128)}), f32[32,3,4,128]{3,2,1,0:T(4,128)S(1)}, u32[]{:S(2)}, u32[]{:S(2)}) async-start(f32[32,3,4,128]{3,2,1,0:T(4,128)} %get-tuple-element.36), calls=%async_computation.1 | async-start | bytes 393216 | tf_op jit(solution)/shard_map/all_to_all | solution.py:781
  56.3 12.1 %all-to-all-start.2 = ((f32[32,3,4,128]{3,2,1,0:T(4,128)}), f32[32,3,4,128]{3,2,1,0:T(4,128)S(1)}, u32[]{:S(2)}, u32[]{:S(2)}) async-start(f32[32,3,4,128]{3,2,1,0:T(4,128)} %solve.1), calls=%async_computation.2 | async-start | bytes 393216 | tf_op jit(solution)/shard_map/all_to_all | solution.py:787
  60.2 8.2 %copy-start.1 = (f32[4,32,128]{2,1,0:T(8,128)S(1)}, f32[4,32,128]{2,1,0:T(8,128)}, u32[]{:S(2)}) copy-start(f32[4,32,128]{2,1,0:T(8,128)} %get-tuple-element.42.fix_ref) | copy-start | bytes 196612

commit v8 on v4

--- a/solution.py
+++ b/solution.py
@@ -263,51 +263,61 @@
 
 
 def pre_kernel(
-    place_ref, vel_hbm, part_hbm, rate_hbm, high_hbm, low_hbm, inner_hbm, outer_hbm, packed_hbm,
-    vel_ref, part_ref, rate_ref, out_ref, sems,
+    place_ref, vel_hbm, part_hbm, rate_hbm, high_hbm, low_hbm, inner_hbm, outer_hbm,
+    packed_hbm, bf_ref, vel_ref, part_ref, rate_ref, out_ref, sems,
 ):
     even = place_ref[0] % 2 == 0
+    order = (2, 3, 0, 1)
     into = [
-        pltpu.make_async_copy(vel_hbm.at[:, 2:4], vel_ref.at[:, 2:4], sems.at[0]),
-        pltpu.make_async_copy(vel_hbm.at[:, 0:2], vel_ref.at[:, 0:2], sems.at[1]),
-        pltpu.make_async_copy(part_hbm, part_ref, sems.at[2]),
-        pltpu.make_async_copy(rate_hbm, rate_ref, sems.at[3]),
+        pltpu.make_async_copy(part_hbm, part_ref, sems.at[0]),
+        pltpu.make_async_copy(rate_hbm, rate_ref, sems.at[1]),
     ]
+    layers = [
+        pltpu.make_async_copy(vel_hbm.at[:, x], vel_ref.at[:, x], sems.at[2 + x]) for x in order
+    ]
+    for copy in into + layers:
+        copy.start()
     for copy in into:
-        copy.start()
-    out = [
-        pltpu.make_async_copy(vel_ref.at[:, 2:4], high_hbm, sems.at[4]),
-        pltpu.make_async_copy(vel_ref.at[:, 0:2], low_hbm, sems.at[5]),
-        pltpu.make_async_copy(vel_ref.at[:, :, ROWS - 2 : ROWS], inner_hbm, sems.at[6]),
-        pltpu.make_async_copy(vel_ref.at[:, :, 0:2], outer_hbm, sems.at[7]),
-        pltpu.make_async_copy(out_ref, packed_hbm, sems.at[8]),
-    ]
-    into[2].wait()
-    into[3].wait()
+        copy.wait()
     left = lax.broadcasted_iota(jnp.int32, (1, 128), 1) < SLOTS
-    for r in range(PEERS // 2):
-        part = [part_ref[i : i + 1, 128 * r : 128 * r + 128] for i in range(3)]
-        part.append(rate_ref[0:1, 128 * r : 128 * r + 128])
-        for n in range(2):
-            one, two = part[2 * n], part[2 * n + 1]
-            out_ref[2 * r, n : n + 1, :] = jnp.where(left, one, pltpu.roll(two, SLOTS, 1))
-            out_ref[2 * r + 1, n : n + 1, :] = jnp.where(left, pltpu.roll(one, SLOTS, 1), two)
-    out[4].start()
-    into[0].wait()
-    out[0].start()
-    into[1].wait()
-    out[1].start()
-
-    @pl.when(even)
-    def _():
-        out[2].start()
-        out[3].start()
-
-    @pl.when(jnp.logical_not(even))
-    def _():
-        pltpu.make_async_copy(vel_ref.at[:, :, 0:2], inner_hbm, sems.at[6]).start()
-        pltpu.make_async_copy(vel_ref.at[:, :, ROWS - 2 : ROWS], outer_hbm, sems.at[7]).start()
-
+
+    def pack(first, last):
+        for r in range(first, last):
+            part = [part_ref[i : i + 1, 128 * r : 128 * r + 128] for i in range(3)]
+            part.append(rate_ref[0:1, 128 * r : 128 * r + 128])
+            for n in range(2):
+                one, two = part[2 * n], part[2 * n + 1]
+                out_ref[2 * r, n : n + 1, :] = jnp.where(left, one, pltpu.roll(two, SLOTS, 1))
+                out_ref[2 * r + 1, n : n + 1, :] = jnp.where(left, pltpu.roll(one, SLOTS, 1), two)
+
+    out = []
+    for n, x in enumerate(order):
+        pack(16 * n, 16 * n + 16)
+        layers[n].wait()
+        target = high_hbm.at[:, x - 2] if x >= 2 else low_hbm.at[:, x]
+        flat = pltpu.make_async_copy(vel_ref.at[:, x], target, sems.at[7 + n])
+        flat.start()
+        out.append(flat)
+        bottom, top = vel_ref.at[:, x, 0:2], vel_ref.at[:, x, ROWS - 2 : ROWS]
+        out.append(pltpu.make_async_copy(top, inner_hbm.at[:, x], sems.at[11 + n]))
+        out.append(pltpu.make_async_copy(bottom, outer_hbm.at[:, x], sems.at[15 + n]))
+
+        @pl.when(even)
+        def _():
+            out[-2].start()
+            out[-1].start()
+
+        @pl.when(jnp.logical_not(even))
+        def _():
+            pltpu.make_async_copy(bottom, inner_hbm.at[:, x], sems.at[11 + n]).start()
+            pltpu.make_async_copy(top, outer_hbm.at[:, x], sems.at[15 + n]).start()
+
+    out.append(pltpu.make_async_copy(out_ref, packed_hbm, sems.at[19]))
+    out[-1].start()
+    for c in range(3):
+        for x in range(CX):
+            span = c * PLANES + x * ROWS
+            bf_ref[span : span + ROWS, :] = vel_ref[c, x].astype(BF16)
     for copy in out:
         copy.wait()
 
@@ -321,15 +331,16 @@
             far_out(3, CX, 2, CZ),
             far_out(3, CX, 2, CZ),
             far_out(PEERS, 2, 128),
-            held((3, CX, ROWS, CZ)),
+            held((3 * PLANES, CZ), BF16),
         ),
         in_specs=[SMEM] + [ANY] * 3,
         out_specs=(ANY,) * 5 + (VMEM,),
         scratch_shapes=[
+            pltpu.VMEM((3, CX, ROWS, CZ), F32),
             pltpu.VMEM((3, TOTAL), F32),
             pltpu.VMEM((1, TOTAL), F32),
             pltpu.VMEM((PEERS, 2, 128), F32),
-            pltpu.SemaphoreType.DMA((9,)),
+            pltpu.SemaphoreType.DMA((20,)),
         ],
         compiler_params=params(16),
         name="prepare",
@@ -364,21 +375,17 @@
 
 
 def find_kernel(
-    place_ref, vel_ref, cell_hbm, rate_hbm, *refs,
+    place_ref, bf_ref, cell_hbm, rate_hbm, *refs,
 ):
     outs, held_refs = refs[:5], refs[5:10]
     fluid_ref, scale_ref, tip_ref, fix_ref, solve_ref = held_refs
-    bf_ref, table_ref, cell_ref, rate_ref, wide_ref, sems = refs[10:]
+    table_ref, cell_ref, rate_ref, wide_ref, sems = refs[10:]
     copies = [
         pltpu.make_async_copy(cell_hbm, cell_ref, sems.at[0]),
         pltpu.make_async_copy(rate_hbm, rate_ref, sems.at[1]),
     ]
     for copy in copies:
         copy.start()
-    for c in range(3):
-        for x in range(CX):
-            top = c * PLANES + x * ROWS
-            bf_ref[top : top + ROWS, :] = vel_ref[c, x].astype(BF16)
     for copy in copies:
         copy.wait()
     own_factors(place_ref[0], rate_ref, scale_ref, tip_ref, fix_ref, solve_ref, wide_ref)
@@ -425,7 +432,6 @@
             pltpu.VMEM((4, ROWS, 128), F32),
             pltpu.VMEM((4, ROWS, 128), F32),
             pltpu.VMEM((ROWS, 128), F32),
-            pltpu.VMEM((3 * PLANES, CZ), BF16),
             pltpu.VMEM((CZ, CHUNK), BF16),
             pltpu.VMEM((1, TOTAL), jnp.int32),
             pltpu.VMEM((8, 128), F32),

time: 70.7 us -> 70.1 us (level)
  no operation moved by 1% of the time
where the time goes in v8:
time: 70.1 us; the launch traced here: 69.7 us
  starting transfers between devices  28.2 us (40%)
  Pallas kernels  27.6 us (39%)
  waiting for transfers between devices  12.8 us (18%)
  between operations  0.97 us (1%)
    pallas_call x1, Pallas kernels, main_part(): pl.pallas_call(main_kernel, out_shape=(far_out(3, TOTAL), far_out(SLABS,...  10.7 us
    all_to_all x1, starting transfers between devices, local(): lax.all_to_all(packed, ('gx', 'gy'), split_axis=0, concat_axis=0, tiled=T...  8.85 us
    pallas_call x1, Pallas kernels, find(): pl.pallas_call(find_kernel, out_shape=(far_out(3, TOTAL), far_out(ROWS, 1...  8.6 us
    all_to_all x1, starting transfers between devices, local(): lax.all_to_all(tips, 'gy', split_axis=0, concat_axis=0, tiled=True)  7.01 us
    all_to_all x1, waiting for transfers between devices, local(): lax.all_to_all(tips, 'gy', split_axis=0, concat_axis=0, tiled=True)  6.85 us
    all_to_all x1, waiting for transfers between devices, local(): edges = lax.all_to_all(reply, 'gy', split_axis=0, concat_axis=0, tiled=True)  5.9 us
    all_to_all x1, starting transfers between devices, local(): edges = lax.all_to_all(reply, 'gy', split_axis=0, concat_axis=0, tiled=True)  3.8 us
    ppermute x1, starting transfers between devices, local(): lax.ppermute(outer, 'gy', [pair for i in range(1, n_gy - 1, 2) for pair i...  2.61 us
  transfers between devices with their start and end apart: 7, of which 2 were waited for; matrix products, arithmetic and copies ran while one was open for 0% of the time, Pallas kernels for 17%

profile of v8, /device:TPU:1, one launch (start us, length us, event | category | flops | bytes accessed | tf_op | source)
XLA Modules:
  0.0 69.7 jit_solution(10101732779193028530)
XLA Ops:
  0.6 2.5 %prepare.1 = (f32[3,2,32,1024]{3,2,1,0:T(8,128)}, f32[3,2,32,1024]{3,2,1,0:T(8,128)}, f32[3,4,2,1024]{3,2,1,0:T(2,128)}, f32[3,4,2,1024]{3,2,1,0:T(2,128)}, f32[...) custom-call(s32[1]{0:T(128)} %bitcast.place_ref, f32[3,4,32,1024]{3,2,1,0:T(8,128)} %vel_hbm.5, f32[3,8192]{1,0:T(4,128)} %part_hbm.1, ...), custom_call_target="tpu_custom_call" | custom-call | tf_op jit(solution)/shard_map/prepare/pallas_call | solution.py:326
  3.1 2.5 %collective-permute-start.2 = (f32[3,2,32,1024]{3,2,1,0:T(8,128)}, f32[3,2,32,1024]{3,2,1,0:T(8,128)S(1)}, u32[]{:S(2)}, u32[]{:S(2)}) collective-permute-start(f32[3,2,32,1024]{3,2,1,0:T(8,128)} %get-tuple-element.25), channel_id=1, source_target_pairs={{0,32},{32,64},{64,96},{96,0},{1,33},{33,65},{65,97},{97,1},{2,34}... | collective-permute-start | bytes 2359304 | tf_op jit(solution)/shard_map/ppermute | solution.py:760
  5.7 2.2 %collective-permute-start.3 = (f32[3,2,32,1024]{3,2,1,0:T(8,128)}, f32[3,2,32,1024]{3,2,1,0:T(8,128)S(1)}, u32[]{:S(2)}, u32[]{:S(2)}) collective-permute-start(f32[3,2,32,1024]{3,2,1,0:T(8,128)} %get-tuple-element.26), channel_id=1, source_target_pairs={{32,0},{64,32},{96,64},{0,96},{33,1},{65,33},{97,65},{1,97},{34,2}... | collective-permute-start | bytes 2359304 | tf_op jit(solution)/shard_map/ppermute | solution.py:761
  7.9 8.9 %all-to-all-start = ((f32[128,2,128]{2,1,0:T(2,128)}), f32[128,2,128]{2,1,0:T(2,128)S(1)}, u32[]{:S(2)}, u32[]{:S(2)}) async-start(f32[128,2,128]{2,1,0:T(2,128)} %get-tuple-element.27), calls=%async_computation | async-start | bytes 262144 | tf_op jit(solution)/shard_map/all_to_all | solution.py:766
  16.7 1.1 %collective-permute-start = (f32[3,4,2,1024]{3,2,1,0:T(2,128)}, f32[3,4,2,1024]{3,2,1,0:T(2,128)S(1)}, u32[]{:S(2)}, u32[]{:S(2)}) collective-permute-start(f32[3,4,2,1024]{3,2,1,0:T(2,128)} %get-tuple-element.23), channel_id=1, source_target_pairs={{0,1},{1,0},{2,3},{3,2},{4,5},{5,4},{6,7},{7,6},{8,9},{9,8},{10,11... | collective-permute-start | bytes 294920 | tf_op jit(solution)/shard_map/ppermute | solution.py:762
  17.9 2.6 %collective-permute-start.1 = (f32[3,4,2,1024]{3,2,1,0:T(2,128)}, f32[3,4,2,1024]{3,2,1,0:T(2,128)S(1)}, u32[]{:S(2)}, u32[]{:S(2)}) collective-permute-start(f32[3,4,2,1024]{3,2,1,0:T(2,128)} %get-tuple-element.24), channel_id=1, source_target_pairs={{1,2},{2,1},{3,4},{4,3},{5,6},{6,5},{7,8},{8,7},{9,10},{10,9},{11,... | collective-permute-start | bytes 294920 | tf_op jit(solution)/shard_map/ppermute | solution.py:763
  20.5 8.6 %find.1 = (f32[3,8192]{1,0:T(4,128)}, f32[32,128]{1,0:T(8,128)}, f32[4,32,128]{2,1,0:T(8,128)}, f32[4,32,128]{2,1,0:T(8,128)}, f32[32,128]{1,0:T(8,128)}) custom-call(s32[1]{0:T(128)} %bitcast.place_ref, bf16[384,1024]{1,0:T(8,128)(2,1)S(1)} %get-tuple-element.28.bf_ref, s32[1,8192]{1,0:T(1,128)} %cell_hbm.3, f32[8,128]{1,0:T(8,128)} %bitcast.8), custom_call_target="tpu_custom_call" | custom-call | tf_op jit(solution)/shard_map/find/pallas_call | solution.py:418
  29.1 0.0 collective-permute-done.inner_hbm
  29.1 0.0 collective-permute-done.1.outer_hbm
  29.1 0.0 all-to-all-done.moved_hbm
  29.1 0.0 collective-permute-done.2.before_hbm
  29.2 0.0 collective-permute-done.3.behind_hbm
  29.2 0.0 copy-start.3
  29.2 0.0 copy-start
  29.2 0.0 copy-start.2
  29.2 10.7 %main_part.1 = (f32[3,8192]{1,0:T(4,128)}, f32[32,3,4,128]{3,2,1,0:T(4,128)}, f32[3,4,32,1024]{3,2,1,0:T(8,128)S(1)}) custom-call(s32[1]{0:T(128)} %bitcast.place_ref, f32[3,4,2,1024]{3,2,1,0:T(2,128)S(1)} %collective-permute-done.inner_hbm, f32[3,4,2,1024]{3,2,1,0:T(2,128)S(1)} %collective-permute-done.1.outer_hbm, ...), custom_call_target="tpu_custom_call" | custom-call | tf_op jit(solution)/shard_map/main_part/pallas_call | solution.py:623
  39.9 7.0 %all-to-all-start.1 = ((f32[32,3,4,128]{3,2,1,0:T(4,128)}), f32[32,3,4,128]{3,2,1,0:T(4,128)S(1)}, u32[]{:S(2)}, u32[]{:S(2)}) async-start(f32[32,3,4,128]{3,2,1,0:T(4,128)} %get-tuple-element.34), calls=%async_computation.1 | async-start | bytes 393216 | tf_op jit(solution)/shard_map/all_to_all | solution.py:773
  46.9 0.0 copy-done.3
  46.9 0.1 reshape.29
  47.0 0.1 copy.12
  47.1 1.2 %green_operator.1.green_ref = f32[128,128]{1,0:T(8,128)S(1)} custom-call(f32[32,128]{1,0:T(8,128)S(1)} %pad.4.rate_ref), custom_call_target="tpu_custom_call" | custom-call | tf_op jit(solution)/shard_map/green_operator/pallas_call | solution.py:254
  48.3 6.8 %all-to-all-done.1.tips_ref = f32[32,3,4,128]{3,2,1,0:T(4,128)S(1)} async-done(((f32[32,3,4,128]{3,2,1,0:T(4,128)}), f32[32,3,4,128]{3,2,1,0:T(4,128)S(1)}, u32[]{:S(2)}, u32[]{:S(2)}) %all-to-all-start.1) | async-done | bytes 196640 | tf_op jit(solution)/shard_map/all_to_all | solution.py:773
  55.2 1.0 %solve.1 = f32[32,3,4,128]{3,2,1,0:T(4,128)} custom-call(f32[32,3,4,128]{3,2,1,0:T(4,128)S(1)} %all-to-all-done.1.tips_ref, f32[128,128]{1,0:T(8,128)S(1)} %green_operator.1.green_ref), custom_call_target="tpu_custom_call" | custom-call | tf_op jit(solution)/shard_map/solve/pallas_call | solution.py:672
  56.2 3.8 %all-to-all-start.2 = ((f32[32,3,4,128]{3,2,1,0:T(4,128)}), f32[32,3,4,128]{3,2,1,0:T(4,128)S(1)}, u32[]{:S(2)}, u32[]{:S(2)}) async-start(f32[32,3,4,128]{3,2,1,0:T(4,128)} %solve.1), calls=%async_computation.2 | async-start | bytes 393216 | tf_op jit(solution)/shard_map/all_to_all | solution.py:779
  60.0 0.0 copy-done
  60.0 0.0 copy-done.2
  60.0 0.0 copy-start.1
  60.0 2.3 %local_solve.1 = (f32[3,4,32,1024]{3,2,1,0:T(8,128)}, f32[3,4,32,1024]{3,2,1,0:T(8,128)S(1)}) custom-call(f32[3,4,32,1024]{3,2,1,0:T(8,128)} %vel_hbm.5, f32[3,4,32,1024]{3,2,1,0:T(8,128)S(1)} %get-tuple-element.32.section_ref, f32[32,128]{1,0:T(8,128)S(1)} %copy-done, f32[32,128]{1,0:T(8,128)S(1)} %copy-done.2), custom_call_target="tpu_custom_call" | custom-call | tf_op jit(solution)/shard_map/local_solve/pallas_call | solution.py:706
  62.4 5.9 %all-to-all-done.2.edge_ref = f32[32,3,4,128]{3,2,1,0:T(4,128)S(1)} async-done(((f32[32,3,4,128]{3,2,1,0:T(4,128)}), f32[32,3,4,128]{3,2,1,0:T(4,128)S(1)}, u32[]{:S(2)}, u32[]{:S(2)}) %all-to-all-start.2) | async-done | bytes 196640 | tf_op jit(solution)/shard_map/all_to_all | solution.py:779
  68.3 0.0 copy-done.1
  68.3 1.3 %finish.1 = f32[3,4,32,1024]{3,2,1,0:T(8,128)} custom-call(f32[3,4,32,1024]{3,2,1,0:T(8,128)S(1)} %get-tuple-element.38.partial_ref, f32[32,3,4,128]{3,2,1,0:T(4,128)S(1)} %all-to-all-done.2.edge_ref, f32[4,32,128]{2,1,0:T(8,128)S(1)} %copy-done.1), custom_call_target="tpu_custom_call" | custom-call | tf_op jit(solution)/shard_map/finish/pallas_call | solution.py:741
  (1 shorter events, 0.0 us)
Async XLA Ops:
  3.1 26.0 %collective-permute-start.2 = (f32[3,2,32,1024]{3,2,1,0:T(8,128)}, f32[3,2,32,1024]{3,2,1,0:T(8,128)S(1)}, u32[]{:S(2)}, u32[]{:S(2)}) collective-permute-start(f32[3,2,32,1024]{3,2,1,0:T(8,128)} %get-tuple-element.25), channel_id=1, source_target_pairs={{0,32},{32,64},{64,96},{96,0},{1,33},{33,65},{65,97},{97,1},{2,34}... | collective-permute-start | bytes 2359304 | tf_op jit(solution)/shard_map/ppermute | solution.py:760
  5.7 23.5 %collective-permute-start.3 = (f32[3,2,32,1024]{3,2,1,0:T(8,128)}, f32[3,2,32,1024]{3,2,1,0:T(8,128)S(1)}, u32[]{:S(2)}, u32[]{:S(2)}) collective-permute-start(f32[3,2,32,1024]{3,2,1,0:T(8,128)} %get-tuple-element.26), channel_id=1, source_target_pairs={{32,0},{64,32},{96,64},{0,96},{33,1},{65,33},{97,65},{1,97},{34,2}... | collective-permute-start | bytes 2359304 | tf_op jit(solution)/shard_map/ppermute | solution.py:761
  7.9 21.3 %all-to-all-start = ((f32[128,2,128]{2,1,0:T(2,128)}), f32[128,2,128]{2,1,0:T(2,128)S(1)}, u32[]{:S(2)}, u32[]{:S(2)}) async-start(f32[128,2,128]{2,1,0:T(2,128)} %get-tuple-element.27), calls=%async_computation | async-start | bytes 262144 | tf_op jit(solution)/shard_map/all_to_all | solution.py:766
  16.7 12.4 %collective-permute-start = (f32[3,4,2,1024]{3,2,1,0:T(2,128)}, f32[3,4,2,1024]{3,2,1,0:T(2,128)S(1)}, u32[]{:S(2)}, u32[]{:S(2)}) collective-permute-start(f32[3,4,2,1024]{3,2,1,0:T(2,128)} %get-tuple-element.23), channel_id=1, source_target_pairs={{0,1},{1,0},{2,3},{3,2},{4,5},{5,4},{6,7},{7,6},{8,9},{9,8},{10,11... | collective-permute-start | bytes 294920 | tf_op jit(solution)/shard_map/ppermute | solution.py:762
  17.9 11.2 %collective-permute-start.1 = (f32[3,4,2,1024]{3,2,1,0:T(2,128)}, f32[3,4,2,1024]{3,2,1,0:T(2,128)S(1)}, u32[]{:S(2)}, u32[]{:S(2)}) collective-permute-start(f32[3,4,2,1024]{3,2,1,0:T(2,128)} %get-tuple-element.24), channel_id=1, source_target_pairs={{1,2},{2,1},{3,4},{4,3},{5,6},{6,5},{7,8},{8,7},{9,10},{10,9},{11,... | collective-permute-start | bytes 294920 | tf_op jit(solution)/shard_map/ppermute | solution.py:763
  29.2 17.7 %copy-start.3 = (f32[1024]{0:T(1024)S(1)}, f32[1024]{0:T(1024)}, u32[]{:S(2)}) copy-start(f32[1024]{0:T(1024)} %param.11) | copy-start | bytes 12292
  29.2 30.8 %copy-start = (f32[32,128]{1,0:T(8,128)S(1)}, f32[32,128]{1,0:T(8,128)}, u32[]{:S(2)}) copy-start(f32[32,128]{1,0:T(8,128)} %get-tuple-element.30.scale_hbm.scale_ref) | copy-start | bytes 49156
  29.2 30.8 %copy-start.2 = (f32[32,128]{1,0:T(8,128)S(1)}, f32[32,128]{1,0:T(8,128)}, u32[]{:S(2)}) copy-start(f32[32,128]{1,0:T(8,128)} %get-tuple-element.37.solve_ref) | copy-start | bytes 49156
  39.9 15.3 %all-to-all-start.1 = ((f32[32,3,4,128]{3,2,1,0:T(4,128)}), f32[32,3,4,128]{3,2,1,0:T(4,128)S(1)}, u32[]{:S(2)}, u32[]{:S(2)}) async-start(f32[32,3,4,128]{3,2,1,0:T(4,128)} %get-tuple-element.34), calls=%async_computation.1 | async-start | bytes 393216 | tf_op jit(solution)/shard_map/all_to_all | solution.py:773
  56.2 12.1 %all-to-all-start.2 = ((f32[32,3,4,128]{3,2,1,0:T(4,128)}), f32[32,3,4,128]{3,2,1,0:T(4,128)S(1)}, u32[]{:S(2)}, u32[]{:S(2)}) async-start(f32[32,3,4,128]{3,2,1,0:T(4,128)} %solve.1), calls=%async_computation.2 | async-start | bytes 393216 | tf_op jit(solution)/shard_map/all_to_all | solution.py:779
  60.0 8.2 %copy-start.1 = (f32[4,32,128]{2,1,0:T(8,128)S(1)}, f32[4,32,128]{2,1,0:T(8,128)}, u32[]{:S(2)}) copy-start(f32[4,32,128]{2,1,0:T(8,128)} %get-tuple-element.40.fix_ref) | copy-start | bytes 196612

commit v9 on v8

--- a/solution.py
+++ b/solution.py
@@ -386,19 +386,19 @@
     ]
     for copy in copies:
         copy.start()
-    for copy in copies:
-        copy.wait()
+    copies[1].wait()
     own_factors(place_ref[0], rate_ref, scale_ref, tip_ref, fix_ref, solve_ref, wide_ref)
     stores = [
         pltpu.make_async_copy(held_refs[n], outs[n], sems.at[1 + n]) for n in range(1, 5)
     ]
     for store in stores:
         store.start()
+    copies[0].wait()
     for step in range(TOTAL // CHUNK):
         lanes = slice(step * CHUNK, (step + 1) * CHUNK)
         plane, high, low = halves(cell_ref[:, lanes])
-        table_ref[...] = span_table(high, low)
-        at = jnp.dot(bf_ref[...], table_ref[...], preferred_element_type=F32)
+        table_ref[step % 2] = span_table(high, low)
+        at = jnp.dot(bf_ref[...], table_ref[step % 2], preferred_element_type=F32)
         mask = lax.broadcasted_iota(jnp.int32, (PLANES, CHUNK), 0) == plane
         for n in range(3):
             fluid_ref[n : n + 1, lanes] = jnp.sum(
@@ -432,7 +432,7 @@
             pltpu.VMEM((4, ROWS, 128), F32),
             pltpu.VMEM((4, ROWS, 128), F32),
             pltpu.VMEM((ROWS, 128), F32),
-            pltpu.VMEM((CZ, CHUNK), BF16),
+            pltpu.VMEM((2, CZ, CHUNK), BF16),
             pltpu.VMEM((1, TOTAL), jnp.int32),
             pltpu.VMEM((8, 128), F32),
             pltpu.VMEM((ROWS, 128), F32),
@@ -492,7 +492,7 @@
     def spread_of(step):
         lanes = lanes_of(step)
         plane, high, low = halves(cell_ref[:, lanes])
-        table_ref[...] = span_table(high, low)
+        table_ref[step % 2] = span_table(high, low)
         mask = lax.broadcasted_iota(jnp.int32, (PLANES, CHUNK), 0) == plane
         mask = mask.astype(F32).astype(BF16)
         live = got_ref[4:5, lanes] > 0.5
@@ -573,7 +573,7 @@
         wide = CZ // 4 if last else CZ
         for z in range(0, CZ, wide):
             new = lax.dot_general(
-                spread, table_ref[z : z + wide, :], (((1,), (1,)), ((), ())),
+                spread, table_ref[step % 2, z : z + wide, :], (((1,), (1,)), ((), ())),
                 preferred_element_type=F32,
             )
             if step == 0:
@@ -634,7 +634,7 @@
             pltpu.VMEM((3, 2, ROWS, CZ), F32),
             pltpu.VMEM((3, 2, ROWS, CZ), F32),
             pltpu.VMEM((3, CX, ROWS, CZ), F32),
-            pltpu.VMEM((CZ, CHUNK), BF16),
+            pltpu.VMEM((2, CZ, CHUNK), BF16),
             pltpu.VMEM((8, TOTAL), F32),
             pltpu.VMEM((3 * PLANES, CZ), F32),
             pltpu.VMEM((PEERS, 2, 128), F32),

time: 70.1 us -> 70.4 us (level)
  transfers between devices with their start and end apart: 7 -> 7, of which waited for: 2 -> 2; matrix products, arithmetic and copies ran while one was open for 0% -> 0% of each run, Pallas kernels for 17% -> 18%
where the time goes in v9:
time: 70.4 us; the launch traced here: 70 us
  Pallas kernels  28.2 us (40%)
  starting transfers between devices  27.8 us (39%)
  waiting for transfers between devices  12.8 us (18%)
  between operations  0.97 us (1%)
    pallas_call x1, Pallas kernels, main_part(): pl.pallas_call(main_kernel, out_shape=(far_out(3, TOTAL), far_out(SLABS,...  10.7 us
    pallas_call x1, Pallas kernels, find(): pl.pallas_call(find_kernel, out_shape=(far_out(3, TOTAL), far_out(ROWS, 1...  9.21 us
    all_to_all x1, starting transfers between devices, local(): lax.all_to_all(packed, ('gx', 'gy'), split_axis=0, concat_axis=0, tiled=T...  8.85 us
    all_to_all x1, waiting for transfers between devices, local(): lax.all_to_all(tips, 'gy', split_axis=0, concat_axis=0, tiled=True)  6.85 us
    all_to_all x1, starting transfers between devices, local(): lax.all_to_all(tips, 'gy', split_axis=0, concat_axis=0, tiled=True)  6.7 us
    all_to_all x1, waiting for transfers between devices, local(): edges = lax.all_to_all(reply, 'gy', split_axis=0, concat_axis=0, tiled=True)  5.9 us
    all_to_all x1, starting transfers between devices, local(): edges = lax.all_to_all(reply, 'gy', split_axis=0, concat_axis=0, tiled=True)  3.8 us
    ppermute x1, starting transfers between devices, local(): lax.ppermute(outer, 'gy', [pair for i in range(1, n_gy - 1, 2) for pair i...  2.61 us
  transfers between devices with their start and end apart: 7, of which 2 were waited for; matrix products, arithmetic and copies ran while one was open for 0% of the time, Pallas kernels for 18%

profile of v9, /device:TPU:1, one launch (start us, length us, event | category | flops | bytes accessed | tf_op | source)
XLA Modules:
  0.0 70.0 jit_solution(148548805339102776)
XLA Ops:
  0.6 2.5 %prepare.1 = (f32[3,2,32,1024]{3,2,1,0:T(8,128)}, f32[3,2,32,1024]{3,2,1,0:T(8,128)}, f32[3,4,2,1024]{3,2,1,0:T(2,128)}, f32[3,4,2,1024]{3,2,1,0:T(2,128)}, f32[...) custom-call(s32[1]{0:T(128)} %bitcast.place_ref, f32[3,4,32,1024]{3,2,1,0:T(8,128)} %vel_hbm.5, f32[3,8192]{1,0:T(4,128)} %part_hbm.1, ...), custom_call_target="tpu_custom_call" | custom-call | tf_op jit(solution)/shard_map/prepare/pallas_call | solution.py:326
  3.1 2.5 %collective-permute-start.2 = (f32[3,2,32,1024]{3,2,1,0:T(8,128)}, f32[3,2,32,1024]{3,2,1,0:T(8,128)S(1)}, u32[]{:S(2)}, u32[]{:S(2)}) collective-permute-start(f32[3,2,32,1024]{3,2,1,0:T(8,128)} %get-tuple-element.25), channel_id=1, source_target_pairs={{0,32},{32,64},{64,96},{96,0},{1,33},{33,65},{65,97},{97,1},{2,34}... | collective-permute-start | bytes 2359304 | tf_op jit(solution)/shard_map/ppermute | solution.py:760
  5.7 2.2 %collective-permute-start.3 = (f32[3,2,32,1024]{3,2,1,0:T(8,128)}, f32[3,2,32,1024]{3,2,1,0:T(8,128)S(1)}, u32[]{:S(2)}, u32[]{:S(2)}) collective-permute-start(f32[3,2,32,1024]{3,2,1,0:T(8,128)} %get-tuple-element.26), channel_id=1, source_target_pairs={{32,0},{64,32},{96,64},{0,96},{33,1},{65,33},{97,65},{1,97},{34,2}... | collective-permute-start | bytes 2359304 | tf_op jit(solution)/shard_map/ppermute | solution.py:761
  7.9 8.9 %all-to-all-start = ((f32[128,2,128]{2,1,0:T(2,128)}), f32[128,2,128]{2,1,0:T(2,128)S(1)}, u32[]{:S(2)}, u32[]{:S(2)}) async-start(f32[128,2,128]{2,1,0:T(2,128)} %get-tuple-element.27), calls=%async_computation | async-start | bytes 262144 | tf_op jit(solution)/shard_map/all_to_all | solution.py:766
  16.7 1.1 %collective-permute-start = (f32[3,4,2,1024]{3,2,1,0:T(2,128)}, f32[3,4,2,1024]{3,2,1,0:T(2,128)S(1)}, u32[]{:S(2)}, u32[]{:S(2)}) collective-permute-start(f32[3,4,2,1024]{3,2,1,0:T(2,128)} %get-tuple-element.23), channel_id=1, source_target_pairs={{0,1},{1,0},{2,3},{3,2},{4,5},{5,4},{6,7},{7,6},{8,9},{9,8},{10,11... | collective-permute-start | bytes 294920 | tf_op jit(solution)/shard_map/ppermute | solution.py:762
  17.9 2.6 %collective-permute-start.1 = (f32[3,4,2,1024]{3,2,1,0:T(2,128)}, f32[3,4,2,1024]{3,2,1,0:T(2,128)S(1)}, u32[]{:S(2)}, u32[]{:S(2)}) collective-permute-start(f32[3,4,2,1024]{3,2,1,0:T(2,128)} %get-tuple-element.24), channel_id=1, source_target_pairs={{1,2},{2,1},{3,4},{4,3},{5,6},{6,5},{7,8},{8,7},{9,10},{10,9},{11,... | collective-permute-start | bytes 294920 | tf_op jit(solution)/shard_map/ppermute | solution.py:763
  20.5 9.2 %find.1 = (f32[3,8192]{1,0:T(4,128)}, f32[32,128]{1,0:T(8,128)}, f32[4,32,128]{2,1,0:T(8,128)}, f32[4,32,128]{2,1,0:T(8,128)}, f32[32,128]{1,0:T(8,128)}) custom-call(s32[1]{0:T(128)} %bitcast.place_ref, bf16[384,1024]{1,0:T(8,128)(2,1)S(1)} %get-tuple-element.28.bf_ref, s32[1,8192]{1,0:T(1,128)} %cell_hbm.3, f32[8,128]{1,0:T(8,128)} %bitcast.8), custom_call_target="tpu_custom_call" | custom-call | tf_op jit(solution)/shard_map/find/pallas_call | solution.py:418
  29.7 0.0 collective-permute-done.inner_hbm
  29.7 0.0 collective-permute-done.1.outer_hbm
  29.7 0.0 all-to-all-done.moved_hbm
  29.8 0.0 collective-permute-done.2.before_hbm
  29.8 0.0 collective-permute-done.3.behind_hbm
  29.8 0.0 copy-start.3
  29.8 0.0 copy-start
  29.8 0.0 copy-start.2
  29.8 10.7 %main_part.1 = (f32[3,8192]{1,0:T(4,128)}, f32[32,3,4,128]{3,2,1,0:T(4,128)}, f32[3,4,32,1024]{3,2,1,0:T(8,128)S(1)}) custom-call(s32[1]{0:T(128)} %bitcast.place_ref, f32[3,4,2,1024]{3,2,1,0:T(2,128)S(1)} %collective-permute-done.inner_hbm, f32[3,4,2,1024]{3,2,1,0:T(2,128)S(1)} %collective-permute-done.1.outer_hbm, ...), custom_call_target="tpu_custom_call" | custom-call | tf_op jit(solution)/shard_map/main_part/pallas_call | solution.py:623
  40.5 6.7 %all-to-all-start.1 = ((f32[32,3,4,128]{3,2,1,0:T(4,128)}), f32[32,3,4,128]{3,2,1,0:T(4,128)S(1)}, u32[]{:S(2)}, u32[]{:S(2)}) async-start(f32[32,3,4,128]{3,2,1,0:T(4,128)} %get-tuple-element.34), calls=%async_computation.1 | async-start | bytes 393216 | tf_op jit(solution)/shard_map/all_to_all | solution.py:773
  47.2 0.0 copy-done.3
  47.2 0.1 reshape.29
  47.3 0.1 copy.12
  47.4 1.2 %green_operator.1.green_ref = f32[128,128]{1,0:T(8,128)S(1)} custom-call(f32[32,128]{1,0:T(8,128)S(1)} %pad.4.rate_ref), custom_call_target="tpu_custom_call" | custom-call | tf_op jit(solution)/shard_map/green_operator/pallas_call | solution.py:254
  48.6 6.8 %all-to-all-done.1.tips_ref = f32[32,3,4,128]{3,2,1,0:T(4,128)S(1)} async-done(((f32[32,3,4,128]{3,2,1,0:T(4,128)}), f32[32,3,4,128]{3,2,1,0:T(4,128)S(1)}, u32[]{:S(2)}, u32[]{:S(2)}) %all-to-all-start.1) | async-done | bytes 196640 | tf_op jit(solution)/shard_map/all_to_all | solution.py:773
  55.5 1.0 %solve.1 = f32[32,3,4,128]{3,2,1,0:T(4,128)} custom-call(f32[32,3,4,128]{3,2,1,0:T(4,128)S(1)} %all-to-all-done.1.tips_ref, f32[128,128]{1,0:T(8,128)S(1)} %green_operator.1.green_ref), custom_call_target="tpu_custom_call" | custom-call | tf_op jit(solution)/shard_map/solve/pallas_call | solution.py:672
  56.5 3.8 %all-to-all-start.2 = ((f32[32,3,4,128]{3,2,1,0:T(4,128)}), f32[32,3,4,128]{3,2,1,0:T(4,128)S(1)}, u32[]{:S(2)}, u32[]{:S(2)}) async-start(f32[32,3,4,128]{3,2,1,0:T(4,128)} %solve.1), calls=%async_computation.2 | async-start | bytes 393216 | tf_op jit(solution)/shard_map/all_to_all | solution.py:779
  60.3 0.0 copy-done
  60.3 0.0 copy-done.2
  60.3 0.0 copy-start.1
  60.3 2.3 %local_solve.1 = (f32[3,4,32,1024]{3,2,1,0:T(8,128)}, f32[3,4,32,1024]{3,2,1,0:T(8,128)S(1)}) custom-call(f32[3,4,32,1024]{3,2,1,0:T(8,128)} %vel_hbm.5, f32[3,4,32,1024]{3,2,1,0:T(8,128)S(1)} %get-tuple-element.32.section_ref, f32[32,128]{1,0:T(8,128)S(1)} %copy-done, f32[32,128]{1,0:T(8,128)S(1)} %copy-done.2), custom_call_target="tpu_custom_call" | custom-call | tf_op jit(solution)/shard_map/local_solve/pallas_call | solution.py:706
  62.7 5.9 %all-to-all-done.2.edge_ref = f32[32,3,4,128]{3,2,1,0:T(4,128)S(1)} async-done(((f32[32,3,4,128]{3,2,1,0:T(4,128)}), f32[32,3,4,128]{3,2,1,0:T(4,128)S(1)}, u32[]{:S(2)}, u32[]{:S(2)}) %all-to-all-start.2) | async-done | bytes 196640 | tf_op jit(solution)/shard_map/all_to_all | solution.py:779
  68.6 0.0 copy-done.1
  68.6 1.3 %finish.1 = f32[3,4,32,1024]{3,2,1,0:T(8,128)} custom-call(f32[3,4,32,1024]{3,2,1,0:T(8,128)S(1)} %get-tuple-element.38.partial_ref, f32[32,3,4,128]{3,2,1,0:T(4,128)S(1)} %all-to-all-done.2.edge_ref, f32[4,32,128]{2,1,0:T(8,128)S(1)} %copy-done.1), custom_call_target="tpu_custom_call" | custom-call | tf_op jit(solution)/shard_map/finish/pallas_call | solution.py:741
  (1 shorter events, 0.0 us)
Async XLA Ops:
  3.1 26.6 %collective-permute-start.2 = (f32[3,2,32,1024]{3,2,1,0:T(8,128)}, f32[3,2,32,1024]{3,2,1,0:T(8,128)S(1)}, u32[]{:S(2)}, u32[]{:S(2)}) collective-permute-start(f32[3,2,32,1024]{3,2,1,0:T(8,128)} %get-tuple-element.25), channel_id=1, source_target_pairs={{0,32},{32,64},{64,96},{96,0},{1,33},{33,65},{65,97},{97,1},{2,34}... | collective-permute-start | bytes 2359304 | tf_op jit(solution)/shard_map/ppermute | solution.py:760
  5.7 24.1 %collective-permute-start.3 = (f32[3,2,32,1024]{3,2,1,0:T(8,128)}, f32[3,2,32,1024]{3,2,1,0:T(8,128)S(1)}, u32[]{:S(2)}, u32[]{:S(2)}) collective-permute-start(f32[3,2,32,1024]{3,2,1,0:T(8,128)} %get-tuple-element.26), channel_id=1, source_target_pairs={{32,0},{64,32},{96,64},{0,96},{33,1},{65,33},{97,65},{1,97},{34,2}... | collective-permute-start | bytes 2359304 | tf_op jit(solution)/shard_map/ppermute | solution.py:761
  7.9 21.9 %all-to-all-start = ((f32[128,2,128]{2,1,0:T(2,128)}), f32[128,2,128]{2,1,0:T(2,128)S(1)}, u32[]{:S(2)}, u32[]{:S(2)}) async-start(f32[128,2,128]{2,1,0:T(2,128)} %get-tuple-element.27), calls=%async_computation | async-start | bytes 262144 | tf_op jit(solution)/shard_map/all_to_all | solution.py:766
  16.7 13.0 %collective-permute-start = (f32[3,4,2,1024]{3,2,1,0:T(2,128)}, f32[3,4,2,1024]{3,2,1,0:T(2,128)S(1)}, u32[]{:S(2)}, u32[]{:S(2)}) collective-permute-start(f32[3,4,2,1024]{3,2,1,0:T(2,128)} %get-tuple-element.23), channel_id=1, source_target_pairs={{0,1},{1,0},{2,3},{3,2},{4,5},{5,4},{6,7},{7,6},{8,9},{9,8},{10,11... | collective-permute-start | bytes 294920 | tf_op jit(solution)/shard_map/ppermute | solution.py:762
  17.9 11.8 %collective-permute-start.1 = (f32[3,4,2,1024]{3,2,1,0:T(2,128)}, f32[3,4,2,1024]{3,2,1,0:T(2,128)S(1)}, u32[]{:S(2)}, u32[]{:S(2)}) collective-permute-start(f32[3,4,2,1024]{3,2,1,0:T(2,128)} %get-tuple-element.24), channel_id=1, source_target_pairs={{1,2},{2,1},{3,4},{4,3},{5,6},{6,5},{7,8},{8,7},{9,10},{10,9},{11,... | collective-permute-start | bytes 294920 | tf_op jit(solution)/shard_map/ppermute | solution.py:763
  29.8 17.4 %copy-start.3 = (f32[1024]{0:T(1024)S(1)}, f32[1024]{0:T(1024)}, u32[]{:S(2)}) copy-start(f32[1024]{0:T(1024)} %param.11) | copy-start | bytes 12292
  29.8 30.5 %copy-start = (f32[32,128]{1,0:T(8,128)S(1)}, f32[32,128]{1,0:T(8,128)}, u32[]{:S(2)}) copy-start(f32[32,128]{1,0:T(8,128)} %get-tuple-element.30.scale_hbm.scale_ref) | copy-start | bytes 49156
  29.8 30.5 %copy-start.2 = (f32[32,128]{1,0:T(8,128)S(1)}, f32[32,128]{1,0:T(8,128)}, u32[]{:S(2)}) copy-start(f32[32,128]{1,0:T(8,128)} %get-tuple-element.37.solve_ref) | copy-start | bytes 49156
  40.5 15.0 %all-to-all-start.1 = ((f32[32,3,4,128]{3,2,1,0:T(4,128)}), f32[32,3,4,128]{3,2,1,0:T(4,128)S(1)}, u32[]{:S(2)}, u32[]{:S(2)}) async-start(f32[32,3,4,128]{3,2,1,0:T(4,128)} %get-tuple-element.34), calls=%async_computation.1 | async-start | bytes 393216 | tf_op jit(solution)/shard_map/all_to_all | solution.py:773
  56.5 12.1 %all-to-all-start.2 = ((f32[32,3,4,128]{3,2,1,0:T(4,128)}), f32[32,3,4,128]{3,2,1,0:T(4,128)S(1)}, u32[]{:S(2)}, u32[]{:S(2)}) async-start(f32[32,3,4,128]{3,2,1,0:T(4,128)} %solve.1), calls=%async_computation.2 | async-start | bytes 393216 | tf_op jit(solution)/shard_map/all_to_all | solution.py:779
  60.3 8.2 %copy-start.1 = (f32[4,32,128]{2,1,0:T(8,128)S(1)}, f32[4,32,128]{2,1,0:T(8,128)}, u32[]{:S(2)}) copy-start(f32[4,32,128]{2,1,0:T(8,128)} %get-tuple-element.40.fix_ref) | copy-start | bytes 196612
